TPU v7x, 32 devices: a whole 2x2x4 slice. The times are simulated.
32 devices in a mesh: hel: 4 (over y, x), ang: 8 (over z, core).
Axes of the slice: x: 2, y: 2, z: 4, core: 2. Of those that a mesh axis runs over, the one named last changes fastest.
Arguments:
- wavepacket: float32 [64, 128, 32, 256], P('hel', 'ang'), may hold values from -6 to 6
- potential: float32 [128, 32, 256], P('ang'), may hold values from -0.4 to 0.4
- kinetic: float32 [256, 256], replicated, may hold values from -0.25 to 0.25
- ang_basis: float32 [64, 128, 128], P('hel'), may hold values from -1 to 1, as said below
- rot_energy: float32 [128], replicated, may hold values from -0.9 to -0.1
- radial_weight: float32 [256], replicated, may hold values from 0.2 to 1
- distance_weight: float32 [32], replicated, may hold values from 0.25 to 1
- truncation: int32 [64], P('hel'), may hold values from 32 to 128, as said below
- coupling: float32 [64], replicated, may hold values from 0.1 to 0.4
Outputs:
- evolved: float32 [64, 128, 32, 256], P('hel', 'ang')
Inputs may be any that keep to these rules, and one draw needn't show every extreme that they name: Each ang_basis[k] is an orthogonal matrix. `truncation`: some helicity retains all 128 functions and some retains a quarter of them.
All inputs are finite; a program needn't handle non-finite values.
Results may differ from a plain program's by a relative error of at most 0.00011.
Values sent between devices are 32-bit elements; how exact they have to be, the bound alone decides.
No kernel may reach another device: no remote copies, remote signals or barrier semaphores. Data moves between devices by JAX's collectives and lax.ppermute only.
A program may use at most 128 MiB of HBM per device.

v0:
```python
import jax
import jax.numpy as jnp
from jax import lax
from jax.sharding import PartitionSpec as P

OUTER = 3


def padded_2(array, sides, width):
    for axis, dim in sides:
        size, length = (lax.axis_size(axis), array.shape[dim])
        up = [(i, (i + 1) % size) for i in range(size - 1)]
        down = [(j, i) for i, j in up]
        last = lax.slice_in_dim(array, length - width, length, axis=dim)
        first = lax.slice_in_dim(array, 0, width, axis=dim)
        before = lax.ppermute(last, axis, up)
        after = lax.ppermute(first, axis, down)
        array = jnp.concatenate([before, array, after], axis=dim)
    return array


def hamiltonian(field, potential, kinetic):
    return (
        jnp.dot(field, kinetic, precision=lax.Precision.HIGHEST, preferred_element_type=jnp.float32)
        + potential * field
    )


def chebyshev(field, potential, kinetic):
    first = hamiltonian(field, potential, kinetic)
    second = 2.0 * hamiltonian(first, potential, kinetic) - field
    return 0.6 * field + 0.3 * first - 0.1 * second


def angular(field, basis, scale):
    coeffs = jnp.einsum("kji,kirs->kjrs", basis, field, precision=lax.Precision.HIGHEST)
    return field + jnp.einsum(
        "kji,kjrs->kirs", basis, coeffs * scale[:, :, None, :], precision=lax.Precision.HIGHEST
    )


def coriolis(field, coupling, rows_weight):
    count = field.shape[0]
    first_index = lax.axis_index("hel") * count
    padded = padded_2(field, (("hel", 0),), 1)
    shifted = jnp.concatenate([jnp.zeros((1,), jnp.float32), coupling])
    local_coupling = lax.dynamic_slice_in_dim(coupling, first_index, count)
    before = lax.dynamic_slice_in_dim(shifted, first_index, count)
    return field + rows_weight[None, None, :, None] * (
        local_coupling[:, None, None, None] * padded[2:] + before[:, None, None, None] * padded[:-2]
    )


def body(
    wavepacket,
    potential,
    kinetic,
    ang_basis,
    rot_energy,
    radial_weight,
    distance_weight,
    truncation,
    coupling,
):
    orders = jnp.arange(ang_basis.shape[1], dtype=jnp.int32)
    mask = (orders[None, :] < truncation[:, None]).astype(jnp.float32)
    scale = mask[:, :, None] * rot_energy[None, :, None] * radial_weight[None, None, :]
    field = lax.all_to_all(wavepacket, "ang", split_axis=2, concat_axis=1, tiled=True)
    regrouped = lax.all_to_all(potential, "ang", split_axis=1, concat_axis=0, tiled=True)
    height = field.shape[2]
    rows_weight = lax.dynamic_slice_in_dim(distance_weight, lax.axis_index("ang") * height, height)
    for outer_turn in range(OUTER):
        field = coriolis(field, coupling, rows_weight)
        field = chebyshev(field, regrouped, kinetic)
        field = angular(field, ang_basis, scale)
    return lax.all_to_all(field, "ang", split_axis=1, concat_axis=2, tiled=True)


def solution(mesh):
    placed = (
        P("hel", "ang", None, None),
        P("ang", None, None),
        P(),
        P("hel", None, None),
        P(),
        P(),
        P(),
        P("hel"),
        P(),
    )
    return jax.shard_map(
        body, mesh=mesh, in_specs=placed, out_specs=P("hel", "ang", None, None), check_vma=False
    )
```

profile of v0, /device:TPU:6, one launch (start us, length us, event | category | flops | bytes accessed | tf_op | source)
XLA Modules:
  0.0 749.7 jit_solution(11782355134684832367)
XLA Ops:
  0.0 11.7 %copy.16 = f32[16,16,32,256]{3,1,0,2:T(8,128)} copy(f32[16,16,32,256]{3,2,1,0:T(8,128)} %param.9) | data formatting | bytes 16777216 | tf_op args[0]
  11.7 5.1 all-to-all-start
  18.0 182.7 %all-to-all-done = f32[16,16,32,256]{3,1,0,2:T(8,128)} async-done(((f32[16,16,32,256]{3,1,0,2:T(8,128)}), f32[16,16,32,256]{3,1,0,2:T(8,128)}, u32[]{:S(2)}, u32[]{:S(2)}) %all-to-all-start) | async-done | bytes 8388640 | tf_op jit(solution)/shard_map/all_to_all | solution.py:68
  200.7 4.2 all-to-all-start.1
  204.9 4.4 copy.32
  209.4 3.4 copy-done.4
  215.1 5.5 collective-permute-start
  222.4 8.4 %collective-permute-done.1 = f32[1,128,4,256]{3,1,2,0:T(8,128)} collective-permute-done((f32[1,128,4,256]{3,1,2,0:T(8,128)}, f32[1,128,4,256]{3,1,2,0:T(8,128)}, u32[]{:S(2)}, u32[]{:S(2)}) %collective-permute-start.1) | collective-permute-done | bytes 524320 | tf_op jit(solution)/shard_map/ppermute | solution.py:16
  231.4 14.2 %fusion.43 = f32[16,128,4,256]{3,1,2,0:T(8,128)} fusion(f32[256,256]{1,0:T(8,128)S(1)} %copy-done.9, f32[16,128,4,256]{3,1,2,0:T(8,128)} %bitcast.71, f32[1,128,4,256]{3,1,2,0:T(8,128)} %collective-permute-done.1, f32[1,128,4,256]{3,1,2,0:T(8,128)} %collective-permute-done, f32[16]{0:T(128)S(1)} %dynamic_slice.15, f32[16]{0:T(128)S(1)} %dynamic_slice.14, ...), kind=kOutput, calls=%fused_computation.62 | convolution fusion | flops 6457131008 | bytes 18088080 | tf_op jit(solution)/shard_map/dot_general | solution.py:24
  245.6 31.6 %multiply_subtract_fusion.2 = f32[16,128,4,256]{3,1,2,0:T(8,128)S(1)} fusion(f32[16,128,4,256]{3,1,2,0:T(8,128)} %fusion.43, f32[128,4,256]{2,0,1:T(8,128)S(1)} %bitcast.73, f32[256,256]{1,0:T(8,128)S(1)} %copy-done.9, f32[16,128,4,256]{3,1,2,0:T(8,128)} %bitcast.72, f32[1,128,4,256]{3,1,2,0:T(8,128)} %collective-permute-done.1, f32[16]{0:T(128)S(1)} %dynamic_slice.15, ...), kind=kOutput, calls=%fused_computation.34 | convolution fusion | flops 6499074048 | bytes 27000976 | tf_op jit(solution)/shard_map/dot_general | solution.py:24
  277.3 3.4 copy-done.2
  280.7 15.8 %fusion.34 = f32[16,4,256,128]{3,2,1,0:T(8,128)} fusion(f32[16,128,4,256]{3,1,2,0:T(8,128)S(1)} %multiply_subtract_fusion.2, f32[16,128,128]{2,1,0:T(8,128)S(1)} %copy-done), kind=kOutput, calls=%fused_computation.52 | convolution fusion | flops 3221225472 | bytes 17825792 | tf_op jit(solution)/shard_map/kji,kirs->kjrs/dot_general | solution.py:36
  296.5 17.3 %bitcast_add_fusion.2 = f32[16,128,4,256]{3,1,2,0:T(8,128)} fusion(f32[16,128,4,256]{3,1,2,0:T(8,128)} %copy-done.2, f32[16,4,256,128]{3,2,1,0:T(8,128)} %fusion.34, f32[16,128,256]{1,2,0:T(8,128)S(1)} %broadcast_multiply_fusion, f32[16,128,128]{2,1,0:T(8,128)S(1)} %copy-done), kind=kOutput, calls=%fused_computation.27 | convolution fusion | flops 3225419776 | bytes 28311552 | tf_op jit(solution)/shard_map/kji,kjrs->kirs/dot_general | solution.py:37
  315.0 11.5 %collective-permute-start.2 = (f32[1,128,4,256]{3,1,2,0:T(8,128)S(1)}, f32[1,128,4,256]{3,1,2,0:T(8,128)S(1)}, u32[]{:S(2)}, u32[]{:S(2)}) collective-permute-start(f32[1,128,4,256]{3,1,2,0:T(8,128)S(1)} %get-tuple-element.7), channel_id=1, source_target_pairs={{8,0},{16,8},{24,16},{9,1},{17,9},{25,17},{10,2},{18,10},{26,18},{... | collective-permute-start | bytes 1572872 | tf_op jit(solution)/shard_map/ppermute | solution.py:17
  327.9 9.5 %collective-permute-done.2 = f32[1,128,4,256]{3,1,2,0:T(8,128)S(1)} collective-permute-done((f32[1,128,4,256]{3,1,2,0:T(8,128)S(1)}, f32[1,128,4,256]{3,1,2,0:T(8,128)S(1)}, u32[]{:S(2)}, u32[]{:S(2)}) %collective-permute-start.2) | collective-permute-done | bytes 524320 | tf_op jit(solution)/shard_map/ppermute | solution.py:17
  337.4 15.1 %collective-permute-done.3 = f32[1,128,4,256]{3,1,2,0:T(8,128)S(1)} collective-permute-done((f32[1,128,4,256]{3,1,2,0:T(8,128)S(1)}, f32[1,128,4,256]{3,1,2,0:T(8,128)S(1)}, u32[]{:S(2)}, u32[]{:S(2)}) %collective-permute-start.3) | collective-permute-done | bytes 524320 | tf_op jit(solution)/shard_map/ppermute | solution.py:16
  352.4 14.7 %fusion.40 = f32[16,128,4,256]{3,1,2,0:T(8,128)} fusion(f32[256,256]{1,0:T(8,128)S(1)} %copy-done.9, f32[16,128,4,256]{3,1,2,0:T(8,128)} %bitcast_add_fusion.2, f32[1,128,4,256]{3,1,2,0:T(8,128)S(1)} %collective-permute-done.3, f32[1,128,4,256]{3,1,2,0:T(8,128)S(1)} %collective-permute-done.2, f32[16]{0:T(128)S(1)} %dynamic_slice.15, ...), kind=kOutput, calls=%fused_computation.59 | convolution fusion | flops 6457131008 | bytes 18088080 | tf_op jit(solution)/shard_map/dot_general | solution.py:24
  367.1 24.2 %multiply_subtract_fusion.1 = f32[16,128,4,256]{3,1,2,0:T(8,128)S(1)} fusion(f32[16,128,4,256]{3,1,2,0:T(8,128)} %fusion.40, f32[128,4,256]{2,0,1:T(8,128)S(1)} %bitcast.74, f32[256,256]{1,0:T(8,128)S(1)} %copy-done.9, f32[16,128,4,256]{3,1,2,0:T(8,128)} %bitcast_add_fusion.2, f32[1,128,4,256]{3,1,2,0:T(8,128)S(1)} %collective-permute-done.3, ...), kind=kOutput, calls=%fused_computation.32 | convolution fusion | flops 6499074048 | bytes 27000976 | tf_op jit(solution)/shard_map/dot_general | solution.py:24
  391.3 3.4 copy-done.3
  394.7 15.7 %fusion.31 = f32[16,4,256,128]{3,2,1,0:T(8,128)} fusion(f32[16,128,4,256]{3,1,2,0:T(8,128)S(1)} %multiply_subtract_fusion.1, f32[16,128,128]{2,1,0:T(8,128)S(1)} %copy-done), kind=kOutput, calls=%fused_computation.49 | convolution fusion | flops 3221225472 | bytes 17825792 | tf_op jit(solution)/shard_map/kji,kirs->kjrs/dot_general | solution.py:36
  410.4 17.3 %bitcast_add_fusion.1 = f32[16,128,4,256]{3,1,2,0:T(8,128)} fusion(f32[16,128,4,256]{3,1,2,0:T(8,128)} %copy-done.3, f32[16,4,256,128]{3,2,1,0:T(8,128)} %fusion.31, f32[16,128,256]{1,2,0:T(8,128)S(1)} %broadcast_multiply_fusion, f32[16,128,128]{2,1,0:T(8,128)S(1)} %copy-done), kind=kOutput, calls=%fused_computation.24 | convolution fusion | flops 3225419776 | bytes 28311552 | tf_op jit(solution)/shard_map/kji,kjrs->kirs/dot_general | solution.py:37
  432.8 8.6 %collective-permute-done.4 = f32[1,128,4,256]{3,1,2,0:T(8,128)S(1)} collective-permute-done((f32[1,128,4,256]{3,1,2,0:T(8,128)S(1)}, f32[1,128,4,256]{3,1,2,0:T(8,128)S(1)}, u32[]{:S(2)}, u32[]{:S(2)}) %collective-permute-start.4) | collective-permute-done | bytes 524320 | tf_op jit(solution)/shard_map/ppermute | solution.py:17
  441.4 12.0 %collective-permute-done.5 = f32[1,128,4,256]{3,1,2,0:T(8,128)S(1)} collective-permute-done((f32[1,128,4,256]{3,1,2,0:T(8,128)S(1)}, f32[1,128,4,256]{3,1,2,0:T(8,128)S(1)}, u32[]{:S(2)}, u32[]{:S(2)}) %collective-permute-start.5) | collective-permute-done | bytes 524320 | tf_op jit(solution)/shard_map/ppermute | solution.py:16
  453.4 14.5 %fusion.37 = f32[16,128,4,256]{3,1,2,0:T(8,128)} fusion(f32[256,256]{1,0:T(8,128)S(1)} %copy-done.9, f32[16,128,4,256]{3,1,2,0:T(8,128)} %bitcast_add_fusion.1, f32[1,128,4,256]{3,1,2,0:T(8,128)S(1)} %collective-permute-done.5, f32[1,128,4,256]{3,1,2,0:T(8,128)S(1)} %collective-permute-done.4, f32[16]{0:T(128)S(1)} %dynamic_slice.15, ...), kind=kOutput, calls=%fused_computation.56 | convolution fusion | flops 6457131008 | bytes 18088080 | tf_op jit(solution)/shard_map/dot_general | solution.py:24
  467.9 24.2 %multiply_subtract_fusion = f32[16,128,4,256]{3,1,2,0:T(8,128)S(1)} fusion(f32[16,128,4,256]{3,1,2,0:T(8,128)} %fusion.37, f32[128,4,256]{2,0,1:T(8,128)S(1)} %bitcast.75, f32[256,256]{1,0:T(8,128)S(1)} %copy-done.9, f32[16,128,4,256]{3,1,2,0:T(8,128)} %bitcast_add_fusion.1, f32[1,128,4,256]{3,1,2,0:T(8,128)S(1)} %collective-permute-done.5, ...), kind=kOutput, calls=%fused_computation.30 | convolution fusion | flops 6499074048 | bytes 27000976 | tf_op jit(solution)/shard_map/dot_general | solution.py:24
  492.1 3.4 copy-done.1
  495.5 16.0 %fusion.28 = f32[16,4,256,128]{3,2,1,0:T(8,128)} fusion(f32[16,128,4,256]{3,1,2,0:T(8,128)S(1)} %multiply_subtract_fusion, f32[16,128,128]{2,1,0:T(8,128)S(1)} %copy-done), kind=kOutput, calls=%fused_computation.46 | convolution fusion | flops 3221225472 | bytes 17825792 | tf_op jit(solution)/shard_map/kji,kirs->kjrs/dot_general | solution.py:36
  511.4 17.3 %bitcast_add_fusion = f32[16,128,4,256]{3,1,2,0:T(8,128)} fusion(f32[16,128,4,256]{3,1,2,0:T(8,128)} %copy-done.1, f32[16,4,256,128]{3,2,1,0:T(8,128)} %fusion.28, f32[16,128,256]{1,2,0:T(8,128)S(1)} %broadcast_multiply_fusion, f32[16,128,128]{2,1,0:T(8,128)S(1)} %copy-done), kind=kOutput, calls=%fused_computation.21 | convolution fusion | flops 3225419776 | bytes 28311552 | tf_op jit(solution)/shard_map/kji,kjrs->kirs/dot_general | solution.py:37
  528.7 12.2 %copy.23 = f32[16,128,4,256]{3,2,0,1:T(4,128)} copy(f32[16,128,4,256]{3,1,2,0:T(8,128)} %bitcast_add_fusion) | data formatting | bytes 16777216 | tf_op jit(solution)/shard_map/add | solution.py:37
  540.9 189.6 %all_to_all.51 = f32[16,128,4,256]{3,2,0,1:T(4,128)} all-to-all(f32[16,128,4,256]{3,2,0,1:T(4,128)} %copy.23), channel_id=1, replica_groups=mesh['hel'=4,'ang'=8] {'ang'}, dimensions={1} | all-to-all | bytes 16777216 | tf_op jit(solution)/shard_map/all_to_all | solution.py:76
  730.5 9.1 %copy.24 = f32[16,16,8,4,256]{4,3,2,1,0:T(4,128)} copy(f32[16,16,8,4,256]{4,3,0,1,2:T(4,128)} %bitcast.69) | data formatting | bytes 16777216 | tf_op jit(solution)/shard_map/all_to_all | solution.py:76
  739.6 10.0 %all_to_all.47 = f32[16,16,32,256]{3,2,1,0:T(8,128)} reshape(f32[16,16,8,4,256]{4,3,2,1,0:T(4,128)} %copy.24) | data formatting | bytes 16777216 | tf_op jit(solution)/shard_map/all_to_all | solution.py:76
  (37 shorter events, 13.5 us)
Async XLA Ops:
  0.0 280.6 %copy-start = (f32[16,128,128]{2,1,0:T(8,128)S(1)}, f32[16,128,128]{2,1,0:T(8,128)}, u32[]{:S(2)}) copy-start(f32[16,128,128]{2,1,0:T(8,128)} %param.12) | copy-start | bytes 3145732
  11.7 5.1 copy-start.5
  11.7 189.0 %all-to-all-start = ((f32[16,16,32,256]{3,1,0,2:T(8,128)}), f32[16,16,32,256]{3,1,0,2:T(8,128)}, u32[]{:S(2)}, u32[]{:S(2)}) async-start(f32[16,16,32,256]{3,1,0,2:T(8,128)} %copy.16), calls=%async_computation | async-start | bytes 16777216 | tf_op jit(solution)/shard_map/all_to_all | solution.py:68
  200.7 20.6 %all-to-all-start.1 = ((f32[16,32,256]{2,0,1:T(8,128)}), f32[16,32,256]{2,0,1:T(8,128)}, u32[]{:S(2)}, u32[]{:S(2)}) async-start(f32[16,32,256]{2,0,1:T(8,128)} %copy.18), calls=%async_computation.1 | async-start | bytes 1048576 | tf_op jit(solution)/shard_map/all_to_all | solution.py:69
  204.9 15.8 %copy-start.10 = (f32[64]{0:T(128)S(1)}, f32[64]{0:T(128)}, u32[]{:S(2)}) copy-start(f32[64]{0:T(128)} %param.17) | copy-start | bytes 772
  204.9 15.9 %copy-start.11 = (f32[32]{0:T(128)S(1)}, f32[32]{0:T(128)}, u32[]{:S(2)}) copy-start(f32[32]{0:T(128)} %param.15) | copy-start | bytes 388
  204.9 16.0 %copy-start.7 = (f32[128]{0:T(128)S(1)}, f32[128]{0:T(128)}, u32[]{:S(2)}) copy-start(f32[128]{0:T(128)} %param.13) | copy-start | bytes 1540
  204.9 16.0 %copy-start.8 = (s32[16]{0:T(128)S(1)}, s32[16]{0:T(128)}, u32[]{:S(2)}) copy-start(s32[16]{0:T(128)} %param.16) | copy-start | bytes 196
  204.9 16.1 %copy-start.6 = (f32[256]{0:T(256)S(1)}, f32[256]{0:T(256)}, u32[]{:S(2)}) copy-start(f32[256]{0:T(256)} %param.14) | copy-start | bytes 3076
  204.9 26.5 %copy-start.9 = (f32[256,256]{1,0:T(8,128)S(1)}, f32[256,256]{1,0:T(8,128)}, u32[]{:S(2)}) copy-start(f32[256,256]{1,0:T(8,128)} %param.11) | copy-start | bytes 786436
  209.4 3.4 copy-start.4
  213.8 17.0 %collective-permute-start.1 = (f32[1,128,4,256]{3,1,2,0:T(8,128)}, f32[1,128,4,256]{3,1,2,0:T(8,128)}, u32[]{:S(2)}, u32[]{:S(2)}) collective-permute-start(f32[1,128,4,256]{3,1,2,0:T(8,128)} %bitcast.5), channel_id=1, source_target_pairs={{0,8},{8,16},{16,24},{1,9},{9,17},{17,25},{2,10},{10,18},{18,26},{... | collective-permute-start | bytes 1572872 | tf_op jit(solution)/shard_map/ppermute | solution.py:16
  215.1 16.3 %collective-permute-start = (f32[1,128,4,256]{3,1,2,0:T(8,128)}, f32[1,128,4,256]{3,1,2,0:T(8,128)}, u32[]{:S(2)}, u32[]{:S(2)}) collective-permute-start(f32[1,128,4,256]{3,1,2,0:T(8,128)} %bitcast.4), channel_id=1, source_target_pairs={{8,0},{16,8},{24,16},{9,1},{17,9},{25,17},{10,2},{18,10},{26,18},{... | collective-permute-start | bytes 1572872 | tf_op jit(solution)/shard_map/ppermute | solution.py:17
  277.2 3.4 copy-start.2
  315.0 22.3 %collective-permute-start.2 = (f32[1,128,4,256]{3,1,2,0:T(8,128)S(1)}, f32[1,128,4,256]{3,1,2,0:T(8,128)S(1)}, u32[]{:S(2)}, u32[]{:S(2)}) collective-permute-start(f32[1,128,4,256]{3,1,2,0:T(8,128)S(1)} %get-tuple-element.7), channel_id=1, source_target_pairs={{8,0},{16,8},{24,16},{9,1},{17,9},{25,17},{10,2},{18,10},{26,18},{... | collective-permute-start | bytes 1572872 | tf_op jit(solution)/shard_map/ppermute | solution.py:17
  326.6 25.9 %collective-permute-start.3 = (f32[1,128,4,256]{3,1,2,0:T(8,128)S(1)}, f32[1,128,4,256]{3,1,2,0:T(8,128)S(1)}, u32[]{:S(2)}, u32[]{:S(2)}) collective-permute-start(f32[1,128,4,256]{3,1,2,0:T(8,128)S(1)} %get-tuple-element.8), channel_id=1, source_target_pairs={{0,8},{8,16},{16,24},{1,9},{9,17},{17,25},{2,10},{10,18},{18,26},{... | collective-permute-start | bytes 1572872 | tf_op jit(solution)/shard_map/ppermute | solution.py:16
  391.3 3.4 copy-start.3
  429.0 12.4 %collective-permute-start.4 = (f32[1,128,4,256]{3,1,2,0:T(8,128)S(1)}, f32[1,128,4,256]{3,1,2,0:T(8,128)S(1)}, u32[]{:S(2)}, u32[]{:S(2)}) collective-permute-start(f32[1,128,4,256]{3,1,2,0:T(8,128)S(1)} %get-tuple-element.5), channel_id=1, source_target_pairs={{8,0},{16,8},{24,16},{9,1},{17,9},{25,17},{10,2},{18,10},{26,18},{... | collective-permute-start | bytes 1572872 | tf_op jit(solution)/shard_map/ppermute | solution.py:17
  431.5 21.9 %collective-permute-start.5 = (f32[1,128,4,256]{3,1,2,0:T(8,128)S(1)}, f32[1,128,4,256]{3,1,2,0:T(8,128)S(1)}, u32[]{:S(2)}, u32[]{:S(2)}) collective-permute-start(f32[1,128,4,256]{3,1,2,0:T(8,128)S(1)} %get-tuple-element.6), channel_id=1, source_target_pairs={{0,8},{8,16},{16,24},{1,9},{9,17},{17,25},{2,10},{10,18},{18,26},{... | collective-permute-start | bytes 1572872 | tf_op jit(solution)/shard_map/ppermute | solution.py:16
  492.1 3.4 copy-start.1
where the time goes:
time: 756 us; the launch traced here: 750 us
  waiting for transfers between devices  237 us (31%)
  matrix products  223 us (29%)
  blocking collectives  190 us (25%)
  local copies, waits for them, and re-layouts  67.1 us (9%)
  starting transfers between devices  32.6 us (4%)
    all_to_all x1, blocking collectives, body(): return lax.all_to_all(field, 'ang', split_axis=1, concat_axis=2, tiled=True)  190 us
    all_to_all x1, waiting for transfers between devices, body(): lax.all_to_all(wavepacket, 'ang', split_axis=2, concat_axis=1, tiled=True)  183 us
    dot_general x6, matrix products, hamiltonian(): jnp.dot(field, kinetic, precision=lax.Precision.HIGHEST, preferred_elemen...  123 us
    dot_general x3, matrix products, angular(): jnp.einsum('kji,kjrs->kirs', basis, coeffs * scale[:, :, None, :], precis...  51.8 us
    dot_general x3, matrix products, angular(): jnp.einsum('kji,kirs->kjrs', basis, field, precision=lax.Precision.HIGHEST)  47.5 us
    ppermute x3, waiting for transfers between devices, padded_2(): before = lax.ppermute(last, axis, up)  35.5 us
    unnamed x26, local copies, waits for them, and re-layouts  26.5 us
    ppermute x3, starting transfers between devices, padded_2(): after = lax.ppermute(first, axis, down)  19.5 us
  transfers between devices with their start and end apart: 8, of which 7 were waited for; matrix products, arithmetic and copies ran while one was open for 1% of the time, Pallas kernels for 0%

commit v1 on v0

v1 whole, which is shorter than its diff:
```python
import jax
import jax.numpy as jnp
from jax import lax
from jax.experimental import pallas as pl
from jax.experimental.pallas import tpu as pltpu
from jax.sharding import PartitionSpec as P


OUTER = 3
PAIR = 2
LANES = 128


def partner(array, axis, bits):
    size = lax.axis_size(axis)
    return lax.ppermute(array, axis, [(i, i ^ bits) for i in range(size)])


def pack(wave, potential, chunk, places):
    count, angles, _, width = wave.shape
    size = lax.axis_size("ang")

    def kernel(place_ref, wave_ref, pot_ref, *outs):
        for d in range(size):
            start = place_ref[d]
            for k in range(count):
                rows = wave_ref.at[k].reshape(angles * size, LANES)
                outs[d][k] = rows[pl.ds(start, angles, stride=size), :]
            rows = pot_ref.reshape(angles * size, LANES)
            outs[d][count] = rows[pl.ds(start, angles, stride=size), :]

    return pl.pallas_call(
        kernel,
        name="pack",
        grid=(width // LANES,),
        in_specs=[
            pl.BlockSpec(memory_space=pltpu.SMEM),
            pl.BlockSpec((count, angles, size, LANES), lambda g: (0, 0, chunk, g)),
            pl.BlockSpec((angles, size, LANES), lambda g: (0, chunk, g)),
        ],
        out_specs=[pl.BlockSpec((count + 1, angles, LANES), lambda g: (0, 0, g))] * size,
        out_shape=[jax.ShapeDtypeStruct((count + 1, angles, width), jnp.float32)] * size,
    )(places, wave, potential)


def unpack(pieces, whole, shape, chunk, places):
    count, angles, _, width = shape
    size = len(pieces)

    def kernel(place_ref, *refs):
        ins, out = refs[:size], refs[-1]
        for d in range(size):
            start = place_ref[d]
            for k in range(count):
                rows = out.at[k].reshape(angles * size, LANES)
                rows[pl.ds(start, angles, stride=size), :] = ins[d][k]

    args = [places, *pieces]
    specs = [pl.BlockSpec(memory_space=pltpu.SMEM)] + [
        pl.BlockSpec((count, angles, LANES), lambda g: (0, 0, g))
    ] * size
    aliases = {}
    if whole is not None:
        aliases = {len(args): 0}
        args.append(whole)
        specs.append(pl.BlockSpec(memory_space=pl.ANY))
    return pl.pallas_call(
        kernel,
        name="unpack",
        grid=(width // LANES,),
        in_specs=specs,
        out_specs=pl.BlockSpec((count, angles, size, LANES), lambda g: (0, 0, chunk, g)),
        out_shape=jax.ShapeDtypeStruct(shape, jnp.float32),
        input_output_aliases=aliases,
    )(*args)


def halves(values):
    high = values.astype(jnp.bfloat16)
    return high, (values - high.astype(jnp.float32)).astype(jnp.bfloat16)


def window(pieces, below, above, mats, mats_below, mats_above, kinetic, radial, weights, places):
    size = len(pieces)
    count, angles, width = pieces[0].shape
    count -= 1
    full = size * angles
    total = count + 2 * OUTER

    def kernel(*refs):
        place_ref, weight_ref, kin_ref, rad_ref = refs[:4]
        ins = refs[4 : 4 + size]
        below_ref, above_ref, mat_ref, mat_below_ref, mat_above_ref = refs[4 + size : 9 + size]
        outs = refs[9 + size : 9 + 2 * size]
        one, two, mat, pot, kin, sems = refs[9 + 2 * size :]
        copies = []

        def fetch(source, target):
            copy = pltpu.make_async_copy(source, target, sems.at[len(copies)])
            copy.start()
            copies.append(copy)

        def spot(d):
            return pl.ds(pl.multiple_of(place_ref[d] * angles, angles), angles)

        for d in range(size):
            fetch(ins[d].at[pl.ds(0, count)], one.at[pl.ds(OUTER, count), spot(d), :])
            fetch(ins[d].at[count], pot.at[spot(d), :])
            fetch(below_ref.at[d], one.at[pl.ds(0, OUTER), spot(d), :])
            fetch(above_ref.at[d], one.at[pl.ds(OUTER + count, OUTER), spot(d), :])
        fetch(mat_below_ref, mat.at[pl.ds(0, OUTER)])
        fetch(mat_ref, mat.at[pl.ds(OUTER, count)])
        fetch(mat_above_ref, mat.at[pl.ds(OUTER + count, OUTER)])
        kin_high, kin_low = halves(kin_ref[...])
        kin[0], kin[1] = kin_high, kin_low
        for copy in copies:
            copy.wait()

        def times_kinetic(field):
            high, low = halves(field)
            dot = lambda a, b: jnp.dot(a, b, preferred_element_type=jnp.float32)
            return dot(high, kin[0]) + dot(low, kin[0]) + dot(high, kin[1])

        def step(source, target, turn):
            first = turn + 1
            amount = total - 2 * first
            potential = pot[...]
            spread = jnp.concatenate([potential] * PAIR, axis=0)

            def body(index, carry):
                m = first + index * PAIR
                fields = []
                for p in range(PAIR):
                    at = m + p - turn
                    fields.append(
                        source[at] + weight_ref[m + p + 1] * source[at + 1] + weight_ref[m + p] * source[at - 1]
                    )
                field = jnp.concatenate(fields, axis=0)
                once = times_kinetic(field) + spread * field
                mixed = 0.3 * field - 0.2 * once
                passed = 0.7 * field + times_kinetic(mixed) + spread * mixed
                for p in range(PAIR):
                    part = passed[p * full : (p + 1) * full]
                    high, low = halves(part)
                    mat_high, mat_low = halves(mat[m + p])
                    left = jnp.concatenate(
                        [
                            jnp.concatenate([mat_high, mat_high], axis=1),
                            jnp.concatenate([mat_low, mat_low], axis=1),
                        ],
                        axis=0,
                    )
                    both = jnp.dot(
                        left, jnp.concatenate([high, low], axis=0), preferred_element_type=jnp.float32
                    )
                    target[m + p - first] = part + rad_ref[...] * (both[:full] + both[full:])
                return carry

            lax.fori_loop(0, amount // PAIR, body, 0)

        buffers = [one, two]
        for turn in range(OUTER):
            step(buffers[turn % 2], buffers[(turn + 1) % 2], turn)
        result = buffers[OUTER % 2]
        stores = []
        for d in range(size):
            copy = pltpu.make_async_copy(result.at[pl.ds(0, count), spot(d), :], outs[d], sems.at[d])
            copy.start()
            stores.append(copy)
        for copy in stores:
            copy.wait()

    anywhere = pl.BlockSpec(memory_space=pl.ANY)
    return pl.pallas_call(
        kernel,
        name="window",
        in_specs=[
            pl.BlockSpec(memory_space=pltpu.SMEM),
            pl.BlockSpec(memory_space=pltpu.SMEM),
            pl.BlockSpec(memory_space=pltpu.VMEM),
            pl.BlockSpec(memory_space=pltpu.VMEM),
        ]
        + [anywhere] * (size + 5),
        out_specs=[anywhere] * size,
        out_shape=[jax.ShapeDtypeStruct((count, angles, width), jnp.float32)] * size,
        scratch_shapes=[
            pltpu.VMEM((total, full, width), jnp.float32),
            pltpu.VMEM((total, full, width), jnp.float32),
            pltpu.VMEM((total, full, full), jnp.float32),
            pltpu.VMEM((full, width), jnp.float32),
            pltpu.VMEM((2, width, width), jnp.bfloat16),
            pltpu.SemaphoreType.DMA((4 * size + 3,)),
        ],
    )(places, weights, kinetic, radial, *pieces, below, above, mats, mats_below, mats_above)


def edges(pieces):
    size = len(pieces)
    count, angles, width = pieces[0].shape
    count -= 1

    def kernel(*refs):
        ins, lows, highs, sems = refs[:size], refs[size], refs[size + 1], refs[size + 2]
        copies = []
        for d in range(size):
            for side, (target, start) in enumerate(((lows, 0), (highs, count - OUTER))):
                copies.append(
                    pltpu.make_async_copy(
                        ins[d].at[pl.ds(start, OUTER)], target.at[d], sems.at[2 * d + side]
                    )
                )
                copies[-1].start()
        for copy in copies:
            copy.wait()

    anywhere = pl.BlockSpec(memory_space=pl.ANY)
    shape = jax.ShapeDtypeStruct((size, OUTER, angles, width), jnp.float32)
    return pl.pallas_call(
        kernel,
        name="edges",
        in_specs=[anywhere] * size,
        out_specs=[anywhere] * 2,
        out_shape=[shape] * 2,
        scratch_shapes=[pltpu.SemaphoreType.DMA((2 * size,))],
    )(*pieces)


def along_hel(array, step):
    size = lax.axis_size("hel")
    return lax.ppermute(array, "hel", [(i, i + step) for i in range(size) if 0 <= i + step < size])


def body(
    wavepacket,
    potential,
    kinetic,
    ang_basis,
    rot_energy,
    radial_weight,
    distance_weight,
    truncation,
    coupling,
):
    count, _, cells, _ = wavepacket.shape
    size = lax.axis_size("ang")
    me = lax.axis_index("ang")
    chunks = cells // size
    places = jnp.bitwise_xor(me, jnp.arange(size, dtype=jnp.int32))

    received = []
    for c in range(chunks):
        sent = pack(wavepacket, potential, c, places)
        received.append([sent[d] if d == 0 else partner(sent[d], "ang", d) for d in range(size)])

    orders = jnp.arange(ang_basis.shape[1], dtype=jnp.int32)
    mask = (orders[None, :] < truncation[:, None]).astype(jnp.float32)
    factor = mask * rot_energy[None, :]
    mats = jnp.einsum(
        "kji,kjm->kim", ang_basis * factor[:, :, None], ang_basis, precision=lax.Precision.HIGHEST
    )
    mats_below = along_hel(mats[-OUTER:], 1)
    mats_above = along_hel(mats[:OUTER], -1)

    first = lax.axis_index("hel") * count
    ends = jnp.concatenate([jnp.zeros((OUTER + 1,)), coupling[:-1], jnp.zeros((OUTER + 1,))])
    near = lax.dynamic_slice_in_dim(ends, first, count + 2 * OUTER + 1)
    out = None
    for c in range(chunks):
        pieces = received[c]
        if c:
            pieces = lax.optimization_barrier((*pieces, done[0]))[:-1]
        lows, highs = edges(pieces)
        below = along_hel(highs, 1)
        above = along_hel(lows, -1)
        weights = near * lax.dynamic_index_in_dim(distance_weight, c * size + me, keepdims=False)
        done = window(
            pieces, below, above, mats, mats_below, mats_above, kinetic, radial_weight[None], weights, places
        )
        back = [done[d] if d == 0 else partner(done[d], "ang", d) for d in range(size)]
        out = unpack(back, out, wavepacket.shape, c, places)
    return out


def solution(mesh):
    placed = (
        P("hel", "ang", None, None),
        P("ang", None, None),
        P(),
        P("hel", None, None),
        P(),
        P(),
        P(),
        P("hel"),
        P(),
    )
    whole = P("hel", "ang", None, None)
    return jax.shard_map(body, mesh=mesh, in_specs=placed, out_specs=whole, check_vma=False)
```

time: 756 us -> 567 us (0.75)
  the two profiles are of different devices: /device:TPU:6 before, /device:TPU:13 now
where the time goes in v1:
time: 567 us; the launch traced here: 566 us
  Pallas kernels  233 us (41%)
  waiting for transfers between devices  206 us (36%)
  starting transfers between devices  113 us (20%)
    ppermute x56, waiting for transfers between devices, partner(): return lax.ppermute(array, axis, [(i, i ^ bits) for i in range(size)])  206 us
    pallas_call x4, Pallas kernels, window(): pl.pallas_call(kernel, name='window', in_specs=[pl.BlockSpec(memory_space...  109 us
    pallas_call x4, Pallas kernels, edges(): pl.pallas_call(kernel, name='edges', in_specs=[anywhere] * size, out_spec...  100 us
    ppermute x56, starting transfers between devices, partner(): return lax.ppermute(array, axis, [(i, i ^ bits) for i in range(size)])  82.1 us
    ppermute x10, starting transfers between devices, along_hel(): lax.ppermute(array, 'hel', [(i, i + step) for i in range(size) if 0 <= i...  31.2 us
    pallas_call x4, Pallas kernels, pack(): pl.pallas_call(kernel, name='pack', grid=(width // LANES,), in_specs=[pl....  12 us
    pallas_call x4, Pallas kernels, unpack(): pl.pallas_call(kernel, name='unpack', grid=(width // LANES,), in_specs=sp...  11.6 us
  transfers between devices with their start and end apart: 66, of which 23 were waited for; matrix products, arithmetic and copies ran while one was open for 1% of the time, Pallas kernels for 41%

profile of v1, /device:TPU:13, one launch (start us, length us, event | category | flops | bytes accessed | tf_op | source)
XLA Modules:
  0.0 566.3 jit_solution(13679880729625500135)
XLA Ops:
  36.8 19.4 %collective-permute-done.25.refs_5_.refs_9_ = f32[17,16,256]{2,1,0:T(8,128)S(1)} collective-permute-done((f32[17,16,256]{2,1,0:T(8,128)}, f32[17,16,256]{2,1,0:T(8,128)S(1)}, u32[]{:S(2)}, u32[]{:S(2)}) %collective-permute-start.25) | collective-permute-done | bytes 278560 | tf_op jit(solution)/shard_map/ppermute | solution.py:16
  57.2 4.9 collective-permute-done.26.refs_6_.refs_10_
  62.8 11.4 %collective-permute-done.27.refs_7_.refs_11_ = f32[17,16,256]{2,1,0:T(8,128)S(1)} collective-permute-done((f32[17,16,256]{2,1,0:T(8,128)}, f32[17,16,256]{2,1,0:T(8,128)S(1)}, u32[]{:S(2)}, u32[]{:S(2)}) %collective-permute-start.27) | collective-permute-done | bytes 278560 | tf_op jit(solution)/shard_map/ppermute | solution.py:16
  77.6 25.1 %edges.4 = (f32[8,3,16,256]{3,2,1,0:T(8,128)}, f32[8,3,16,256]{3,2,1,0:T(8,128)}) custom-call(f32[17,16,256]{2,1,0:T(8,128)} %get-tuple-element.125.refs_0_.refs_4_, f32[17,16,256]{2,1,0:T(8,128)} %collective-permute-done.21.refs_1_.refs_5_, f32[17,16,256]{2,1,0:T(8,128)} %collective-permute-done.22.refs_2_.refs_6_, f32[17,16,256]{2,1,0:T(8,128)} %copy-done.18, ...), custom_call_target="tpu_custom_call" | custom-call | tf_op jit(solution)/shard_map/edges/pallas_call | solution.py:218
  105.0 4.1 collective-permute-start.29
  118.4 21.2 %collective-permute-done.10.refs_4_.refs_8_ = f32[17,16,256]{2,1,0:T(8,128)S(1)} collective-permute-done((f32[17,16,256]{2,1,0:T(8,128)}, f32[17,16,256]{2,1,0:T(8,128)S(1)}, u32[]{:S(2)}, u32[]{:S(2)}) %collective-permute-start.10) | collective-permute-done | bytes 278560 | tf_op jit(solution)/shard_map/ppermute | solution.py:16
  140.9 10.5 %collective-permute-done.11.refs_5_.refs_9_ = f32[17,16,256]{2,1,0:T(8,128)S(1)} collective-permute-done((f32[17,16,256]{2,1,0:T(8,128)}, f32[17,16,256]{2,1,0:T(8,128)S(1)}, u32[]{:S(2)}, u32[]{:S(2)}) %collective-permute-start.11) | collective-permute-done | bytes 278560 | tf_op jit(solution)/shard_map/ppermute | solution.py:16
  162.7 27.2 %window.4 = (f32[16,16,256]{2,1,0:T(8,128)}, f32[16,16,256]{2,1,0:T(8,128)}, f32[16,16,256]{2,1,0:T(8,128)}, f32[16,16,256]{2,1,0:T(8,128)}, f32[16,16,256]{2,1,...) custom-call(s32[8]{0:T(128)} %iota_xor_fusion.place_ref.refs_0_, ...), custom_call_target="tpu_custom_call" | custom-call | tf_op jit(solution)/shard_map/window/pallas_call | solution.py:174
  189.9 25.1 %edges.5 = (f32[8,3,16,256]{3,2,1,0:T(8,128)}, f32[8,3,16,256]{3,2,1,0:T(8,128)}) custom-call(f32[17,16,256]{2,1,0:T(8,128)} %get-tuple-element.136.refs_0_.refs_4_, f32[17,16,256]{2,1,0:T(8,128)} %copy-done.7, f32[17,16,256]{2,1,0:T(8,128)} %copy-done.9, f32[17,16,256]{2,1,0:T(8,128)} %copy-done.11, f32[17,16,256]{2,1,0:T(8,128)} %copy-done.12, ...), custom_call_target="tpu_custom_call" | custom-call | tf_op jit(solution)/shard_map/edges/pallas_call | solution.py:218
  225.7 7.3 %collective-permute-done.1.refs_2_.refs_6_ = f32[17,16,256]{2,1,0:T(8,128)S(1)} collective-permute-done((f32[17,16,256]{2,1,0:T(8,128)}, f32[17,16,256]{2,1,0:T(8,128)S(1)}, u32[]{:S(2)}, u32[]{:S(2)}) %collective-permute-start.1) | collective-permute-done | bytes 278560 | tf_op jit(solution)/shard_map/ppermute | solution.py:16
  233.0 6.6 %collective-permute-start.4 = (f32[17,16,256]{2,1,0:T(8,128)}, f32[17,16,256]{2,1,0:T(8,128)S(1)}, u32[]{:S(2)}, u32[]{:S(2)}) collective-permute-start(f32[17,16,256]{2,1,0:T(8,128)} %get-tuple-element.106), channel_id=1, source_target_pairs={{0,5},{1,4},{2,7},{3,6},{4,1},{5,0},{6,3},{7,2},{8,13},{9,12},{10,... | collective-permute-start | bytes 835592 | tf_op jit(solution)/shard_map/ppermute | solution.py:16
  248.8 27.2 %window.5 = (f32[16,16,256]{2,1,0:T(8,128)}, f32[16,16,256]{2,1,0:T(8,128)}, f32[16,16,256]{2,1,0:T(8,128)}, f32[16,16,256]{2,1,0:T(8,128)}, f32[16,16,256]{2,1,...) custom-call(s32[8]{0:T(128)} %iota_xor_fusion.place_ref.refs_0_, ...), custom_call_target="tpu_custom_call" | custom-call | tf_op jit(solution)/shard_map/window/pallas_call | solution.py:174
  276.1 25.1 %edges.6 = (f32[8,3,16,256]{3,2,1,0:T(8,128)}, f32[8,3,16,256]{3,2,1,0:T(8,128)}) custom-call(f32[17,16,256]{2,1,0:T(8,128)} %get-tuple-element.147.refs_0_.refs_4_, f32[17,16,256]{2,1,0:T(8,128)} %copy-done.10, f32[17,16,256]{2,1,0:T(8,128)} %copy-done.24, f32[17,16,256]{2,1,0:T(8,128)} %copy-done.27, f32[17,16,256]{2,1,0:T(8,128)} %copy-done.3, ...), custom_call_target="tpu_custom_call" | custom-call | tf_op jit(solution)/shard_map/edges/pallas_call | solution.py:218
  303.2 4.4 collective-permute-start.35
  311.7 9.5 %collective-permute-done.61.refs_3_ = f32[16,16,256]{2,1,0:T(8,128)S(1)} collective-permute-done((f32[16,16,256]{2,1,0:T(8,128)}, f32[16,16,256]{2,1,0:T(8,128)S(1)}, u32[]{:S(2)}, u32[]{:S(2)}) %collective-permute-start.61) | collective-permute-done | bytes 262176 | tf_op jit(solution)/shard_map/ppermute | solution.py:16
  321.3 12.6 %collective-permute-done.62.refs_4_ = f32[16,16,256]{2,1,0:T(8,128)S(1)} collective-permute-done((f32[16,16,256]{2,1,0:T(8,128)}, f32[16,16,256]{2,1,0:T(8,128)S(1)}, u32[]{:S(2)}, u32[]{:S(2)}) %collective-permute-start.62) | collective-permute-done | bytes 262176 | tf_op jit(solution)/shard_map/ppermute | solution.py:16
  334.0 5.5 collective-permute-done.63.refs_5_
  339.5 7.2 %collective-permute-start.52 = (f32[16,16,256]{2,1,0:T(8,128)}, f32[16,16,256]{2,1,0:T(8,128)S(1)}, u32[]{:S(2)}, u32[]{:S(2)}) collective-permute-start(f32[16,16,256]{2,1,0:T(8,128)} %get-tuple-element.183), channel_id=1, source_target_pairs={{0,1},{1,0},{2,3},{3,2},{4,5},{5,4},{6,7},{7,6},{8,9},{9,8},{10,11... | collective-permute-start | bytes 786440 | tf_op jit(solution)/shard_map/ppermute | solution.py:16
  349.1 27.1 %window.6 = (f32[16,16,256]{2,1,0:T(8,128)}, f32[16,16,256]{2,1,0:T(8,128)}, f32[16,16,256]{2,1,0:T(8,128)}, f32[16,16,256]{2,1,0:T(8,128)}, f32[16,16,256]{2,1,...) custom-call(s32[8]{0:T(128)} %iota_xor_fusion.place_ref.refs_0_, ...), custom_call_target="tpu_custom_call" | custom-call | tf_op jit(solution)/shard_map/window/pallas_call | solution.py:174
  376.3 25.1 %edges.7 = (f32[8,3,16,256]{3,2,1,0:T(8,128)}, f32[8,3,16,256]{3,2,1,0:T(8,128)}) custom-call(f32[17,16,256]{2,1,0:T(8,128)} %get-tuple-element.158.refs_0_.refs_4_, f32[17,16,256]{2,1,0:T(8,128)} %copy-done.6, f32[17,16,256]{2,1,0:T(8,128)} %copy-done.16, f32[17,16,256]{2,1,0:T(8,128)} %copy-done.17, f32[17,16,256]{2,1,0:T(8,128)} %copy-done.19, ...), custom_call_target="tpu_custom_call" | custom-call | tf_op jit(solution)/shard_map/edges/pallas_call | solution.py:218
  403.4 4.3 collective-permute-start.37
  412.6 20.3 %collective-permute-done.55.refs_4_ = f32[16,16,256]{2,1,0:T(8,128)S(1)} collective-permute-done((f32[16,16,256]{2,1,0:T(8,128)}, f32[16,16,256]{2,1,0:T(8,128)S(1)}, u32[]{:S(2)}, u32[]{:S(2)}) %collective-permute-start.55) | collective-permute-done | bytes 262176 | tf_op jit(solution)/shard_map/ppermute | solution.py:16
  433.8 10.1 %collective-permute-done.56.refs_5_ = f32[16,16,256]{2,1,0:T(8,128)S(1)} collective-permute-done((f32[16,16,256]{2,1,0:T(8,128)}, f32[16,16,256]{2,1,0:T(8,128)S(1)}, u32[]{:S(2)}, u32[]{:S(2)}) %collective-permute-start.56) | collective-permute-done | bytes 262176 | tf_op jit(solution)/shard_map/ppermute | solution.py:16
  444.5 5.9 %collective-permute-done.57.refs_6_ = f32[16,16,256]{2,1,0:T(8,128)S(1)} collective-permute-done((f32[16,16,256]{2,1,0:T(8,128)}, f32[16,16,256]{2,1,0:T(8,128)S(1)}, u32[]{:S(2)}, u32[]{:S(2)}) %collective-permute-start.57) | collective-permute-done | bytes 262176 | tf_op jit(solution)/shard_map/ppermute | solution.py:16
  453.8 27.2 %window.7 = (f32[16,16,256]{2,1,0:T(8,128)}, f32[16,16,256]{2,1,0:T(8,128)}, f32[16,16,256]{2,1,0:T(8,128)}, f32[16,16,256]{2,1,0:T(8,128)}, f32[16,16,256]{2,1,...) custom-call(s32[8]{0:T(128)} %iota_xor_fusion.place_ref.refs_0_, ...), custom_call_target="tpu_custom_call" | custom-call | tf_op jit(solution)/shard_map/window/pallas_call | solution.py:174
  487.1 17.5 %collective-permute-done.49.refs_5_ = f32[16,16,256]{2,1,0:T(8,128)S(1)} collective-permute-done((f32[16,16,256]{2,1,0:T(8,128)}, f32[16,16,256]{2,1,0:T(8,128)S(1)}, u32[]{:S(2)}, u32[]{:S(2)}) %collective-permute-start.49) | collective-permute-done | bytes 262176 | tf_op jit(solution)/shard_map/ppermute | solution.py:16
  508.6 4.2 collective-permute-done.50.refs_6_
  512.8 11.5 %collective-permute-done.51.refs_7_ = f32[16,16,256]{2,1,0:T(8,128)S(1)} collective-permute-done((f32[16,16,256]{2,1,0:T(8,128)}, f32[16,16,256]{2,1,0:T(8,128)S(1)}, u32[]{:S(2)}, u32[]{:S(2)}) %collective-permute-start.51) | collective-permute-done | bytes 262176 | tf_op jit(solution)/shard_map/ppermute | solution.py:16
  535.0 9.0 %collective-permute-done.41.refs_4_ = f32[16,16,256]{2,1,0:T(8,128)} collective-permute-done((f32[16,16,256]{2,1,0:T(8,128)}, f32[16,16,256]{2,1,0:T(8,128)}, u32[]{:S(2)}, u32[]{:S(2)}) %collective-permute-start.41) | collective-permute-done | bytes 262176 | tf_op jit(solution)/shard_map/ppermute | solution.py:16
  544.0 5.6 collective-permute-done.42.refs_5_
  549.6 8.2 %collective-permute-done.43.refs_6_ = f32[16,16,256]{2,1,0:T(8,128)} collective-permute-done((f32[16,16,256]{2,1,0:T(8,128)}, f32[16,16,256]{2,1,0:T(8,128)}, u32[]{:S(2)}, u32[]{:S(2)}) %collective-permute-start.43) | collective-permute-done | bytes 262176 | tf_op jit(solution)/shard_map/ppermute | solution.py:16
  557.7 5.7 collective-permute-done.44.refs_7_
  (231 shorter events, 129.5 us)
Async XLA Ops:
  24.0 50.2 %collective-permute-start.27 = (f32[17,16,256]{2,1,0:T(8,128)}, f32[17,16,256]{2,1,0:T(8,128)S(1)}, u32[]{:S(2)}, u32[]{:S(2)}) collective-permute-start(f32[17,16,256]{2,1,0:T(8,128)} %get-tuple-element.132), channel_id=1, source_target_pairs={{0,7},{1,6},{2,5},{3,4},{4,3},{5,2},{6,1},{7,0},{8,15},{9,14},{10,... | collective-permute-start | bytes 835592 | tf_op jit(solution)/shard_map/ppermute | solution.py:16
  33.4 41.6 %collective-permute-start.14 = (f32[17,16,256]{2,1,0:T(8,128)}, f32[17,16,256]{2,1,0:T(8,128)S(1)}, u32[]{:S(2)}, u32[]{:S(2)}) collective-permute-start(f32[17,16,256]{2,1,0:T(8,128)} %get-tuple-element.118), channel_id=1, source_target_pairs={{0,1},{1,0},{2,3},{3,2},{4,5},{5,4},{6,7},{7,6},{8,9},{9,8},{10,11... | collective-permute-start | bytes 835592 | tf_op jit(solution)/shard_map/ppermute | solution.py:16
  35.0 42.2 %collective-permute-start.15 = (f32[17,16,256]{2,1,0:T(8,128)}, f32[17,16,256]{2,1,0:T(8,128)S(1)}, u32[]{:S(2)}, u32[]{:S(2)}) collective-permute-start(f32[17,16,256]{2,1,0:T(8,128)} %get-tuple-element.119), channel_id=1, source_target_pairs={{0,2},{1,3},{2,0},{3,1},{4,6},{5,7},{6,4},{7,5},{8,10},{9,11},{10,... | collective-permute-start | bytes 835592 | tf_op jit(solution)/shard_map/ppermute | solution.py:16
  56.1 46.5 %collective-permute-start.16 = (f32[17,16,256]{2,1,0:T(8,128)}, f32[17,16,256]{2,1,0:T(8,128)S(1)}, u32[]{:S(2)}, u32[]{:S(2)}) collective-permute-start(f32[17,16,256]{2,1,0:T(8,128)} %get-tuple-element.120), channel_id=1, source_target_pairs={{0,3},{1,2},{2,1},{3,0},{4,7},{5,6},{6,5},{7,4},{8,11},{9,10},{10,... | collective-permute-start | bytes 835592 | tf_op jit(solution)/shard_map/ppermute | solution.py:16
  62.8 42.1 %collective-permute-start.17 = (f32[17,16,256]{2,1,0:T(8,128)}, f32[17,16,256]{2,1,0:T(8,128)S(1)}, u32[]{:S(2)}, u32[]{:S(2)}) collective-permute-start(f32[17,16,256]{2,1,0:T(8,128)} %get-tuple-element.121), channel_id=1, source_target_pairs={{0,4},{1,5},{2,6},{3,7},{4,0},{5,1},{6,2},{7,3},{8,12},{9,13},{10,... | collective-permute-start | bytes 835592 | tf_op jit(solution)/shard_map/ppermute | solution.py:16
  75.0 40.9 %collective-permute-start.19 = (f32[17,16,256]{2,1,0:T(8,128)}, f32[17,16,256]{2,1,0:T(8,128)S(1)}, u32[]{:S(2)}, u32[]{:S(2)}) collective-permute-start(f32[17,16,256]{2,1,0:T(8,128)} %get-tuple-element.123), channel_id=1, source_target_pairs={{0,6},{1,7},{2,4},{3,5},{4,2},{5,3},{6,0},{7,1},{8,14},{9,15},{10,... | collective-permute-start | bytes 835592 | tf_op jit(solution)/shard_map/ppermute | solution.py:16
  77.3 39.7 %collective-permute-start.20 = (f32[17,16,256]{2,1,0:T(8,128)}, f32[17,16,256]{2,1,0:T(8,128)S(1)}, u32[]{:S(2)}, u32[]{:S(2)}) collective-permute-start(f32[17,16,256]{2,1,0:T(8,128)} %get-tuple-element.124), channel_id=1, source_target_pairs={{0,7},{1,6},{2,5},{3,4},{4,3},{5,2},{6,1},{7,0},{8,15},{9,14},{10,... | collective-permute-start | bytes 835592 | tf_op jit(solution)/shard_map/ppermute | solution.py:16
  102.7 56.4 %collective-permute-start.28 = (f32[8,3,16,256]{3,2,1,0:T(8,128)}, f32[8,3,16,256]{3,2,1,0:T(8,128)}, u32[]{:S(2)}, u32[]{:S(2)}) collective-permute-start(f32[8,3,16,256]{3,2,1,0:T(8,128)} %get-tuple-element.133), channel_id=1, source_target_pairs={{0,8},{8,16},{16,24},{1,9},{9,17},{17,25},{2,10},{10,18},{18,26},{... | collective-permute-start | bytes 1179656 | tf_op jit(solution)/shard_map/ppermute | solution.py:230
  105.0 56.4 %collective-permute-start.29 = (f32[8,3,16,256]{3,2,1,0:T(8,128)}, f32[8,3,16,256]{3,2,1,0:T(8,128)}, u32[]{:S(2)}, u32[]{:S(2)}) collective-permute-start(f32[8,3,16,256]{3,2,1,0:T(8,128)} %get-tuple-element.134), channel_id=1, source_target_pairs={{8,0},{16,8},{24,16},{9,1},{17,9},{25,17},{10,2},{18,10},{26,18},{... | collective-permute-start | bytes 1179656 | tf_op jit(solution)/shard_map/ppermute | solution.py:230
  117.0 42.0 %collective-permute-start.12 = (f32[17,16,256]{2,1,0:T(8,128)}, f32[17,16,256]{2,1,0:T(8,128)S(1)}, u32[]{:S(2)}, u32[]{:S(2)}) collective-permute-start(f32[17,16,256]{2,1,0:T(8,128)} %get-tuple-element.115), channel_id=1, source_target_pairs={{0,6},{1,7},{2,4},{3,5},{4,2},{5,3},{6,0},{7,1},{8,14},{9,15},{10,... | collective-permute-start | bytes 835592 | tf_op jit(solution)/shard_map/ppermute | solution.py:16
  139.7 75.3 %collective-permute-start.13 = (f32[17,16,256]{2,1,0:T(8,128)}, f32[17,16,256]{2,1,0:T(8,128)S(1)}, u32[]{:S(2)}, u32[]{:S(2)}) collective-permute-start(f32[17,16,256]{2,1,0:T(8,128)} %get-tuple-element.116), channel_id=1, source_target_pairs={{0,7},{1,6},{2,5},{3,4},{4,3},{5,2},{6,1},{7,0},{8,15},{9,14},{10,... | collective-permute-start | bytes 835592 | tf_op jit(solution)/shard_map/ppermute | solution.py:16
  151.5 65.7 %collective-permute-start.7 = (f32[17,16,256]{2,1,0:T(8,128)}, f32[17,16,256]{2,1,0:T(8,128)S(1)}, u32[]{:S(2)}, u32[]{:S(2)}) collective-permute-start(f32[17,16,256]{2,1,0:T(8,128)} %get-tuple-element.110), channel_id=1, source_target_pairs={{0,1},{1,0},{2,3},{3,2},{4,5},{5,4},{6,7},{7,6},{8,9},{9,8},{10,11... | collective-permute-start | bytes 835592 | tf_op jit(solution)/shard_map/ppermute | solution.py:16
  159.0 62.2 %collective-permute-start.8 = (f32[17,16,256]{2,1,0:T(8,128)}, f32[17,16,256]{2,1,0:T(8,128)S(1)}, u32[]{:S(2)}, u32[]{:S(2)}) collective-permute-start(f32[17,16,256]{2,1,0:T(8,128)} %get-tuple-element.111), channel_id=1, source_target_pairs={{0,2},{1,3},{2,0},{3,1},{4,6},{5,7},{6,4},{7,5},{8,10},{9,11},{10,... | collective-permute-start | bytes 835592 | tf_op jit(solution)/shard_map/ppermute | solution.py:16
  159.0 62.5 %collective-permute-start.9 = (f32[17,16,256]{2,1,0:T(8,128)}, f32[17,16,256]{2,1,0:T(8,128)S(1)}, u32[]{:S(2)}, u32[]{:S(2)}) collective-permute-start(f32[17,16,256]{2,1,0:T(8,128)} %get-tuple-element.112), channel_id=1, source_target_pairs={{0,3},{1,2},{2,1},{3,0},{4,7},{5,6},{6,5},{7,4},{8,11},{9,10},{10,... | collective-permute-start | bytes 835592 | tf_op jit(solution)/shard_map/ppermute | solution.py:16
  161.4 62.6 %collective-permute-start = (f32[17,16,256]{2,1,0:T(8,128)}, f32[17,16,256]{2,1,0:T(8,128)S(1)}, u32[]{:S(2)}, u32[]{:S(2)}) collective-permute-start(f32[17,16,256]{2,1,0:T(8,128)} %get-tuple-element.102), channel_id=1, source_target_pairs={{0,1},{1,0},{2,3},{3,2},{4,5},{5,4},{6,7},{7,6},{8,9},{9,8},{10,11... | collective-permute-start | bytes 835592 | tf_op jit(solution)/shard_map/ppermute | solution.py:16
  233.0 68.2 %collective-permute-start.4 = (f32[17,16,256]{2,1,0:T(8,128)}, f32[17,16,256]{2,1,0:T(8,128)S(1)}, u32[]{:S(2)}, u32[]{:S(2)}) collective-permute-start(f32[17,16,256]{2,1,0:T(8,128)} %get-tuple-element.106), channel_id=1, source_target_pairs={{0,5},{1,4},{2,7},{3,6},{4,1},{5,0},{6,3},{7,2},{8,13},{9,12},{10,... | collective-permute-start | bytes 835592 | tf_op jit(solution)/shard_map/ppermute | solution.py:16
  239.6 63.6 %collective-permute-start.5 = (f32[17,16,256]{2,1,0:T(8,128)}, f32[17,16,256]{2,1,0:T(8,128)S(1)}, u32[]{:S(2)}, u32[]{:S(2)}) collective-permute-start(f32[17,16,256]{2,1,0:T(8,128)} %get-tuple-element.107), channel_id=1, source_target_pairs={{0,6},{1,7},{2,4},{3,5},{4,2},{5,3},{6,0},{7,1},{8,14},{9,15},{10,... | collective-permute-start | bytes 835592 | tf_op jit(solution)/shard_map/ppermute | solution.py:16
  242.5 65.1 %collective-permute-start.6 = (f32[17,16,256]{2,1,0:T(8,128)}, f32[17,16,256]{2,1,0:T(8,128)S(1)}, u32[]{:S(2)}, u32[]{:S(2)}) collective-permute-start(f32[17,16,256]{2,1,0:T(8,128)} %get-tuple-element.108), channel_id=1, source_target_pairs={{0,7},{1,6},{2,5},{3,4},{4,3},{5,2},{6,1},{7,0},{8,15},{9,14},{10,... | collective-permute-start | bytes 835592 | tf_op jit(solution)/shard_map/ppermute | solution.py:16
  245.2 64.4 %collective-permute-start.59 = (f32[16,16,256]{2,1,0:T(8,128)}, f32[16,16,256]{2,1,0:T(8,128)}, u32[]{:S(2)}, u32[]{:S(2)}) collective-permute-start(f32[16,16,256]{2,1,0:T(8,128)} %get-tuple-element.190), channel_id=1, source_target_pairs={{0,1},{1,0},{2,3},{3,2},{4,5},{5,4},{6,7},{7,6},{8,9},{9,8},{10,11... | collective-permute-start | bytes 786440 | tf_op jit(solution)/shard_map/ppermute | solution.py:16
  246.1 65.1 %collective-permute-start.60 = (f32[16,16,256]{2,1,0:T(8,128)}, f32[16,16,256]{2,1,0:T(8,128)}, u32[]{:S(2)}, u32[]{:S(2)}) collective-permute-start(f32[16,16,256]{2,1,0:T(8,128)} %get-tuple-element.191), channel_id=1, source_target_pairs={{0,2},{1,3},{2,0},{3,1},{4,6},{5,7},{6,4},{7,5},{8,10},{9,11},{10,... | collective-permute-start | bytes 786440 | tf_op jit(solution)/shard_map/ppermute | solution.py:16
  301.2 45.4 %collective-permute-start.34 = (f32[8,3,16,256]{3,2,1,0:T(8,128)}, f32[8,3,16,256]{3,2,1,0:T(8,128)S(1)}, u32[]{:S(2)}, u32[]{:S(2)}) collective-permute-start(f32[8,3,16,256]{3,2,1,0:T(8,128)} %get-tuple-element.155), channel_id=1, source_target_pairs={{0,8},{8,16},{16,24},{1,9},{9,17},{17,25},{2,10},{10,18},{18,26},{... | collective-permute-start | bytes 1179656 | tf_op jit(solution)/shard_map/ppermute | solution.py:230
  303.2 45.2 %collective-permute-start.35 = (f32[8,3,16,256]{3,2,1,0:T(8,128)}, f32[8,3,16,256]{3,2,1,0:T(8,128)S(1)}, u32[]{:S(2)}, u32[]{:S(2)}) collective-permute-start(f32[8,3,16,256]{3,2,1,0:T(8,128)} %get-tuple-element.156), channel_id=1, source_target_pairs={{8,0},{16,8},{24,16},{9,1},{17,9},{25,17},{10,2},{18,10},{26,18},{... | collective-permute-start | bytes 1179656 | tf_op jit(solution)/shard_map/ppermute | solution.py:230
  321.2 80.2 %collective-permute-start.64 = (f32[16,16,256]{2,1,0:T(8,128)}, f32[16,16,256]{2,1,0:T(8,128)}, u32[]{:S(2)}, u32[]{:S(2)}) collective-permute-start(f32[16,16,256]{2,1,0:T(8,128)} %get-tuple-element.195), channel_id=1, source_target_pairs={{0,6},{1,7},{2,4},{3,5},{4,2},{5,3},{6,0},{7,1},{8,14},{9,15},{10,... | collective-permute-start | bytes 786440 | tf_op jit(solution)/shard_map/ppermute | solution.py:16
  333.9 69.4 %collective-permute-start.65 = (f32[16,16,256]{2,1,0:T(8,128)}, f32[16,16,256]{2,1,0:T(8,128)}, u32[]{:S(2)}, u32[]{:S(2)}) collective-permute-start(f32[16,16,256]{2,1,0:T(8,128)} %get-tuple-element.196), channel_id=1, source_target_pairs={{0,7},{1,6},{2,5},{3,4},{4,3},{5,2},{6,1},{7,0},{8,15},{9,14},{10,... | collective-permute-start | bytes 786440 | tf_op jit(solution)/shard_map/ppermute | solution.py:16
  339.5 68.2 %collective-permute-start.52 = (f32[16,16,256]{2,1,0:T(8,128)}, f32[16,16,256]{2,1,0:T(8,128)S(1)}, u32[]{:S(2)}, u32[]{:S(2)}) collective-permute-start(f32[16,16,256]{2,1,0:T(8,128)} %get-tuple-element.183), channel_id=1, source_target_pairs={{0,1},{1,0},{2,3},{3,2},{4,5},{5,4},{6,7},{7,6},{8,9},{9,8},{10,11... | collective-permute-start | bytes 786440 | tf_op jit(solution)/shard_map/ppermute | solution.py:16
  346.7 63.2 %collective-permute-start.53 = (f32[16,16,256]{2,1,0:T(8,128)}, f32[16,16,256]{2,1,0:T(8,128)S(1)}, u32[]{:S(2)}, u32[]{:S(2)}) collective-permute-start(f32[16,16,256]{2,1,0:T(8,128)} %get-tuple-element.184), channel_id=1, source_target_pairs={{0,2},{1,3},{2,0},{3,1},{4,6},{5,7},{6,4},{7,5},{8,10},{9,11},{10,... | collective-permute-start | bytes 786440 | tf_op jit(solution)/shard_map/ppermute | solution.py:16
  348.4 62.8 %collective-permute-start.54 = (f32[16,16,256]{2,1,0:T(8,128)}, f32[16,16,256]{2,1,0:T(8,128)}, u32[]{:S(2)}, u32[]{:S(2)}) collective-permute-start(f32[16,16,256]{2,1,0:T(8,128)} %get-tuple-element.185), channel_id=1, source_target_pairs={{0,3},{1,2},{2,1},{3,0},{4,7},{5,6},{6,5},{7,4},{8,11},{9,10},{10,... | collective-permute-start | bytes 786440 | tf_op jit(solution)/shard_map/ppermute | solution.py:16
  401.4 49.0 %collective-permute-start.36 = (f32[8,3,16,256]{3,2,1,0:T(8,128)}, f32[8,3,16,256]{3,2,1,0:T(8,128)S(1)}, u32[]{:S(2)}, u32[]{:S(2)}) collective-permute-start(f32[8,3,16,256]{3,2,1,0:T(8,128)} %get-tuple-element.166), channel_id=1, source_target_pairs={{0,8},{8,16},{16,24},{1,9},{9,17},{17,25},{2,10},{10,18},{18,26},{... | collective-permute-start | bytes 1179656 | tf_op jit(solution)/shard_map/ppermute | solution.py:230
  403.4 49.6 %collective-permute-start.37 = (f32[8,3,16,256]{3,2,1,0:T(8,128)}, f32[8,3,16,256]{3,2,1,0:T(8,128)S(1)}, u32[]{:S(2)}, u32[]{:S(2)}) collective-permute-start(f32[8,3,16,256]{3,2,1,0:T(8,128)} %get-tuple-element.167), channel_id=1, source_target_pairs={{8,0},{16,8},{24,16},{9,1},{17,9},{25,17},{10,2},{18,10},{26,18},{... | collective-permute-start | bytes 1179656 | tf_op jit(solution)/shard_map/ppermute | solution.py:230
  432.8 48.1 %collective-permute-start.58 = (f32[16,16,256]{2,1,0:T(8,128)}, f32[16,16,256]{2,1,0:T(8,128)S(1)}, u32[]{:S(2)}, u32[]{:S(2)}) collective-permute-start(f32[16,16,256]{2,1,0:T(8,128)} %get-tuple-element.189), channel_id=1, source_target_pairs={{0,7},{1,6},{2,5},{3,4},{4,3},{5,2},{6,1},{7,0},{8,15},{9,14},{10,... | collective-permute-start | bytes 786440 | tf_op jit(solution)/shard_map/ppermute | solution.py:16
  483.5 40.8 %collective-permute-start.51 = (f32[16,16,256]{2,1,0:T(8,128)}, f32[16,16,256]{2,1,0:T(8,128)S(1)}, u32[]{:S(2)}, u32[]{:S(2)}) collective-permute-start(f32[16,16,256]{2,1,0:T(8,128)} %get-tuple-element.182), channel_id=1, source_target_pairs={{0,7},{1,6},{2,5},{3,4},{4,3},{5,2},{6,1},{7,0},{8,15},{9,14},{10,... | collective-permute-start | bytes 786440 | tf_op jit(solution)/shard_map/ppermute | solution.py:16
  484.7 40.2 %collective-permute-start.39 = (f32[16,16,256]{2,1,0:T(8,128)}, f32[16,16,256]{2,1,0:T(8,128)S(1)}, u32[]{:S(2)}, u32[]{:S(2)}) collective-permute-start(f32[16,16,256]{2,1,0:T(8,128)} %get-tuple-element.170), channel_id=1, source_target_pairs={{0,2},{1,3},{2,0},{3,1},{4,6},{5,7},{6,4},{7,5},{8,10},{9,11},{10,... | collective-permute-start | bytes 786440 | tf_op jit(solution)/shard_map/ppermute | solution.py:16
  (87 other events, 3852.5 us)

commit v2 on v1

--- a/solution.py
+++ b/solution.py
@@ -1,3 +1,5 @@
+import math
+
 import jax
 import jax.numpy as jnp
 from jax import lax
@@ -16,31 +18,55 @@
     return lax.ppermute(array, axis, [(i, i ^ bits) for i in range(size)])
 
 
-def pack(wave, potential, chunk, places):
-    count, angles, _, width = wave.shape
+def swap(arrays, axis, ranks):
+    swapped = {d: partner(arrays[d], axis, d) for d in ranks}
+    return [swapped.get(d, arrays[d]) for d in range(len(arrays))]
+
+
+def spread_potential(potential, chunks, places):
+    size, groups = lax.axis_size("ang"), lax.axis_size("hel")
+    if chunks != groups:
+        packed = pack(potential, tuple(range(chunks)), places)
+        pieces = swap(packed, "ang", range(1, size))
+        return [jnp.stack([piece[c] for piece in pieces]) for c in range(chunks)]
+    group = lax.axis_index("hel")
+    own = lax.dynamic_slice_in_dim(potential, group * size, size, axis=1)
+    packed = pack(own, (0,), places)
+    pieces = swap(packed, "ang", range(1, size))
+    mine = jnp.concatenate(pieces)
+    known = jnp.stack(swap([mine] * groups, "hel", range(1, groups)))
+    return [lax.dynamic_index_in_dim(known, jnp.bitwise_xor(group, c), keepdims=False) for c in range(chunks)]
+
+
+def pack(array, chunks, places):
+    *_, angles, cells, width = array.shape
+    lead = array.shape[:-3]
+    count = math.prod(lead)
     size = lax.axis_size("ang")
 
-    def kernel(place_ref, wave_ref, pot_ref, *outs):
+    def kernel(place_ref, *refs):
+        ins, outs = refs[: len(chunks)], refs[len(chunks) :]
         for d in range(size):
             start = place_ref[d]
-            for k in range(count):
-                rows = wave_ref.at[k].reshape(angles * size, LANES)
-                outs[d][k] = rows[pl.ds(start, angles, stride=size), :]
-            rows = pot_ref.reshape(angles * size, LANES)
-            outs[d][count] = rows[pl.ds(start, angles, stride=size), :]
-
+            for c, block in enumerate(ins):
+                for k in range(count):
+                    view = block.at[k] if lead else block
+                    rows = view.reshape(angles * size, LANES)
+                    outs[d][c * count + k] = rows[pl.ds(start, angles, stride=size), :]
+
+    def spec(chunk):
+        shape = (*lead, angles, size, LANES)
+        return pl.BlockSpec(shape, lambda g: (*(0 for _ in lead), 0, chunk, g))
+
+    packed = (len(chunks) * count, angles, width)
     return pl.pallas_call(
         kernel,
         name="pack",
         grid=(width // LANES,),
-        in_specs=[
-            pl.BlockSpec(memory_space=pltpu.SMEM),
-            pl.BlockSpec((count, angles, size, LANES), lambda g: (0, 0, chunk, g)),
-            pl.BlockSpec((angles, size, LANES), lambda g: (0, chunk, g)),
-        ],
-        out_specs=[pl.BlockSpec((count + 1, angles, LANES), lambda g: (0, 0, g))] * size,
-        out_shape=[jax.ShapeDtypeStruct((count + 1, angles, width), jnp.float32)] * size,
-    )(places, wave, potential)
+        in_specs=[pl.BlockSpec(memory_space=pltpu.SMEM)] + [spec(chunk) for chunk in chunks],
+        out_specs=[pl.BlockSpec((packed[0], angles, LANES), lambda g: (0, 0, g))] * size,
+        out_shape=[jax.ShapeDtypeStruct(packed, jnp.float32)] * size,
+    )(places, *[array] * len(chunks))
 
 
 def unpack(pieces, whole, shape, chunk, places):
@@ -80,19 +106,18 @@
     return high, (values - high.astype(jnp.float32)).astype(jnp.bfloat16)
 
 
-def window(pieces, below, above, mats, mats_below, mats_above, kinetic, radial, weights, places):
+def window(pieces, potential, below, above, mats, mats_below, mats_above, kinetic, radial, weights, places):
     size = len(pieces)
     count, angles, width = pieces[0].shape
-    count -= 1
     full = size * angles
     total = count + 2 * OUTER
 
     def kernel(*refs):
         place_ref, weight_ref, kin_ref, rad_ref = refs[:4]
         ins = refs[4 : 4 + size]
-        below_ref, above_ref, mat_ref, mat_below_ref, mat_above_ref = refs[4 + size : 9 + size]
-        outs = refs[9 + size : 9 + 2 * size]
-        one, two, mat, pot, kin, sems = refs[9 + 2 * size :]
+        pot_ref, below_ref, above_ref, mat_ref, mat_below_ref, mat_above_ref = refs[4 + size : 10 + size]
+        outs = refs[10 + size : 10 + 2 * size]
+        one, two, mat, pot, kin, sems = refs[10 + 2 * size :]
         copies = []
 
         def fetch(source, target):
@@ -104,8 +129,8 @@
             return pl.ds(pl.multiple_of(place_ref[d] * angles, angles), angles)
 
         for d in range(size):
-            fetch(ins[d].at[pl.ds(0, count)], one.at[pl.ds(OUTER, count), spot(d), :])
-            fetch(ins[d].at[count], pot.at[spot(d), :])
+            fetch(ins[d], one.at[pl.ds(OUTER, count), spot(d), :])
+            fetch(pot_ref.at[d], pot.at[spot(d), :])
             fetch(below_ref.at[d], one.at[pl.ds(0, OUTER), spot(d), :])
             fetch(above_ref.at[d], one.at[pl.ds(OUTER + count, OUTER), spot(d), :])
         fetch(mat_below_ref, mat.at[pl.ds(0, OUTER)])
@@ -180,7 +205,7 @@
             pl.BlockSpec(memory_space=pltpu.VMEM),
             pl.BlockSpec(memory_space=pltpu.VMEM),
         ]
-        + [anywhere] * (size + 5),
+        + [anywhere] * (size + 6),
         out_specs=[anywhere] * size,
         out_shape=[jax.ShapeDtypeStruct((count, angles, width), jnp.float32)] * size,
         scratch_shapes=[
@@ -191,13 +216,12 @@
             pltpu.VMEM((2, width, width), jnp.bfloat16),
             pltpu.SemaphoreType.DMA((4 * size + 3,)),
         ],
-    )(places, weights, kinetic, radial, *pieces, below, above, mats, mats_below, mats_above)
+    )(places, weights, kinetic, radial, *pieces, potential, below, above, mats, mats_below, mats_above)
 
 
 def edges(pieces):
     size = len(pieces)
     count, angles, width = pieces[0].shape
-    count -= 1
 
     def kernel(*refs):
         ins, lows, highs, sems = refs[:size], refs[size], refs[size + 1], refs[size + 2]
@@ -219,7 +243,7 @@
         kernel,
         name="edges",
         in_specs=[anywhere] * size,
-        out_specs=[anywhere] * 2,
+        out_specs=[pl.BlockSpec(memory_space=pltpu.VMEM)] * 2,
         out_shape=[shape] * 2,
         scratch_shapes=[pltpu.SemaphoreType.DMA((2 * size,))],
     )(*pieces)
@@ -247,10 +271,13 @@
     chunks = cells // size
     places = jnp.bitwise_xor(me, jnp.arange(size, dtype=jnp.int32))
 
+    ranks = sorted(range(1, size), key=lambda d: -(d // 2))
     received = []
     for c in range(chunks):
-        sent = pack(wavepacket, potential, c, places)
-        received.append([sent[d] if d == 0 else partner(sent[d], "ang", d) for d in range(size)])
+        sent = pack(wavepacket, (c,), places)
+        received.append(swap(sent, "ang", ranks))
+        if c == 0:
+            potentials = spread_potential(potential, chunks, places)
 
     orders = jnp.arange(ang_basis.shape[1], dtype=jnp.int32)
     mask = (orders[None, :] < truncation[:, None]).astype(jnp.float32)
@@ -264,20 +291,41 @@
     first = lax.axis_index("hel") * count
     ends = jnp.concatenate([jnp.zeros((OUTER + 1,)), coupling[:-1], jnp.zeros((OUTER + 1,))])
     near = lax.dynamic_slice_in_dim(ends, first, count + 2 * OUTER + 1)
+    halos = {}
+    done = {}
+
+    def exchange(c):
+        pieces = received[c]
+        if c >= 2:
+            pieces = lax.optimization_barrier((*pieces, done[c - 2][0]))[:-1]
+        lows, highs = edges(pieces)
+        halos[c] = pieces, along_hel(highs, 1), along_hel(lows, -1), lows
+
+    exchange(0)
+    backs = []
+    for c in range(chunks):
+        weights = near * lax.dynamic_index_in_dim(distance_weight, c * size + me, keepdims=False)
+        pieces, below, above, _ = halos[c]
+        if c + 1 < chunks:
+            exchange(c + 1)
+            weights, _ = lax.optimization_barrier((weights, halos[c + 1][3]))
+        done[c] = window(
+            pieces,
+            potentials[c],
+            below,
+            above,
+            mats,
+            mats_below,
+            mats_above,
+            kinetic,
+            radial_weight[None],
+            weights,
+            places,
+        )
+        backs.append(swap(done[c], "ang", ranks))
     out = None
     for c in range(chunks):
-        pieces = received[c]
-        if c:
-            pieces = lax.optimization_barrier((*pieces, done[0]))[:-1]
-        lows, highs = edges(pieces)
-        below = along_hel(highs, 1)
-        above = along_hel(lows, -1)
-        weights = near * lax.dynamic_index_in_dim(distance_weight, c * size + me, keepdims=False)
-        done = window(
-            pieces, below, above, mats, mats_below, mats_above, kinetic, radial_weight[None], weights, places
-        )
-        back = [done[d] if d == 0 else partner(done[d], "ang", d) for d in range(size)]
-        out = unpack(back, out, wavepacket.shape, c, places)
+        out = unpack(backs[c], out, wavepacket.shape, c, places)
     return out
 
 

time: 567 us -> 475 us (0.84)
  Pallas kernels: 233 us -> 142 us
  waiting for transfers between devices: 206 us -> 182 us
  starting transfers between devices: 113 us -> 132 us
    pallas_call x4, Pallas kernels: 100 us -> 8.58 us  [edges(): pl.pallas_call(kernel, name='edges', in_specs=[anywhere] * size, out_spec...]
    ppermute x56 -> x66, waiting for transfers between devices: 206 us -> 180 us  [partner(): return lax.ppermute(array, axis, [(i, i ^ bits) for i in range(size)])]
    ppermute x56 -> x66, starting transfers between devices: 82.1 us -> 96.9 us  [partner(): return lax.ppermute(array, axis, [(i, i ^ bits) for i in range(size)])]
    pallas_call x4 -> x5, Pallas kernels: 12 us -> 13.2 us  [pack(): pl.pallas_call(kernel, name='pack', grid=(width // LANES,), in_specs=[pl....]
  transfers between devices with their start and end apart: 66 -> 76, of which waited for: 23 -> 28; matrix products, arithmetic and copies ran while one was open for 1% -> 2% of each run, Pallas kernels for 41% -> 29%
where the time goes in v2:
time: 475 us; the launch traced here: 473 us
  waiting for transfers between devices  182 us (38%)
  Pallas kernels  142 us (30%)
  starting transfers between devices  132 us (28%)
  other arithmetic  6.3 us (1%)
  local copies, waits for them, and re-layouts  6.12 us (1%)
    ppermute x66, waiting for transfers between devices, partner(): return lax.ppermute(array, axis, [(i, i ^ bits) for i in range(size)])  180 us
    pallas_call x4, Pallas kernels, window(): pl.pallas_call(kernel, name='window', in_specs=[pl.BlockSpec(memory_space...  109 us
    ppermute x66, starting transfers between devices, partner(): return lax.ppermute(array, axis, [(i, i ^ bits) for i in range(size)])  96.9 us
    ppermute x10, starting transfers between devices, along_hel(): lax.ppermute(array, 'hel', [(i, i + step) for i in range(size) if 0 <= i...  34.9 us
    pallas_call x5, Pallas kernels, pack(): pl.pallas_call(kernel, name='pack', grid=(width // LANES,), in_specs=[pl....  13.2 us
    pallas_call x4, Pallas kernels, unpack(): pl.pallas_call(kernel, name='unpack', grid=(width // LANES,), in_specs=sp...  11.6 us
  transfers between devices with their start and end apart: 76, of which 28 were waited for; matrix products, arithmetic and copies ran while one was open for 2% of the time, Pallas kernels for 29%

profile of v2, /device:TPU:13, one launch (start us, length us, event | category | flops | bytes accessed | tf_op | source)
XLA Modules:
  0.0 473.3 jit_solution(2035719454331474321)
XLA Ops:
  9.2 3.7 fusion.refs_15_
  30.5 4.1 collective-permute-start.8
  37.8 4.0 collective-permute-start.11
  58.9 11.8 %collective-permute-done.11.refs_5_.refs_9_ = f32[16,16,256]{2,1,0:T(8,128)S(1)} collective-permute-done((f32[16,16,256]{2,1,0:T(8,128)}, f32[16,16,256]{2,1,0:T(8,128)S(1)}, u32[]{:S(2)}, u32[]{:S(2)}) %collective-permute-start.11) | collective-permute-done | bytes 262176 | tf_op jit(solution)/shard_map/ppermute | solution.py:18
  70.7 7.9 %collective-permute-done.12.refs_6_.refs_10_ = f32[16,16,256]{2,1,0:T(8,128)S(1)} collective-permute-done((f32[16,16,256]{2,1,0:T(8,128)}, f32[16,16,256]{2,1,0:T(8,128)S(1)}, u32[]{:S(2)}, u32[]{:S(2)}) %collective-permute-start.12) | collective-permute-done | bytes 262176 | tf_op jit(solution)/shard_map/ppermute | solution.py:18
  78.7 5.5 %collective-permute-done.13.refs_7_.refs_11_ = f32[16,16,256]{2,1,0:T(8,128)S(1)} collective-permute-done((f32[16,16,256]{2,1,0:T(8,128)}, f32[16,16,256]{2,1,0:T(8,128)S(1)}, u32[]{:S(2)}, u32[]{:S(2)}) %collective-permute-start.13) | collective-permute-done | bytes 262176 | tf_op jit(solution)/shard_map/ppermute | solution.py:18
  97.9 19.9 %collective-permute-start.15 = (f32[16,16,256]{2,1,0:T(8,128)}, f32[16,16,256]{2,1,0:T(8,128)S(1)}, u32[]{:S(2)}, u32[]{:S(2)}) collective-permute-start(f32[16,16,256]{2,1,0:T(8,128)} %get-tuple-element.122), channel_id=1, source_target_pairs={{0,2},{1,3},{2,0},{3,1},{4,6},{5,7},{6,4},{7,5},{8,10},{9,11},{10,... | collective-permute-start | bytes 786440 | tf_op jit(solution)/shard_map/ppermute | solution.py:18
  119.4 4.4 collective-permute-start.16
  123.8 4.1 collective-permute-done.26.refs_6_.refs_10_
  127.9 11.7 %collective-permute-done.27.refs_7_.refs_11_ = f32[16,16,256]{2,1,0:T(8,128)} collective-permute-done((f32[16,16,256]{2,1,0:T(8,128)}, f32[16,16,256]{2,1,0:T(8,128)}, u32[]{:S(2)}, u32[]{:S(2)}) %collective-permute-start.27) | collective-permute-done | bytes 262176 | tf_op jit(solution)/shard_map/ppermute | solution.py:18
  146.2 12.4 %collective-permute-done.17.refs_4_.refs_8_ = f32[16,16,256]{2,1,0:T(8,128)S(1)} collective-permute-done((f32[16,16,256]{2,1,0:T(8,128)}, f32[16,16,256]{2,1,0:T(8,128)S(1)}, u32[]{:S(2)}, u32[]{:S(2)}) %collective-permute-start.17) | collective-permute-done | bytes 262176 | tf_op jit(solution)/shard_map/ppermute | solution.py:18
  159.3 5.1 %collective-permute-start.2 = (f32[16,16,256]{2,1,0:T(8,128)}, f32[16,16,256]{2,1,0:T(8,128)S(1)}, u32[]{:S(2)}, u32[]{:S(2)}) collective-permute-start(f32[16,16,256]{2,1,0:T(8,128)} %get-tuple-element.107), channel_id=1, source_target_pairs={{0,3},{1,2},{2,1},{3,0},{4,7},{5,6},{6,5},{7,4},{8,11},{9,10},{10,... | collective-permute-start | bytes 786440 | tf_op jit(solution)/shard_map/ppermute | solution.py:18
  164.4 3.6 collective-permute-start.3
  169.4 9.1 %collective-permute-done.19.refs_6_.refs_10_ = f32[16,16,256]{2,1,0:T(8,128)} collective-permute-done((f32[16,16,256]{2,1,0:T(8,128)}, f32[16,16,256]{2,1,0:T(8,128)}, u32[]{:S(2)}, u32[]{:S(2)}) %collective-permute-start.19) | collective-permute-done | bytes 262176 | tf_op jit(solution)/shard_map/ppermute | solution.py:18
  178.5 11.7 %collective-permute-done.20.refs_7_.refs_11_ = f32[16,16,256]{2,1,0:T(8,128)} collective-permute-done((f32[16,16,256]{2,1,0:T(8,128)}, f32[16,16,256]{2,1,0:T(8,128)}, u32[]{:S(2)}, u32[]{:S(2)}) %collective-permute-start.20) | collective-permute-done | bytes 262176 | tf_op jit(solution)/shard_map/ppermute | solution.py:18
  190.1 10.7 %collective-permute-start.39 = (f32[8,3,16,256]{3,2,1,0:T(8,128)}, f32[8,3,16,256]{3,2,1,0:T(8,128)}, u32[]{:S(2)}, u32[]{:S(2)}) collective-permute-start(f32[8,3,16,256]{3,2,1,0:T(8,128)} %get-tuple-element.147), channel_id=1, source_target_pairs={{8,0},{16,8},{24,16},{9,1},{17,9},{25,17},{10,2},{18,10},{26,18},{... | collective-permute-start | bytes 1179656 | tf_op jit(solution)/shard_map/ppermute | solution.py:254
  207.6 4.3 collective-permute-start.43
  214.1 27.2 %window.4 = (f32[16,16,256]{2,1,0:T(8,128)}, f32[16,16,256]{2,1,0:T(8,128)}, f32[16,16,256]{2,1,0:T(8,128)}, f32[16,16,256]{2,1,0:T(8,128)}, f32[16,16,256]{2,1,...) custom-call(s32[8]{0:T(128)} %iota_xor_fusion.place_ref.refs_0_, ...), custom_call_target="tpu_custom_call" | custom-call | tf_op jit(solution)/shard_map/window/pallas_call | solution.py:199
  247.6 11.5 %collective-permute-done.70.refs_2_ = f32[16,16,256]{2,1,0:T(8,128)S(1)} collective-permute-done((f32[16,16,256]{2,1,0:T(8,128)}, f32[16,16,256]{2,1,0:T(8,128)S(1)}, u32[]{:S(2)}, u32[]{:S(2)}) %collective-permute-start.70) | collective-permute-done | bytes 262176 | tf_op jit(solution)/shard_map/ppermute | solution.py:18
  267.5 27.3 %window.5 = (f32[16,16,256]{2,1,0:T(8,128)}, f32[16,16,256]{2,1,0:T(8,128)}, f32[16,16,256]{2,1,0:T(8,128)}, f32[16,16,256]{2,1,0:T(8,128)}, f32[16,16,256]{2,1,...) custom-call(s32[8]{0:T(128)} %iota_xor_fusion.place_ref.refs_0_, ...), custom_call_target="tpu_custom_call" | custom-call | tf_op jit(solution)/shard_map/window/pallas_call | solution.py:199
  294.9 4.3 collective-permute-start.54
  311.2 3.7 collective-permute-done.64.refs_3_
  318.0 27.2 %window.7 = (f32[16,16,256]{2,1,0:T(8,128)}, f32[16,16,256]{2,1,0:T(8,128)}, f32[16,16,256]{2,1,0:T(8,128)}, f32[16,16,256]{2,1,0:T(8,128)}, f32[16,16,256]{2,1,...) custom-call(s32[8]{0:T(128)} %iota_xor_fusion.place_ref.refs_0_, ...), custom_call_target="tpu_custom_call" | custom-call | tf_op jit(solution)/shard_map/window/pallas_call | solution.py:199
  346.7 11.4 %collective-permute-done.67.refs_6_ = f32[16,16,256]{2,1,0:T(8,128)S(1)} collective-permute-done((f32[16,16,256]{2,1,0:T(8,128)}, f32[16,16,256]{2,1,0:T(8,128)S(1)}, u32[]{:S(2)}, u32[]{:S(2)}) %collective-permute-start.67) | collective-permute-done | bytes 262176 | tf_op jit(solution)/shard_map/ppermute | solution.py:18
  360.9 27.2 %window.6 = (f32[16,16,256]{2,1,0:T(8,128)}, f32[16,16,256]{2,1,0:T(8,128)}, f32[16,16,256]{2,1,0:T(8,128)}, f32[16,16,256]{2,1,0:T(8,128)}, f32[16,16,256]{2,1,...) custom-call(s32[8]{0:T(128)} %iota_xor_fusion.place_ref.refs_0_, ...), custom_call_target="tpu_custom_call" | custom-call | tf_op jit(solution)/shard_map/window/pallas_call | solution.py:199
  393.9 19.1 %collective-permute-done.59.refs_5_ = f32[16,16,256]{2,1,0:T(8,128)S(1)} collective-permute-done((f32[16,16,256]{2,1,0:T(8,128)}, f32[16,16,256]{2,1,0:T(8,128)S(1)}, u32[]{:S(2)}, u32[]{:S(2)}) %collective-permute-start.59) | collective-permute-done | bytes 262176 | tf_op jit(solution)/shard_map/ppermute | solution.py:18
  415.6 4.2 collective-permute-done.60.refs_6_
  419.8 11.2 %collective-permute-done.61.refs_7_ = f32[16,16,256]{2,1,0:T(8,128)S(1)} collective-permute-done((f32[16,16,256]{2,1,0:T(8,128)}, f32[16,16,256]{2,1,0:T(8,128)S(1)}, u32[]{:S(2)}, u32[]{:S(2)}) %collective-permute-start.61) | collective-permute-done | bytes 262176 | tf_op jit(solution)/shard_map/ppermute | solution.py:18
  442.0 10.3 %collective-permute-done.49.refs_4_ = f32[16,16,256]{2,1,0:T(8,128)} collective-permute-done((f32[16,16,256]{2,1,0:T(8,128)}, f32[16,16,256]{2,1,0:T(8,128)}, u32[]{:S(2)}, u32[]{:S(2)}) %collective-permute-start.49) | collective-permute-done | bytes 262176 | tf_op jit(solution)/shard_map/ppermute | solution.py:18
  452.3 5.6 %collective-permute-done.50.refs_5_ = f32[16,16,256]{2,1,0:T(8,128)} collective-permute-done((f32[16,16,256]{2,1,0:T(8,128)}, f32[16,16,256]{2,1,0:T(8,128)}, u32[]{:S(2)}, u32[]{:S(2)}) %collective-permute-start.50) | collective-permute-done | bytes 262176 | tf_op jit(solution)/shard_map/ppermute | solution.py:18
  457.9 6.8 %collective-permute-done.51.refs_6_ = f32[16,16,256]{2,1,0:T(8,128)} collective-permute-done((f32[16,16,256]{2,1,0:T(8,128)}, f32[16,16,256]{2,1,0:T(8,128)}, u32[]{:S(2)}, u32[]{:S(2)}) %collective-permute-start.51) | collective-permute-done | bytes 262176 | tf_op jit(solution)/shard_map/ppermute | solution.py:18
  464.7 5.6 %collective-permute-done.52.refs_7_ = f32[16,16,256]{2,1,0:T(8,128)} collective-permute-done((f32[16,16,256]{2,1,0:T(8,128)}, f32[16,16,256]{2,1,0:T(8,128)}, u32[]{:S(2)}, u32[]{:S(2)}) %collective-permute-start.52) | collective-permute-done | bytes 262176 | tf_op jit(solution)/shard_map/ppermute | solution.py:18
  (261 shorter events, 136.0 us)
Async XLA Ops:
  41.7 36.9 %collective-permute-start.12 = (f32[16,16,256]{2,1,0:T(8,128)}, f32[16,16,256]{2,1,0:T(8,128)S(1)}, u32[]{:S(2)}, u32[]{:S(2)}) collective-permute-start(f32[16,16,256]{2,1,0:T(8,128)} %get-tuple-element.118), channel_id=1, source_target_pairs={{0,6},{1,7},{2,4},{3,5},{4,2},{5,3},{6,0},{7,1},{8,14},{9,15},{10,... | collective-permute-start | bytes 786440 | tf_op jit(solution)/shard_map/ppermute | solution.py:18
  47.6 36.5 %collective-permute-start.13 = (f32[16,16,256]{2,1,0:T(8,128)}, f32[16,16,256]{2,1,0:T(8,128)S(1)}, u32[]{:S(2)}, u32[]{:S(2)}) collective-permute-start(f32[16,16,256]{2,1,0:T(8,128)} %get-tuple-element.119), channel_id=1, source_target_pairs={{0,7},{1,6},{2,5},{3,4},{4,3},{5,2},{6,1},{7,0},{8,15},{9,14},{10,... | collective-permute-start | bytes 786440 | tf_op jit(solution)/shard_map/ppermute | solution.py:18
  85.3 34.1 %collective-permute-start.25 = (f32[16,16,256]{2,1,0:T(8,128)}, f32[16,16,256]{2,1,0:T(8,128)}, u32[]{:S(2)}, u32[]{:S(2)}) collective-permute-start(f32[16,16,256]{2,1,0:T(8,128)} %get-tuple-element.135), channel_id=1, source_target_pairs={{0,5},{1,4},{2,7},{3,6},{4,1},{5,0},{6,3},{7,2},{8,13},{9,12},{10,... | collective-permute-start | bytes 786440 | tf_op jit(solution)/shard_map/ppermute | solution.py:18
  87.4 40.5 %collective-permute-start.26 = (f32[16,16,256]{2,1,0:T(8,128)}, f32[16,16,256]{2,1,0:T(8,128)}, u32[]{:S(2)}, u32[]{:S(2)}) collective-permute-start(f32[16,16,256]{2,1,0:T(8,128)} %get-tuple-element.136), channel_id=1, source_target_pairs={{0,6},{1,7},{2,4},{3,5},{4,2},{5,3},{6,0},{7,1},{8,14},{9,15},{10,... | collective-permute-start | bytes 786440 | tf_op jit(solution)/shard_map/ppermute | solution.py:18
  87.4 52.2 %collective-permute-start.27 = (f32[16,16,256]{2,1,0:T(8,128)}, f32[16,16,256]{2,1,0:T(8,128)}, u32[]{:S(2)}, u32[]{:S(2)}) collective-permute-start(f32[16,16,256]{2,1,0:T(8,128)} %get-tuple-element.137), channel_id=1, source_target_pairs={{0,7},{1,6},{2,5},{3,4},{4,3},{5,2},{6,1},{7,0},{8,15},{9,14},{10,... | collective-permute-start | bytes 786440 | tf_op jit(solution)/shard_map/ppermute | solution.py:18
  93.7 45.9 %collective-permute-start.14 = (f32[16,16,256]{2,1,0:T(8,128)}, f32[16,16,256]{2,1,0:T(8,128)S(1)}, u32[]{:S(2)}, u32[]{:S(2)}) collective-permute-start(f32[16,16,256]{2,1,0:T(8,128)} %get-tuple-element.121), channel_id=1, source_target_pairs={{0,1},{1,0},{2,3},{3,2},{4,5},{5,4},{6,7},{7,6},{8,9},{9,8},{10,11... | collective-permute-start | bytes 786440 | tf_op jit(solution)/shard_map/ppermute | solution.py:18
  97.9 41.7 %collective-permute-start.15 = (f32[16,16,256]{2,1,0:T(8,128)}, f32[16,16,256]{2,1,0:T(8,128)S(1)}, u32[]{:S(2)}, u32[]{:S(2)}) collective-permute-start(f32[16,16,256]{2,1,0:T(8,128)} %get-tuple-element.122), channel_id=1, source_target_pairs={{0,2},{1,3},{2,0},{3,1},{4,6},{5,7},{6,4},{7,5},{8,10},{9,11},{10,... | collective-permute-start | bytes 786440 | tf_op jit(solution)/shard_map/ppermute | solution.py:18
  139.6 38.9 %collective-permute-start.19 = (f32[16,16,256]{2,1,0:T(8,128)}, f32[16,16,256]{2,1,0:T(8,128)}, u32[]{:S(2)}, u32[]{:S(2)}) collective-permute-start(f32[16,16,256]{2,1,0:T(8,128)} %get-tuple-element.126), channel_id=1, source_target_pairs={{0,6},{1,7},{2,4},{3,5},{4,2},{5,3},{6,0},{7,1},{8,14},{9,15},{10,... | collective-permute-start | bytes 786440 | tf_op jit(solution)/shard_map/ppermute | solution.py:18
  139.7 50.4 %collective-permute-start.20 = (f32[16,16,256]{2,1,0:T(8,128)}, f32[16,16,256]{2,1,0:T(8,128)}, u32[]{:S(2)}, u32[]{:S(2)}) collective-permute-start(f32[16,16,256]{2,1,0:T(8,128)} %get-tuple-element.127), channel_id=1, source_target_pairs={{0,7},{1,6},{2,5},{3,4},{4,3},{5,2},{6,1},{7,0},{8,15},{9,14},{10,... | collective-permute-start | bytes 786440 | tf_op jit(solution)/shard_map/ppermute | solution.py:18
  143.4 64.2 %collective-permute-start.38 = (f32[8,3,16,256]{3,2,1,0:T(8,128)}, f32[8,3,16,256]{3,2,1,0:T(8,128)}, u32[]{:S(2)}, u32[]{:S(2)}) collective-permute-start(f32[8,3,16,256]{3,2,1,0:T(8,128)} %get-tuple-element.146), channel_id=1, source_target_pairs={{0,8},{8,16},{16,24},{1,9},{9,17},{17,25},{2,10},{10,18},{18,26},{... | collective-permute-start | bytes 1179656 | tf_op jit(solution)/shard_map/ppermute | solution.py:254
  159.3 46.2 %collective-permute-start.2 = (f32[16,16,256]{2,1,0:T(8,128)}, f32[16,16,256]{2,1,0:T(8,128)S(1)}, u32[]{:S(2)}, u32[]{:S(2)}) collective-permute-start(f32[16,16,256]{2,1,0:T(8,128)} %get-tuple-element.107), channel_id=1, source_target_pairs={{0,3},{1,2},{2,1},{3,0},{4,7},{5,6},{6,5},{7,4},{8,11},{9,10},{10,... | collective-permute-start | bytes 786440 | tf_op jit(solution)/shard_map/ppermute | solution.py:18
  164.4 41.2 %collective-permute-start.3 = (f32[16,16,256]{2,1,0:T(8,128)}, f32[16,16,256]{2,1,0:T(8,128)S(1)}, u32[]{:S(2)}, u32[]{:S(2)}) collective-permute-start(f32[16,16,256]{2,1,0:T(8,128)} %get-tuple-element.108), channel_id=1, source_target_pairs={{0,4},{1,5},{2,6},{3,7},{4,0},{5,1},{6,2},{7,3},{8,12},{9,13},{10,... | collective-permute-start | bytes 786440 | tf_op jit(solution)/shard_map/ppermute | solution.py:18
  178.5 62.9 %collective-permute-start.4 = (f32[16,16,256]{2,1,0:T(8,128)}, f32[16,16,256]{2,1,0:T(8,128)S(1)}, u32[]{:S(2)}, u32[]{:S(2)}) collective-permute-start(f32[16,16,256]{2,1,0:T(8,128)} %get-tuple-element.109), channel_id=1, source_target_pairs={{0,5},{1,4},{2,7},{3,6},{4,1},{5,0},{6,3},{7,2},{8,13},{9,12},{10,... | collective-permute-start | bytes 786440 | tf_op jit(solution)/shard_map/ppermute | solution.py:18
  205.6 37.4 %collective-permute-start.5 = (f32[16,16,256]{2,1,0:T(8,128)}, f32[16,16,256]{2,1,0:T(8,128)S(1)}, u32[]{:S(2)}, u32[]{:S(2)}) collective-permute-start(f32[16,16,256]{2,1,0:T(8,128)} %get-tuple-element.110), channel_id=1, source_target_pairs={{0,6},{1,7},{2,4},{3,5},{4,2},{5,3},{6,0},{7,1},{8,14},{9,15},{10,... | collective-permute-start | bytes 786440 | tf_op jit(solution)/shard_map/ppermute | solution.py:18
  205.7 39.0 %collective-permute-start.42 = (f32[8,3,16,256]{3,2,1,0:T(8,128)}, f32[8,3,16,256]{3,2,1,0:T(8,128)S(1)}, u32[]{:S(2)}, u32[]{:S(2)}) collective-permute-start(f32[8,3,16,256]{3,2,1,0:T(8,128)} %get-tuple-element.159), channel_id=1, source_target_pairs={{0,8},{8,16},{16,24},{1,9},{9,17},{17,25},{2,10},{10,18},{18,26},{... | collective-permute-start | bytes 1179656 | tf_op jit(solution)/shard_map/ppermute | solution.py:254
  207.6 37.2 %collective-permute-start.43 = (f32[8,3,16,256]{3,2,1,0:T(8,128)}, f32[8,3,16,256]{3,2,1,0:T(8,128)}, u32[]{:S(2)}, u32[]{:S(2)}) collective-permute-start(f32[8,3,16,256]{3,2,1,0:T(8,128)} %get-tuple-element.128), channel_id=1, source_target_pairs={{8,0},{16,8},{24,16},{9,1},{17,9},{25,17},{10,2},{18,10},{26,18},{... | collective-permute-start | bytes 1179656 | tf_op jit(solution)/shard_map/ppermute | solution.py:254
  244.7 50.1 %collective-permute-start.72 = (f32[16,16,256]{2,1,0:T(8,128)}, f32[16,16,256]{2,1,0:T(8,128)S(1)}, u32[]{:S(2)}, u32[]{:S(2)}) collective-permute-start(f32[16,16,256]{2,1,0:T(8,128)} %get-tuple-element.199), channel_id=1, source_target_pairs={{0,4},{1,5},{2,6},{3,7},{4,0},{5,1},{6,2},{7,3},{8,12},{9,13},{10,... | collective-permute-start | bytes 786440 | tf_op jit(solution)/shard_map/ppermute | solution.py:18
  244.8 54.4 %collective-permute-start.73 = (f32[16,16,256]{2,1,0:T(8,128)}, f32[16,16,256]{2,1,0:T(8,128)S(1)}, u32[]{:S(2)}, u32[]{:S(2)}) collective-permute-start(f32[16,16,256]{2,1,0:T(8,128)} %get-tuple-element.200), channel_id=1, source_target_pairs={{0,5},{1,4},{2,7},{3,6},{4,1},{5,0},{6,3},{7,2},{8,13},{9,12},{10,... | collective-permute-start | bytes 786440 | tf_op jit(solution)/shard_map/ppermute | solution.py:18
  247.4 53.1 %collective-permute-start.74 = (f32[16,16,256]{2,1,0:T(8,128)}, f32[16,16,256]{2,1,0:T(8,128)}, u32[]{:S(2)}, u32[]{:S(2)}) collective-permute-start(f32[16,16,256]{2,1,0:T(8,128)} %get-tuple-element.201), channel_id=1, source_target_pairs={{0,6},{1,7},{2,4},{3,5},{4,2},{5,3},{6,0},{7,1},{8,14},{9,15},{10,... | collective-permute-start | bytes 786440 | tf_op jit(solution)/shard_map/ppermute | solution.py:18
  259.1 43.2 %collective-permute-start.75 = (f32[16,16,256]{2,1,0:T(8,128)}, f32[16,16,256]{2,1,0:T(8,128)}, u32[]{:S(2)}, u32[]{:S(2)}) collective-permute-start(f32[16,16,256]{2,1,0:T(8,128)} %get-tuple-element.202), channel_id=1, source_target_pairs={{0,7},{1,6},{2,5},{3,4},{4,3},{5,2},{6,1},{7,0},{8,15},{9,14},{10,... | collective-permute-start | bytes 786440 | tf_op jit(solution)/shard_map/ppermute | solution.py:18
  265.4 51.2 %collective-permute-start.53 = (f32[8,3,16,256]{3,2,1,0:T(8,128)}, f32[8,3,16,256]{3,2,1,0:T(8,128)S(1)}, u32[]{:S(2)}, u32[]{:S(2)}) collective-permute-start(f32[8,3,16,256]{3,2,1,0:T(8,128)} %get-tuple-element.180), channel_id=1, source_target_pairs={{0,8},{8,16},{16,24},{1,9},{9,17},{17,25},{2,10},{10,18},{18,26},{... | collective-permute-start | bytes 1179656 | tf_op jit(solution)/shard_map/ppermute | solution.py:254
  305.0 53.1 %collective-permute-start.44 = (f32[8,3,16,256]{3,2,1,0:T(8,128)}, f32[8,3,16,256]{3,2,1,0:T(8,128)S(1)}, u32[]{:S(2)}, u32[]{:S(2)}) collective-permute-start(f32[8,3,16,256]{3,2,1,0:T(8,128)} %get-tuple-element.169), channel_id=1, source_target_pairs={{0,8},{8,16},{16,24},{1,9},{9,17},{17,25},{2,10},{10,18},{18,26},{... | collective-permute-start | bytes 1179656 | tf_op jit(solution)/shard_map/ppermute | solution.py:254
  308.5 51.6 %collective-permute-start.45 = (f32[8,3,16,256]{3,2,1,0:T(8,128)}, f32[8,3,16,256]{3,2,1,0:T(8,128)S(1)}, u32[]{:S(2)}, u32[]{:S(2)}) collective-permute-start(f32[8,3,16,256]{3,2,1,0:T(8,128)} %get-tuple-element.170), channel_id=1, source_target_pairs={{8,0},{16,8},{24,16},{9,1},{17,9},{25,17},{10,2},{18,10},{26,18},{... | collective-permute-start | bytes 1179656 | tf_op jit(solution)/shard_map/ppermute | solution.py:254
  317.3 40.8 %collective-permute-start.67 = (f32[16,16,256]{2,1,0:T(8,128)}, f32[16,16,256]{2,1,0:T(8,128)S(1)}, u32[]{:S(2)}, u32[]{:S(2)}) collective-permute-start(f32[16,16,256]{2,1,0:T(8,128)} %get-tuple-element.194), channel_id=1, source_target_pairs={{0,6},{1,7},{2,4},{3,5},{4,2},{5,3},{6,0},{7,1},{8,14},{9,15},{10,... | collective-permute-start | bytes 786440 | tf_op jit(solution)/shard_map/ppermute | solution.py:18
  345.3 42.8 %collective-permute-start.68 = (f32[16,16,256]{2,1,0:T(8,128)}, f32[16,16,256]{2,1,0:T(8,128)S(1)}, u32[]{:S(2)}, u32[]{:S(2)}) collective-permute-start(f32[16,16,256]{2,1,0:T(8,128)} %get-tuple-element.195), channel_id=1, source_target_pairs={{0,7},{1,6},{2,5},{3,4},{4,3},{5,2},{6,1},{7,0},{8,15},{9,14},{10,... | collective-permute-start | bytes 786440 | tf_op jit(solution)/shard_map/ppermute | solution.py:18
  346.7 43.1 %collective-permute-start.55 = (f32[16,16,256]{2,1,0:T(8,128)}, f32[16,16,256]{2,1,0:T(8,128)S(1)}, u32[]{:S(2)}, u32[]{:S(2)}) collective-permute-start(f32[16,16,256]{2,1,0:T(8,128)} %get-tuple-element.182), channel_id=1, source_target_pairs={{0,1},{1,0},{2,3},{3,2},{4,5},{5,4},{6,7},{7,6},{8,9},{9,8},{10,11... | collective-permute-start | bytes 786440 | tf_op jit(solution)/shard_map/ppermute | solution.py:18
  358.1 33.7 %collective-permute-start.57 = (f32[16,16,256]{2,1,0:T(8,128)}, f32[16,16,256]{2,1,0:T(8,128)}, u32[]{:S(2)}, u32[]{:S(2)}) collective-permute-start(f32[16,16,256]{2,1,0:T(8,128)} %get-tuple-element.184), channel_id=1, source_target_pairs={{0,3},{1,2},{2,1},{3,0},{4,7},{5,6},{6,5},{7,4},{8,11},{9,10},{10,... | collective-permute-start | bytes 786440 | tf_op jit(solution)/shard_map/ppermute | solution.py:18
  390.3 40.7 %collective-permute-start.61 = (f32[16,16,256]{2,1,0:T(8,128)}, f32[16,16,256]{2,1,0:T(8,128)S(1)}, u32[]{:S(2)}, u32[]{:S(2)}) collective-permute-start(f32[16,16,256]{2,1,0:T(8,128)} %get-tuple-element.188), channel_id=1, source_target_pairs={{0,7},{1,6},{2,5},{3,4},{4,3},{5,2},{6,1},{7,0},{8,15},{9,14},{10,... | collective-permute-start | bytes 786440 | tf_op jit(solution)/shard_map/ppermute | solution.py:18
  391.9 39.1 %collective-permute-start.46 = (f32[16,16,256]{2,1,0:T(8,128)}, f32[16,16,256]{2,1,0:T(8,128)S(1)}, u32[]{:S(2)}, u32[]{:S(2)}) collective-permute-start(f32[16,16,256]{2,1,0:T(8,128)} %get-tuple-element.172), channel_id=1, source_target_pairs={{0,1},{1,0},{2,3},{3,2},{4,5},{5,4},{6,7},{7,6},{8,9},{9,8},{10,11... | collective-permute-start | bytes 786440 | tf_op jit(solution)/shard_map/ppermute | solution.py:18
  391.9 40.2 %collective-permute-start.47 = (f32[16,16,256]{2,1,0:T(8,128)}, f32[16,16,256]{2,1,0:T(8,128)S(1)}, u32[]{:S(2)}, u32[]{:S(2)}) collective-permute-start(f32[16,16,256]{2,1,0:T(8,128)} %get-tuple-element.173), channel_id=1, source_target_pairs={{0,2},{1,3},{2,0},{3,1},{4,6},{5,7},{6,4},{7,5},{8,10},{9,11},{10,... | collective-permute-start | bytes 786440 | tf_op jit(solution)/shard_map/ppermute | solution.py:18
  431.0 33.7 %collective-permute-start.51 = (f32[16,16,256]{2,1,0:T(8,128)}, f32[16,16,256]{2,1,0:T(8,128)}, u32[]{:S(2)}, u32[]{:S(2)}) collective-permute-start(f32[16,16,256]{2,1,0:T(8,128)} %get-tuple-element.177), channel_id=1, source_target_pairs={{0,6},{1,7},{2,4},{3,5},{4,2},{5,3},{6,0},{7,1},{8,14},{9,15},{10,... | collective-permute-start | bytes 786440 | tf_op jit(solution)/shard_map/ppermute | solution.py:18
  432.1 38.3 %collective-permute-start.52 = (f32[16,16,256]{2,1,0:T(8,128)}, f32[16,16,256]{2,1,0:T(8,128)}, u32[]{:S(2)}, u32[]{:S(2)}) collective-permute-start(f32[16,16,256]{2,1,0:T(8,128)} %get-tuple-element.178), channel_id=1, source_target_pairs={{0,7},{1,6},{2,5},{3,4},{4,3},{5,2},{6,1},{7,0},{8,15},{9,14},{10,... | collective-permute-start | bytes 786440 | tf_op jit(solution)/shard_map/ppermute | solution.py:18
  (96 other events, 3566.4 us)

commit v3 on v2

v3 whole, which is shorter than its diff:
```python
import math

import jax
import jax.numpy as jnp
from jax import lax
from jax.experimental import pallas as pl
from jax.experimental.pallas import tpu as pltpu
from jax.sharding import PartitionSpec as P


OUTER = 3
GROUP = 6
LANES = 128


def swap(arrays, axis, ranks):
    size = lax.axis_size(axis)
    swapped = {}
    for d in ranks:
        swapped[d] = lax.ppermute(arrays[d], axis, [(i, i ^ d) for i in range(size)])
    return [swapped.get(d, arrays[d]) for d in range(size)]


def place(d):
    return jnp.bitwise_xor(lax.axis_index("ang"), d)


def pack(wave, chunk, span, potential=None):
    _, angles, cells, width = wave.shape
    start, stop = span
    block = math.gcd(start, stop) if potential is None else stop - start
    size = lax.axis_size("ang")
    extra = 0 if potential is None else len(slabs_of(cells // size))

    def kernel(*refs):
        wave_ref, outs = refs[0], refs[-size:]
        slabs = slabs_of(cells // size) if extra else []
        for d in range(size):
            first = place(d)
            for k in range(block):
                rows = wave_ref.at[k].reshape(angles * size, LANES)
                outs[d][k] = rows[pl.ds(first, angles, stride=size), :]
            for s, slab in enumerate(slabs):
                rows = refs[1].reshape(angles * cells, LANES)
                outs[d][block + s] = rows[pl.ds(slab * size + first, angles, stride=cells), :]

    args = [wave]
    specs = [pl.BlockSpec((block, angles, size, LANES), lambda k, g: (start // block + k, 0, chunk, g))]
    if extra:
        args.append(potential)
        specs.append(pl.BlockSpec((angles, cells, LANES), lambda k, g: (0, 0, g)))
    packed = (stop - start + extra, angles, width)
    return pl.pallas_call(
        kernel,
        name="pack",
        grid=((stop - start) // block, width // LANES),
        in_specs=specs,
        out_specs=[pl.BlockSpec((block + extra, angles, LANES), lambda k, g: (k, 0, g))] * size,
        out_shape=[jax.ShapeDtypeStruct(packed, jnp.float32)] * size,
    )(*args)


def unpack(pieces, whole, shape, chunk, span):
    _, angles, _, width = shape
    start, stop = span
    block = math.gcd(start, stop)
    size = len(pieces)

    def kernel(*refs):
        ins, out = refs[:size], refs[-1]
        for d in range(size):
            first = place(d)
            for k in range(block):
                rows = out.at[k].reshape(angles * size, LANES)
                rows[pl.ds(first, angles, stride=size), :] = ins[d][k]

    args = [*pieces]
    specs = [pl.BlockSpec((block, angles, LANES), lambda k, g: (k, 0, g))] * size
    aliases = {}
    if whole is not None:
        aliases = {len(args): 0}
        args.append(whole)
        specs.append(pl.BlockSpec(memory_space=pl.ANY))
    return pl.pallas_call(
        kernel,
        name="unpack",
        grid=((stop - start) // block, width // LANES),
        in_specs=specs,
        out_specs=pl.BlockSpec(
            (block, angles, size, LANES), lambda k, g: (start // block + k, 0, chunk, g)
        ),
        out_shape=jax.ShapeDtypeStruct(shape, jnp.float32),
        input_output_aliases=aliases,
    )(*args)


def slabs_of(chunks):
    return [lax.axis_index("hel")] if chunks == lax.axis_size("hel") else list(range(chunks))


def gather(arrays, start, stop):
    size = len(arrays)
    shape = (size, stop - start, *arrays[0].shape[1:])

    def kernel(*refs):
        ins, out, sems = refs[:size], refs[size], refs[size + 1]
        copies = [
            pltpu.make_async_copy(ins[d].at[pl.ds(start, stop - start)], out.at[d], sems.at[d])
            for d in range(size)
        ]
        for copy in copies:
            copy.start()
        for copy in copies:
            copy.wait()

    return pl.pallas_call(
        kernel,
        name="gather",
        in_specs=[pl.BlockSpec(memory_space=pl.ANY)] * size,
        out_specs=pl.BlockSpec(memory_space=pltpu.VMEM),
        out_shape=jax.ShapeDtypeStruct(shape, jnp.float32),
        scratch_shapes=[pltpu.SemaphoreType.DMA((size,))],
    )(*arrays)


def spread_potential(mine, chunks):
    groups = lax.axis_size("hel")
    if chunks != groups:
        return [mine[:, c] for c in range(chunks)]
    known = jnp.stack(swap([mine[:, 0]] * groups, "hel", range(1, groups)))
    group = lax.axis_index("hel")
    return [lax.dynamic_index_in_dim(known, jnp.bitwise_xor(group, c), keepdims=False) for c in range(chunks)]


def overlaps(spans, start, stop):
    for s, (low, high) in enumerate(spans):
        first, last = max(low, start), min(high, stop)
        if first < last:
            yield s, first - low, first - start, last - first


def edges(segments, spans):
    size = len(segments[0])
    _, angles, width = segments[0][0].shape
    count = spans[-1][1]
    jobs = [
        (side, *part)
        for side, start in enumerate((0, count - OUTER))
        for part in overlaps(spans, start, start + OUTER)
    ]

    def kernel(*refs):
        ins, targets, sems = refs[: size * len(spans)], refs[-3:-1], refs[-1]
        copies = []
        for d in range(size):
            for side, s, source, target, amount in jobs:
                copies.append(
                    pltpu.make_async_copy(
                        ins[s * size + d].at[pl.ds(source, amount)],
                        targets[side].at[d, pl.ds(target, amount)],
                        sems.at[len(copies)],
                    )
                )
                copies[-1].start()
        for copy in copies:
            copy.wait()

    shape = jax.ShapeDtypeStruct((size, OUTER, angles, width), jnp.float32)
    return pl.pallas_call(
        kernel,
        name="edges",
        in_specs=[pl.BlockSpec(memory_space=pl.ANY)] * (size * len(spans)),
        out_specs=[pl.BlockSpec(memory_space=pltpu.VMEM)] * 2,
        out_shape=[shape] * 2,
        scratch_shapes=[pltpu.SemaphoreType.DMA((len(jobs) * size,))],
    )(*[piece for segment in segments for piece in segment])


def halves(values):
    high = values.astype(jnp.bfloat16)
    return high, (values - high.astype(jnp.float32)).astype(jnp.bfloat16)


def window(segments, spans, result_spans, potential, below, above, mats, mats_below, mats_above, kinetic, radial, weights):
    size = len(segments[0])
    _, angles, width = segments[0][0].shape
    count = spans[-1][1]
    full = size * angles
    total = count + 2 * OUTER
    n_in, n_out = size * len(spans), size * len(result_spans)

    def kernel(*refs):
        weight_ref, kin_ref, rad_ref = refs[:3]
        ins = refs[3 : 3 + n_in]
        pot_ref, below_ref, above_ref, mat_ref, mat_below_ref, mat_above_ref = refs[3 + n_in : 9 + n_in]
        outs = refs[9 + n_in : 9 + n_in + n_out]
        one, two, mat, pot, kin, sems = refs[9 + n_in + n_out :]
        copies = []

        def fetch(source, target):
            copy = pltpu.make_async_copy(source, target, sems.at[len(copies)])
            copy.start()
            copies.append(copy)

        def spot(d):
            return pl.ds(pl.multiple_of(place(d) * angles, angles), angles)

        for d in range(size):
            for s, (start, stop) in enumerate(spans):
                fetch(ins[s * size + d].at[pl.ds(0, stop - start)], one.at[pl.ds(OUTER + start, stop - start), spot(d), :])
            fetch(pot_ref.at[d], pot.at[spot(d), :])
            fetch(below_ref.at[d], one.at[pl.ds(0, OUTER), spot(d), :])
            fetch(above_ref.at[d], one.at[pl.ds(OUTER + count, OUTER), spot(d), :])
        fetch(mat_below_ref, mat.at[pl.ds(0, OUTER)])
        fetch(mat_ref, mat.at[pl.ds(OUTER, count)])
        fetch(mat_above_ref, mat.at[pl.ds(OUTER + count, OUTER)])
        kin_high, kin_low = halves(kin_ref[...])
        kin[0], kin[1] = kin_high, kin_low
        for copy in copies:
            copy.wait()

        def dot(a, b):
            return jnp.dot(a, b, preferred_element_type=jnp.float32)

        def times_kinetic(field):
            high, low = halves(field)
            return dot(high, kin[0]) + dot(low, kin[0]) + dot(high, kin[1])

        def step(source, target, turn):
            first = turn + 1
            amount = total - 2 * first

            def rows(m, group):
                fields = []
                for p in range(group):
                    at = m + p - turn
                    fields.append(
                        source[at] + weight_ref[m + p + 1] * source[at + 1] + weight_ref[m + p] * source[at - 1]
                    )
                field = jnp.concatenate(fields, axis=0)
                spread = jnp.concatenate([pot[...]] * group, axis=0)
                once = times_kinetic(field) + spread * field
                mixed = 0.3 * field - 0.2 * once
                passed = 0.7 * field + times_kinetic(mixed) + spread * mixed
                for p in range(group):
                    part = passed[p * full : (p + 1) * full]
                    high, low = halves(part)
                    rows = [jnp.concatenate([piece, piece], axis=1) for piece in halves(mat[m + p])]
                    both = dot(jnp.concatenate(rows, axis=0), jnp.concatenate([high, low], axis=0))
                    target[m + p - first] = part + rad_ref[...] * (both[:full] + both[full:])

            def body(index, carry):
                rows(first + index * GROUP, GROUP)
                return carry

            lax.fori_loop(0, amount // GROUP, body, 0)
            if amount % GROUP:
                rows(first + amount // GROUP * GROUP, amount % GROUP)

        buffers = [one, two]
        for turn in range(OUTER):
            step(buffers[turn % 2], buffers[(turn + 1) % 2], turn)
        result = buffers[OUTER % 2]
        stores = []
        for d in range(size):
            for s, (start, stop) in enumerate(result_spans):
                copy = pltpu.make_async_copy(
                    result.at[pl.ds(start, stop - start), spot(d), :], outs[s * size + d], sems.at[len(stores)]
                )
                copy.start()
                stores.append(copy)
        for copy in stores:
            copy.wait()

    anywhere = pl.BlockSpec(memory_space=pl.ANY)
    results = pl.pallas_call(
        kernel,
        name="window",
        in_specs=[
            pl.BlockSpec(memory_space=pltpu.SMEM),
            pl.BlockSpec(memory_space=pltpu.VMEM),
            pl.BlockSpec(memory_space=pltpu.VMEM),
        ]
        + [anywhere] * (n_in + 6),
        out_specs=[anywhere] * n_out,
        out_shape=[
            jax.ShapeDtypeStruct((stop - start, angles, width), jnp.float32)
            for start, stop in result_spans
            for _ in range(size)
        ],
        scratch_shapes=[
            pltpu.VMEM((total, full, width), jnp.float32),
            pltpu.VMEM((total, full, width), jnp.float32),
            pltpu.VMEM((total, full, full), jnp.float32),
            pltpu.VMEM((full, width), jnp.float32),
            pltpu.VMEM((2, width, width), jnp.bfloat16),
            pltpu.SemaphoreType.DMA((max(n_in, n_out) + 3 * size + 3,)),
        ],
    )(
        weights,
        kinetic,
        radial,
        *[piece for segment in segments for piece in segment],
        potential,
        below,
        above,
        mats,
        mats_below,
        mats_above,
    )
    return [results[s * size : (s + 1) * size] for s in range(len(result_spans))]


def along_hel(array, step):
    size = lax.axis_size("hel")
    return lax.ppermute(array, "hel", [(i, i + step) for i in range(size) if 0 <= i + step < size])


def body(
    wavepacket,
    potential,
    kinetic,
    ang_basis,
    rot_energy,
    radial_weight,
    distance_weight,
    truncation,
    coupling,
):
    count, _, cells, _ = wavepacket.shape
    size = lax.axis_size("ang")
    chunks = cells // size
    ranks = sorted(range(1, size), key=lambda d: -(d // 2))
    quarter = max(count // 4, 1)
    spans = [[(0, count)] for _ in range(chunks)]
    spans[0] = [(0, quarter), (quarter, count)]
    result_spans = [[(0, count)] for _ in range(chunks)]
    result_spans[-1] = [(0, count - quarter), (count - quarter, count)]

    received = []
    for c in range(chunks):
        segments = []
        for s, span in enumerate(spans[c]):
            sent = pack(wavepacket, c, span, potential if (c, s) == (0, 0) else None)
            segments.append(swap(sent, "ang", ranks))
        received.append(segments)
    slabs = len(slabs_of(chunks))
    potentials = spread_potential(gather(received[0][0], quarter, quarter + slabs), chunks)

    orders = jnp.arange(ang_basis.shape[1], dtype=jnp.int32)
    mask = (orders[None, :] < truncation[:, None]).astype(jnp.float32)
    factor = mask * rot_energy[None, :]
    mats = jnp.einsum(
        "kji,kjm->kim", ang_basis * factor[:, :, None], ang_basis, precision=lax.Precision.HIGHEST
    )
    mats_below = along_hel(mats[-OUTER:], 1)
    mats_above = along_hel(mats[:OUTER], -1)

    first = lax.axis_index("hel") * count
    ends = jnp.concatenate([jnp.zeros((OUTER + 1,)), coupling[:-1], jnp.zeros((OUTER + 1,))])
    near = lax.dynamic_slice_in_dim(ends, first, count + 2 * OUTER + 1)
    halos = {}
    done = {}

    def exchange(c):
        segments = received[c]
        if c >= 2:
            segments, _ = lax.optimization_barrier((segments, done[c - 2][0][0]))
        lows, highs = edges(segments, spans[c])
        halos[c] = segments, along_hel(highs, 1), along_hel(lows, -1), lows

    exchange(0)
    backs = []
    for c in range(chunks):
        weights = near * lax.dynamic_index_in_dim(
            distance_weight, c * size + lax.axis_index("ang"), keepdims=False
        )
        segments, below, above, _ = halos[c]
        if c + 1 < chunks:
            exchange(c + 1)
            weights, _ = lax.optimization_barrier((weights, halos[c + 1][3]))
        done[c] = window(
            segments,
            spans[c],
            result_spans[c],
            potentials[c],
            below,
            above,
            mats,
            mats_below,
            mats_above,
            kinetic,
            radial_weight[None],
            weights,
        )
        for s, segment in enumerate(done[c]):
            backs.append((swap(segment, "ang", ranks), c, result_spans[c][s]))
    out = None
    for back, c, span in backs:
        out = unpack(back, out, wavepacket.shape, c, span)
    return out


def solution(mesh):
    placed = (
        P("hel", "ang", None, None),
        P("ang", None, None),
        P(),
        P("hel", None, None),
        P(),
        P(),
        P(),
        P("hel"),
        P(),
    )
    whole = P("hel", "ang", None, None)
    return jax.shard_map(body, mesh=mesh, in_specs=placed, out_specs=whole, check_vma=False)
```

time: 475 us -> 453 us (0.954)
  Pallas kernels: 142 us -> 116 us
  starting transfers between devices: 132 us -> 147 us
  waiting for transfers between devices: 182 us -> 175 us
    pallas_call x4, Pallas kernels: 109 us -> 77.2 us  [window(): pl.pallas_call(kernel, name='window', in_specs=[pl.BlockSpec(memory_space...]
    ppermute x66 -> x73, starting transfers between devices: 96.9 us -> 118 us  [swap(): lax.ppermute(arrays[d], axis, [(i, i ^ d) for i in range(size)])]
    ppermute x10, starting transfers between devices: 34.9 us -> 28.7 us  [along_hel(): lax.ppermute(array, 'hel', [(i, i + step) for i in range(size) if 0 <= i...]
    pallas_call x13 -> x15, Pallas kernels: 33.4 us -> 38.8 us  [the longest x5 15.5 us: pack(): pl.pallas_call(kernel, name='pack', grid=((stop - start) // block, width...]
    ppermute x66 -> x73, waiting for transfers between devices: 180 us -> 175 us  [swap(): lax.ppermute(arrays[d], axis, [(i, i ^ d) for i in range(size)])]
  transfers between devices with their start and end apart: 76 -> 83, of which waited for: 28 -> 31; matrix products, arithmetic and copies ran while one was open for 2% -> 2% of each run, Pallas kernels for 29% -> 25%
where the time goes in v3:
time: 453 us; the launch traced here: 451 us
  waiting for transfers between devices  175 us (39%)
  starting transfers between devices  147 us (32%)
  Pallas kernels  116 us (26%)
  local copies, waits for them, and re-layouts  5.51 us (1%)
  other arithmetic  4.91 us (1%)
    ppermute x73, waiting for transfers between devices, swap(): lax.ppermute(arrays[d], axis, [(i, i ^ d) for i in range(size)])  175 us
    ppermute x73, starting transfers between devices, swap(): lax.ppermute(arrays[d], axis, [(i, i ^ d) for i in range(size)])  118 us
    pallas_call x4, Pallas kernels, window(): pl.pallas_call(kernel, name='window', in_specs=[pl.BlockSpec(memory_space...  77.2 us
    ppermute x10, starting transfers between devices, along_hel(): lax.ppermute(array, 'hel', [(i, i + step) for i in range(size) if 0 <= i...  28.7 us
    pallas_call x5, Pallas kernels, pack(): pl.pallas_call(kernel, name='pack', grid=((stop - start) // block, width...  15.5 us
    pallas_call x5, Pallas kernels, unpack(): pl.pallas_call(kernel, name='unpack', grid=((stop - start) // block, widt...  13.1 us
  transfers between devices with their start and end apart: 83, of which 31 were waited for; matrix products, arithmetic and copies ran while one was open for 2% of the time, Pallas kernels for 25%

profile of v3, /device:TPU:13, one launch (start us, length us, event | category | flops | bytes accessed | tf_op | source)
XLA Modules:
  0.0 451.1 jit_solution(78201282499733185)
XLA Ops:
  14.2 4.7 %pack.9 = (f32[12,16,256]{2,1,0:T(8,128)}, f32[12,16,256]{2,1,0:T(8,128)}, f32[12,16,256]{2,1,0:T(8,128)}, f32[12,16,256]{2,1,0:T(8,128)}, f32[12,16,256]{2,1,0:...) custom-call(f32[16,16,32,256]{3,2,1,0:T(8,128)} %refs_0_.9), custom_call_target="tpu_custom_call" | custom-call | tf_op jit(solution)/shard_map/pack/pallas_call | solution.py:53
  29.3 4.1 collective-permute-start.30
  42.9 12.0 %collective-permute-start.36 = (f32[8,16,256]{2,1,0:T(8,128)}, f32[8,16,256]{2,1,0:T(8,128)}, u32[]{:S(2)}, u32[]{:S(2)}) collective-permute-start(f32[8,16,256]{2,1,0:T(8,128)} %bitcast.21), channel_id=1, source_target_pairs={{0,16},{8,24},{16,0},{24,8},{1,17},{9,25},{17,1},{25,9},{2,18},{10... | collective-permute-start | bytes 393224 | tf_op jit(solution)/shard_map/ppermute | solution.py:20
  65.8 3.8 collective-permute-done.34.refs_15_.refs_18_
  85.5 19.7 %collective-permute-done.18.refs_5_.refs_8_ = f32[16,16,256]{2,1,0:T(8,128)S(1)} collective-permute-done((f32[16,16,256]{2,1,0:T(8,128)}, f32[16,16,256]{2,1,0:T(8,128)S(1)}, u32[]{:S(2)}, u32[]{:S(2)}) %collective-permute-start.18) | collective-permute-done | bytes 262176 | tf_op jit(solution)/shard_map/ppermute | solution.py:20
  105.1 3.7 collective-permute-start.9
  108.8 4.1 collective-permute-done.19.refs_6_.refs_9_
  113.6 11.9 %collective-permute-done.20.refs_7_.refs_10_ = f32[16,16,256]{2,1,0:T(8,128)S(1)} collective-permute-done((f32[16,16,256]{2,1,0:T(8,128)}, f32[16,16,256]{2,1,0:T(8,128)S(1)}, u32[]{:S(2)}, u32[]{:S(2)}) %collective-permute-start.20) | collective-permute-done | bytes 262176 | tf_op jit(solution)/shard_map/ppermute | solution.py:20
  130.5 17.3 %collective-permute-start.1 = (f32[16,16,256]{2,1,0:T(8,128)}, f32[16,16,256]{2,1,0:T(8,128)S(1)}, u32[]{:S(2)}, u32[]{:S(2)}) collective-permute-start(f32[16,16,256]{2,1,0:T(8,128)} %get-tuple-element.114), channel_id=1, source_target_pairs={{0,2},{1,3},{2,0},{3,1},{4,6},{5,7},{6,4},{7,5},{8,10},{9,11},{10,... | collective-permute-start | bytes 786440 | tf_op jit(solution)/shard_map/ppermute | solution.py:20
  150.1 3.7 collective-permute-start.2
  177.3 13.9 %collective-permute-done.3.refs_4_.refs_7_ = f32[16,16,256]{2,1,0:T(8,128)} collective-permute-done((f32[16,16,256]{2,1,0:T(8,128)}, f32[16,16,256]{2,1,0:T(8,128)}, u32[]{:S(2)}, u32[]{:S(2)}) %collective-permute-start.3) | collective-permute-done | bytes 262176 | tf_op jit(solution)/shard_map/ppermute | solution.py:20
  195.0 3.9 collective-permute-start.43
  200.8 19.4 %window.4 = (f32[16,16,256]{2,1,0:T(8,128)}, f32[16,16,256]{2,1,0:T(8,128)}, f32[16,16,256]{2,1,0:T(8,128)}, f32[16,16,256]{2,1,0:T(8,128)}, f32[16,16,256]{2,1,...) custom-call(f32[23]{0:T(128)} %get-tuple-element.137.refs_0_, ...), custom_call_target="tpu_custom_call" | custom-call | tf_op jit(solution)/shard_map/window/pallas_call | solution.py:276
  221.1 3.7 collective-permute-start.77
  228.1 10.3 %collective-permute-done.77.refs_2_ = f32[16,16,256]{2,1,0:T(8,128)} collective-permute-done((f32[16,16,256]{2,1,0:T(8,128)}, f32[16,16,256]{2,1,0:T(8,128)}, u32[]{:S(2)}, u32[]{:S(2)}) %collective-permute-start.77) | collective-permute-done | bytes 262176 | tf_op jit(solution)/shard_map/ppermute | solution.py:20
  243.8 19.3 %window.5 = (f32[16,16,256]{2,1,0:T(8,128)}, f32[16,16,256]{2,1,0:T(8,128)}, f32[16,16,256]{2,1,0:T(8,128)}, f32[16,16,256]{2,1,0:T(8,128)}, f32[16,16,256]{2,1,...) custom-call(f32[23]{0:T(128)} %get-tuple-element.166.refs_0_, ...), custom_call_target="tpu_custom_call" | custom-call | tf_op jit(solution)/shard_map/window/pallas_call | solution.py:276
  267.3 4.3 collective-permute-start.45
  277.5 7.8 %collective-permute-done.70.refs_2_ = f32[16,16,256]{2,1,0:T(8,128)S(1)} collective-permute-done((f32[16,16,256]{2,1,0:T(8,128)}, f32[16,16,256]{2,1,0:T(8,128)S(1)}, u32[]{:S(2)}, u32[]{:S(2)}) %collective-permute-start.70) | collective-permute-done | bytes 262176 | tf_op jit(solution)/shard_map/ppermute | solution.py:20
  287.3 3.7 collective-permute-done.71.refs_3_
  293.2 4.4 collective-permute-start.73
  299.5 19.3 %window.6 = (f32[12,16,256]{2,1,0:T(8,128)}, f32[12,16,256]{2,1,0:T(8,128)}, f32[12,16,256]{2,1,0:T(8,128)}, f32[12,16,256]{2,1,0:T(8,128)}, f32[12,16,256]{2,1,...) custom-call(f32[23]{0:T(128)} %get-tuple-element.229.refs_0_, ...), custom_call_target="tpu_custom_call" | custom-call | tf_op jit(solution)/shard_map/window/pallas_call | solution.py:276
  320.3 7.0 %collective-permute-done.74.refs_6_ = f32[16,16,256]{2,1,0:T(8,128)S(1)} collective-permute-done((f32[16,16,256]{2,1,0:T(8,128)}, f32[16,16,256]{2,1,0:T(8,128)S(1)}, u32[]{:S(2)}, u32[]{:S(2)}) %collective-permute-start.74) | collective-permute-done | bytes 262176 | tf_op jit(solution)/shard_map/ppermute | solution.py:20
  327.3 5.6 %collective-permute-done.75.refs_7_ = f32[16,16,256]{2,1,0:T(8,128)S(1)} collective-permute-done((f32[16,16,256]{2,1,0:T(8,128)}, f32[16,16,256]{2,1,0:T(8,128)S(1)}, u32[]{:S(2)}, u32[]{:S(2)}) %collective-permute-start.75) | collective-permute-done | bytes 262176 | tf_op jit(solution)/shard_map/ppermute | solution.py:20
  336.4 19.2 %window.7 = (f32[16,16,256]{2,1,0:T(8,128)}, f32[16,16,256]{2,1,0:T(8,128)}, f32[16,16,256]{2,1,0:T(8,128)}, f32[16,16,256]{2,1,0:T(8,128)}, f32[16,16,256]{2,1,...) custom-call(f32[23]{0:T(128)} %get-tuple-element.195.refs_0_, ...), custom_call_target="tpu_custom_call" | custom-call | tf_op jit(solution)/shard_map/window/pallas_call | solution.py:276
  360.7 9.6 %collective-permute-done.57.refs_5_ = f32[12,16,256]{2,1,0:T(8,128)S(1)} collective-permute-done((f32[12,16,256]{2,1,0:T(8,128)}, f32[12,16,256]{2,1,0:T(8,128)S(1)}, u32[]{:S(2)}, u32[]{:S(2)}) %collective-permute-start.57) | collective-permute-done | bytes 196640 | tf_op jit(solution)/shard_map/ppermute | solution.py:20
  371.0 10.5 %collective-permute-done.58.refs_6_ = f32[12,16,256]{2,1,0:T(8,128)S(1)} collective-permute-done((f32[12,16,256]{2,1,0:T(8,128)}, f32[12,16,256]{2,1,0:T(8,128)S(1)}, u32[]{:S(2)}, u32[]{:S(2)}) %collective-permute-start.58) | collective-permute-done | bytes 196640 | tf_op jit(solution)/shard_map/ppermute | solution.py:20
  381.6 10.1 %collective-permute-done.59.refs_7_ = f32[12,16,256]{2,1,0:T(8,128)S(1)} collective-permute-done((f32[12,16,256]{2,1,0:T(8,128)}, f32[12,16,256]{2,1,0:T(8,128)S(1)}, u32[]{:S(2)}, u32[]{:S(2)}) %collective-permute-start.59) | collective-permute-done | bytes 196640 | tf_op jit(solution)/shard_map/ppermute | solution.py:20
  393.5 4.1 collective-permute-start.48
  397.6 15.3 %collective-permute-done.65.refs_4_ = f32[16,16,256]{2,1,0:T(8,128)S(1)} collective-permute-done((f32[16,16,256]{2,1,0:T(8,128)}, f32[16,16,256]{2,1,0:T(8,128)S(1)}, u32[]{:S(2)}, u32[]{:S(2)}) %collective-permute-start.65) | collective-permute-done | bytes 262176 | tf_op jit(solution)/shard_map/ppermute | solution.py:20
  415.9 4.0 collective-permute-done.66.refs_5_
  423.2 7.5 %collective-permute-done.67.refs_6_ = f32[16,16,256]{2,1,0:T(8,128)S(1)} collective-permute-done((f32[16,16,256]{2,1,0:T(8,128)}, f32[16,16,256]{2,1,0:T(8,128)S(1)}, u32[]{:S(2)}, u32[]{:S(2)}) %collective-permute-start.67) | collective-permute-done | bytes 262176 | tf_op jit(solution)/shard_map/ppermute | solution.py:20
  431.9 4.8 %collective-permute-done.68.refs_7_ = f32[16,16,256]{2,1,0:T(8,128)} collective-permute-done((f32[16,16,256]{2,1,0:T(8,128)}, f32[16,16,256]{2,1,0:T(8,128)}, u32[]{:S(2)}, u32[]{:S(2)}) %collective-permute-start.68) | collective-permute-done | bytes 262176 | tf_op jit(solution)/shard_map/ppermute | solution.py:20
  (303 shorter events, 157.5 us)
Async XLA Ops:
  36.8 32.8 %collective-permute-start.34 = (f32[12,16,256]{2,1,0:T(8,128)}, f32[12,16,256]{2,1,0:T(8,128)S(1)}, u32[]{:S(2)}, u32[]{:S(2)}) collective-permute-start(f32[12,16,256]{2,1,0:T(8,128)} %get-tuple-element.153), channel_id=1, source_target_pairs={{0,7},{1,6},{2,5},{3,4},{4,3},{5,2},{6,1},{7,0},{8,15},{9,14},{10,... | collective-permute-start | bytes 589832 | tf_op jit(solution)/shard_map/ppermute | solution.py:20
  74.7 38.2 %collective-permute-start.19 = (f32[16,16,256]{2,1,0:T(8,128)}, f32[16,16,256]{2,1,0:T(8,128)S(1)}, u32[]{:S(2)}, u32[]{:S(2)}) collective-permute-start(f32[16,16,256]{2,1,0:T(8,128)} %get-tuple-element.134), channel_id=1, source_target_pairs={{0,6},{1,7},{2,4},{3,5},{4,2},{5,3},{6,0},{7,1},{8,14},{9,15},{10,... | collective-permute-start | bytes 786440 | tf_op jit(solution)/shard_map/ppermute | solution.py:20
  75.5 50.1 %collective-permute-start.20 = (f32[16,16,256]{2,1,0:T(8,128)}, f32[16,16,256]{2,1,0:T(8,128)S(1)}, u32[]{:S(2)}, u32[]{:S(2)}) collective-permute-start(f32[16,16,256]{2,1,0:T(8,128)} %get-tuple-element.135), channel_id=1, source_target_pairs={{0,7},{1,6},{2,5},{3,4},{4,3},{5,2},{6,1},{7,0},{8,15},{9,14},{10,... | collective-permute-start | bytes 786440 | tf_op jit(solution)/shard_map/ppermute | solution.py:20
  82.2 43.4 %collective-permute-start.7 = (f32[16,16,256]{2,1,0:T(8,128)}, f32[16,16,256]{2,1,0:T(8,128)S(1)}, u32[]{:S(2)}, u32[]{:S(2)}) collective-permute-start(f32[16,16,256]{2,1,0:T(8,128)} %get-tuple-element.121), channel_id=1, source_target_pairs={{0,1},{1,0},{2,3},{3,2},{4,5},{5,4},{6,7},{7,6},{8,9},{9,8},{10,11... | collective-permute-start | bytes 786440 | tf_op jit(solution)/shard_map/ppermute | solution.py:20
  84.4 41.7 %collective-permute-start.8 = (f32[16,16,256]{2,1,0:T(8,128)}, f32[16,16,256]{2,1,0:T(8,128)S(1)}, u32[]{:S(2)}, u32[]{:S(2)}) collective-permute-start(f32[16,16,256]{2,1,0:T(8,128)} %get-tuple-element.122), channel_id=1, source_target_pairs={{0,2},{1,3},{2,0},{3,1},{4,6},{5,7},{6,4},{7,5},{8,10},{9,11},{10,... | collective-permute-start | bytes 786440 | tf_op jit(solution)/shard_map/ppermute | solution.py:20
  125.6 32.3 %collective-permute-start.12 = (f32[16,16,256]{2,1,0:T(8,128)}, f32[16,16,256]{2,1,0:T(8,128)S(1)}, u32[]{:S(2)}, u32[]{:S(2)}) collective-permute-start(f32[16,16,256]{2,1,0:T(8,128)} %get-tuple-element.126), channel_id=1, source_target_pairs={{0,6},{1,7},{2,4},{3,5},{4,2},{5,3},{6,0},{7,1},{8,14},{9,15},{10,... | collective-permute-start | bytes 786440 | tf_op jit(solution)/shard_map/ppermute | solution.py:20
  126.0 38.1 %collective-permute-start.13 = (f32[16,16,256]{2,1,0:T(8,128)}, f32[16,16,256]{2,1,0:T(8,128)S(1)}, u32[]{:S(2)}, u32[]{:S(2)}) collective-permute-start(f32[16,16,256]{2,1,0:T(8,128)} %get-tuple-element.127), channel_id=1, source_target_pairs={{0,7},{1,6},{2,5},{3,4},{4,3},{5,2},{6,1},{7,0},{8,15},{9,14},{10,... | collective-permute-start | bytes 786440 | tf_op jit(solution)/shard_map/ppermute | solution.py:20
  129.2 39.2 %collective-permute-start = (f32[16,16,256]{2,1,0:T(8,128)}, f32[16,16,256]{2,1,0:T(8,128)S(1)}, u32[]{:S(2)}, u32[]{:S(2)}) collective-permute-start(f32[16,16,256]{2,1,0:T(8,128)} %get-tuple-element.113), channel_id=1, source_target_pairs={{0,1},{1,0},{2,3},{3,2},{4,5},{5,4},{6,7},{7,6},{8,9},{9,8},{10,11... | collective-permute-start | bytes 786440 | tf_op jit(solution)/shard_map/ppermute | solution.py:20
  130.5 39.3 %collective-permute-start.1 = (f32[16,16,256]{2,1,0:T(8,128)}, f32[16,16,256]{2,1,0:T(8,128)S(1)}, u32[]{:S(2)}, u32[]{:S(2)}) collective-permute-start(f32[16,16,256]{2,1,0:T(8,128)} %get-tuple-element.114), channel_id=1, source_target_pairs={{0,2},{1,3},{2,0},{3,1},{4,6},{5,7},{6,4},{7,5},{8,10},{9,11},{10,... | collective-permute-start | bytes 786440 | tf_op jit(solution)/shard_map/ppermute | solution.py:20
  157.9 34.6 %collective-permute-start.38 = (f32[8,3,16,256]{3,2,1,0:T(8,128)}, f32[8,3,16,256]{3,2,1,0:T(8,128)}, u32[]{:S(2)}, u32[]{:S(2)}) collective-permute-start(f32[8,3,16,256]{3,2,1,0:T(8,128)} %get-tuple-element.154), channel_id=1, source_target_pairs={{0,8},{8,16},{16,24},{1,9},{9,17},{17,25},{2,10},{10,18},{18,26},{... | collective-permute-start | bytes 1179656 | tf_op jit(solution)/shard_map/ppermute | solution.py:316
  169.8 50.5 %collective-permute-start.4 = (f32[16,16,256]{2,1,0:T(8,128)}, f32[16,16,256]{2,1,0:T(8,128)}, u32[]{:S(2)}, u32[]{:S(2)}) collective-permute-start(f32[16,16,256]{2,1,0:T(8,128)} %get-tuple-element.117), channel_id=1, source_target_pairs={{0,5},{1,4},{2,7},{3,6},{4,1},{5,0},{6,3},{7,2},{8,13},{9,12},{10,... | collective-permute-start | bytes 786440 | tf_op jit(solution)/shard_map/ppermute | solution.py:20
  172.7 48.4 %collective-permute-start.5 = (f32[16,16,256]{2,1,0:T(8,128)}, f32[16,16,256]{2,1,0:T(8,128)}, u32[]{:S(2)}, u32[]{:S(2)}) collective-permute-start(f32[16,16,256]{2,1,0:T(8,128)} %get-tuple-element.118), channel_id=1, source_target_pairs={{0,6},{1,7},{2,4},{3,5},{4,2},{5,3},{6,0},{7,1},{8,14},{9,15},{10,... | collective-permute-start | bytes 786440 | tf_op jit(solution)/shard_map/ppermute | solution.py:20
  191.2 33.6 %collective-permute-start.6 = (f32[16,16,256]{2,1,0:T(8,128)}, f32[16,16,256]{2,1,0:T(8,128)S(1)}, u32[]{:S(2)}, u32[]{:S(2)}) collective-permute-start(f32[16,16,256]{2,1,0:T(8,128)} %get-tuple-element.119), channel_id=1, source_target_pairs={{0,7},{1,6},{2,5},{3,4},{4,3},{5,2},{6,1},{7,0},{8,15},{9,14},{10,... | collective-permute-start | bytes 786440 | tf_op jit(solution)/shard_map/ppermute | solution.py:20
  192.6 32.6 %collective-permute-start.42 = (f32[8,3,16,256]{3,2,1,0:T(8,128)}, f32[8,3,16,256]{3,2,1,0:T(8,128)S(1)}, u32[]{:S(2)}, u32[]{:S(2)}) collective-permute-start(f32[8,3,16,256]{3,2,1,0:T(8,128)} %get-tuple-element.167), channel_id=1, source_target_pairs={{0,8},{8,16},{16,24},{1,9},{9,17},{17,25},{2,10},{10,18},{18,26},{... | collective-permute-start | bytes 1179656 | tf_op jit(solution)/shard_map/ppermute | solution.py:316
  195.0 31.5 %collective-permute-start.43 = (f32[8,3,16,256]{3,2,1,0:T(8,128)}, f32[8,3,16,256]{3,2,1,0:T(8,128)}, u32[]{:S(2)}, u32[]{:S(2)}) collective-permute-start(f32[8,3,16,256]{3,2,1,0:T(8,128)} %get-tuple-element.136), channel_id=1, source_target_pairs={{8,0},{16,8},{24,16},{9,1},{17,9},{25,17},{10,2},{18,10},{26,18},{... | collective-permute-start | bytes 1179656 | tf_op jit(solution)/shard_map/ppermute | solution.py:316
  224.8 38.3 %collective-permute-start.78 = (f32[16,16,256]{2,1,0:T(8,128)}, f32[16,16,256]{2,1,0:T(8,128)S(1)}, u32[]{:S(2)}, u32[]{:S(2)}) collective-permute-start(f32[16,16,256]{2,1,0:T(8,128)} %get-tuple-element.214), channel_id=1, source_target_pairs={{0,3},{1,2},{2,1},{3,0},{4,7},{5,6},{6,5},{7,4},{8,11},{9,10},{10,... | collective-permute-start | bytes 786440 | tf_op jit(solution)/shard_map/ppermute | solution.py:20
  225.1 40.2 %collective-permute-start.79 = (f32[16,16,256]{2,1,0:T(8,128)}, f32[16,16,256]{2,1,0:T(8,128)S(1)}, u32[]{:S(2)}, u32[]{:S(2)}) collective-permute-start(f32[16,16,256]{2,1,0:T(8,128)} %get-tuple-element.215), channel_id=1, source_target_pairs={{0,4},{1,5},{2,6},{3,7},{4,0},{5,1},{6,2},{7,3},{8,12},{9,13},{10,... | collective-permute-start | bytes 786440 | tf_op jit(solution)/shard_map/ppermute | solution.py:20
  226.5 40.8 %collective-permute-start.80 = (f32[16,16,256]{2,1,0:T(8,128)}, f32[16,16,256]{2,1,0:T(8,128)S(1)}, u32[]{:S(2)}, u32[]{:S(2)}) collective-permute-start(f32[16,16,256]{2,1,0:T(8,128)} %get-tuple-element.216), channel_id=1, source_target_pairs={{0,5},{1,4},{2,7},{3,6},{4,1},{5,0},{6,3},{7,2},{8,13},{9,12},{10,... | collective-permute-start | bytes 786440 | tf_op jit(solution)/shard_map/ppermute | solution.py:20
  228.1 43.5 %collective-permute-start.81 = (f32[16,16,256]{2,1,0:T(8,128)}, f32[16,16,256]{2,1,0:T(8,128)}, u32[]{:S(2)}, u32[]{:S(2)}) collective-permute-start(f32[16,16,256]{2,1,0:T(8,128)} %get-tuple-element.217), channel_id=1, source_target_pairs={{0,6},{1,7},{2,4},{3,5},{4,2},{5,3},{6,0},{7,1},{8,14},{9,15},{10,... | collective-permute-start | bytes 786440 | tf_op jit(solution)/shard_map/ppermute | solution.py:20
  238.4 36.4 %collective-permute-start.82 = (f32[16,16,256]{2,1,0:T(8,128)}, f32[16,16,256]{2,1,0:T(8,128)}, u32[]{:S(2)}, u32[]{:S(2)}) collective-permute-start(f32[16,16,256]{2,1,0:T(8,128)} %get-tuple-element.218), channel_id=1, source_target_pairs={{0,7},{1,6},{2,5},{3,4},{4,3},{5,2},{6,1},{7,0},{8,15},{9,14},{10,... | collective-permute-start | bytes 786440 | tf_op jit(solution)/shard_map/ppermute | solution.py:20
  265.4 32.2 %collective-permute-start.44 = (f32[8,3,16,256]{3,2,1,0:T(8,128)}, f32[8,3,16,256]{3,2,1,0:T(8,128)S(1)}, u32[]{:S(2)}, u32[]{:S(2)}) collective-permute-start(f32[8,3,16,256]{3,2,1,0:T(8,128)} %get-tuple-element.177), channel_id=1, source_target_pairs={{0,8},{8,16},{16,24},{1,9},{9,17},{17,25},{2,10},{10,18},{18,26},{... | collective-permute-start | bytes 1179656 | tf_op jit(solution)/shard_map/ppermute | solution.py:316
  285.3 47.6 %collective-permute-start.60 = (f32[8,3,16,256]{3,2,1,0:T(8,128)}, f32[8,3,16,256]{3,2,1,0:T(8,128)S(1)}, u32[]{:S(2)}, u32[]{:S(2)}) collective-permute-start(f32[8,3,16,256]{3,2,1,0:T(8,128)} %get-tuple-element.196), channel_id=1, source_target_pairs={{0,8},{8,16},{16,24},{1,9},{9,17},{17,25},{2,10},{10,18},{18,26},{... | collective-permute-start | bytes 1179656 | tf_op jit(solution)/shard_map/ppermute | solution.py:316
  290.9 43.8 %collective-permute-start.61 = (f32[8,3,16,256]{3,2,1,0:T(8,128)}, f32[8,3,16,256]{3,2,1,0:T(8,128)S(1)}, u32[]{:S(2)}, u32[]{:S(2)}) collective-permute-start(f32[8,3,16,256]{3,2,1,0:T(8,128)} %get-tuple-element.165), channel_id=1, source_target_pairs={{8,0},{16,8},{24,16},{9,1},{17,9},{25,17},{10,2},{18,10},{26,18},{... | collective-permute-start | bytes 1179656 | tf_op jit(solution)/shard_map/ppermute | solution.py:316
  298.7 34.2 %collective-permute-start.75 = (f32[16,16,256]{2,1,0:T(8,128)}, f32[16,16,256]{2,1,0:T(8,128)S(1)}, u32[]{:S(2)}, u32[]{:S(2)}) collective-permute-start(f32[16,16,256]{2,1,0:T(8,128)} %get-tuple-element.211), channel_id=1, source_target_pairs={{0,7},{1,6},{2,5},{3,4},{4,3},{5,2},{6,1},{7,0},{8,15},{9,14},{10,... | collective-permute-start | bytes 786440 | tf_op jit(solution)/shard_map/ppermute | solution.py:20
  320.0 36.3 %collective-permute-start.53 = (f32[12,16,256]{2,1,0:T(8,128)}, f32[12,16,256]{2,1,0:T(8,128)S(1)}, u32[]{:S(2)}, u32[]{:S(2)}) collective-permute-start(f32[12,16,256]{2,1,0:T(8,128)} %get-tuple-element.188), channel_id=1, source_target_pairs={{0,1},{1,0},{2,3},{3,2},{4,5},{5,4},{6,7},{7,6},{8,9},{9,8},{10,11... | collective-permute-start | bytes 589832 | tf_op jit(solution)/shard_map/ppermute | solution.py:20
  355.6 36.0 %collective-permute-start.62 = (f32[16,16,256]{2,1,0:T(8,128)}, f32[16,16,256]{2,1,0:T(8,128)S(1)}, u32[]{:S(2)}, u32[]{:S(2)}) collective-permute-start(f32[16,16,256]{2,1,0:T(8,128)} %get-tuple-element.198), channel_id=1, source_target_pairs={{0,1},{1,0},{2,3},{3,2},{4,5},{5,4},{6,7},{7,6},{8,9},{9,8},{10,11... | collective-permute-start | bytes 786440 | tf_op jit(solution)/shard_map/ppermute | solution.py:20
  356.3 36.6 %collective-permute-start.63 = (f32[16,16,256]{2,1,0:T(8,128)}, f32[16,16,256]{2,1,0:T(8,128)S(1)}, u32[]{:S(2)}, u32[]{:S(2)}) collective-permute-start(f32[16,16,256]{2,1,0:T(8,128)} %get-tuple-element.199), channel_id=1, source_target_pairs={{0,2},{1,3},{2,0},{3,1},{4,6},{5,7},{6,4},{7,5},{8,10},{9,11},{10,... | collective-permute-start | bytes 786440 | tf_op jit(solution)/shard_map/ppermute | solution.py:20
  359.3 32.4 %collective-permute-start.59 = (f32[12,16,256]{2,1,0:T(8,128)}, f32[12,16,256]{2,1,0:T(8,128)S(1)}, u32[]{:S(2)}, u32[]{:S(2)}) collective-permute-start(f32[12,16,256]{2,1,0:T(8,128)} %get-tuple-element.194), channel_id=1, source_target_pairs={{0,7},{1,6},{2,5},{3,4},{4,3},{5,2},{6,1},{7,0},{8,15},{9,14},{10,... | collective-permute-start | bytes 589832 | tf_op jit(solution)/shard_map/ppermute | solution.py:20
  391.7 38.9 %collective-permute-start.67 = (f32[16,16,256]{2,1,0:T(8,128)}, f32[16,16,256]{2,1,0:T(8,128)S(1)}, u32[]{:S(2)}, u32[]{:S(2)}) collective-permute-start(f32[16,16,256]{2,1,0:T(8,128)} %get-tuple-element.203), channel_id=1, source_target_pairs={{0,6},{1,7},{2,4},{3,5},{4,2},{5,3},{6,0},{7,1},{8,14},{9,15},{10,... | collective-permute-start | bytes 786440 | tf_op jit(solution)/shard_map/ppermute | solution.py:20
  392.9 43.8 %collective-permute-start.68 = (f32[16,16,256]{2,1,0:T(8,128)}, f32[16,16,256]{2,1,0:T(8,128)}, u32[]{:S(2)}, u32[]{:S(2)}) collective-permute-start(f32[16,16,256]{2,1,0:T(8,128)} %get-tuple-element.204), channel_id=1, source_target_pairs={{0,7},{1,6},{2,5},{3,4},{4,3},{5,2},{6,1},{7,0},{8,15},{9,14},{10,... | collective-permute-start | bytes 786440 | tf_op jit(solution)/shard_map/ppermute | solution.py:20
  393.5 55.8 %collective-permute-start.48 = (f32[4,16,256]{2,1,0:T(8,128)}, f32[4,16,256]{2,1,0:T(8,128)}, u32[]{:S(2)}, u32[]{:S(2)}) collective-permute-start(f32[4,16,256]{2,1,0:T(8,128)} %get-tuple-element.182), channel_id=1, source_target_pairs={{0,3},{1,2},{2,1},{3,0},{4,7},{5,6},{6,5},{7,4},{8,11},{9,10},{10,... | collective-permute-start | bytes 196616 | tf_op jit(solution)/shard_map/ppermute | solution.py:20
  412.9 36.4 %collective-permute-start.49 = (f32[4,16,256]{2,1,0:T(8,128)}, f32[4,16,256]{2,1,0:T(8,128)}, u32[]{:S(2)}, u32[]{:S(2)}) collective-permute-start(f32[4,16,256]{2,1,0:T(8,128)} %get-tuple-element.183), channel_id=1, source_target_pairs={{0,4},{1,5},{2,6},{3,7},{4,0},{5,1},{6,2},{7,3},{8,12},{9,13},{10,... | collective-permute-start | bytes 196616 | tf_op jit(solution)/shard_map/ppermute | solution.py:20
  (121 other events, 4601.7 us)

commit v4 on v3

--- a/solution.py
+++ b/solution.py
@@ -9,7 +9,8 @@
 
 
 OUTER = 3
-GROUP = 6
+GROUP = 4
+GRANT = 24 << 20
 LANES = 128
 
 
@@ -28,34 +29,48 @@
 def pack(wave, chunk, span, potential=None):
     _, angles, cells, width = wave.shape
     start, stop = span
-    block = math.gcd(start, stop) if potential is None else stop - start
+    block = math.gcd(start, stop, max(wave.shape[0] // 4, 1))
+    many = 1 if potential is None else (stop - start) // block
     size = lax.axis_size("ang")
     extra = 0 if potential is None else len(slabs_of(cells // size))
 
+    lanes = width // LANES
+
     def kernel(*refs):
-        wave_ref, outs = refs[0], refs[-size:]
+        waves, outs = refs[: many * lanes], refs[-size:]
         slabs = slabs_of(cells // size) if extra else []
         for d in range(size):
             first = place(d)
-            for k in range(block):
-                rows = wave_ref.at[k].reshape(angles * size, LANES)
-                outs[d][k] = rows[pl.ds(first, angles, stride=size), :]
-            for s, slab in enumerate(slabs):
-                rows = refs[1].reshape(angles * cells, LANES)
-                outs[d][block + s] = rows[pl.ds(slab * size + first, angles, stride=cells), :]
-
-    args = [wave]
-    specs = [pl.BlockSpec((block, angles, size, LANES), lambda k, g: (start // block + k, 0, chunk, g))]
+            for g in range(lanes):
+                columns = slice(g * LANES, (g + 1) * LANES)
+                for k in range(many * block):
+                    rows = waves[k // block * lanes + g].at[k % block].reshape(angles * size, LANES)
+                    outs[d][k, :, columns] = rows[pl.ds(first, angles, stride=size), :]
+                for s, slab in enumerate(slabs):
+                    rows = refs[many * lanes + g].reshape(angles * cells, LANES)
+                    outs[d][many * block + s, :, columns] = rows[pl.ds(slab * size + first, angles, stride=cells), :]
+
+    def wave_spec(j, g):
+        return pl.BlockSpec(
+            (block, angles, size, LANES), lambda k: (start // block + k * many + j, 0, chunk, g)
+        )
+
+    def potential_spec(g):
+        return pl.BlockSpec((angles, cells, LANES), lambda k: (0, 0, g))
+
+    args = [pltpu.with_memory_space_constraint(wave, pltpu.HBM)] * (many * lanes)
+    specs = [wave_spec(j, g) for j in range(many) for g in range(lanes)]
     if extra:
-        args.append(potential)
-        specs.append(pl.BlockSpec((angles, cells, LANES), lambda k, g: (0, 0, g)))
+        args += [pltpu.with_memory_space_constraint(potential, pltpu.HBM)] * lanes
+        specs += [potential_spec(g) for g in range(lanes)]
     packed = (stop - start + extra, angles, width)
     return pl.pallas_call(
         kernel,
         name="pack",
-        grid=((stop - start) // block, width // LANES),
+        compiler_params=pltpu.CompilerParams(vmem_limit_bytes=GRANT),
+        grid=((stop - start) // (many * block),),
         in_specs=specs,
-        out_specs=[pl.BlockSpec((block + extra, angles, LANES), lambda k, g: (k, 0, g))] * size,
+        out_specs=[pl.BlockSpec((many * block + extra, angles, width), lambda k: (k, 0, 0))] * size,
         out_shape=[jax.ShapeDtypeStruct(packed, jnp.float32)] * size,
     )(*args)
 
@@ -63,19 +78,33 @@
 def unpack(pieces, whole, shape, chunk, span):
     _, angles, _, width = shape
     start, stop = span
-    block = math.gcd(start, stop)
+    amount = stop - start
     size = len(pieces)
+    lanes = width // LANES
 
     def kernel(*refs):
-        ins, out = refs[:size], refs[-1]
-        for d in range(size):
-            first = place(d)
-            for k in range(block):
-                rows = out.at[k].reshape(angles * size, LANES)
-                rows[pl.ds(first, angles, stride=size), :] = ins[d][k]
+        ins, out, parts, sems = refs[:size], refs[-3], refs[-2], refs[-1]
+        copies = []
+        for g in range(lanes):
+            columns = slice(g * LANES, (g + 1) * LANES)
+            for d in range(size):
+                first = place(d)
+                for k in range(amount):
+                    rows = parts.at[g, k].reshape(angles * size, LANES)
+                    rows[pl.ds(first, angles, stride=size), :] = ins[d][k, :, columns]
+            copies.append(
+                pltpu.make_async_copy(
+                    parts.at[g],
+                    out.at[pl.ds(start, amount), :, pl.ds(chunk * size, size), pl.ds(g * LANES, LANES)],
+                    sems.at[g],
+                )
+            )
+            copies[-1].start()
+        for copy in copies:
+            copy.wait()
 
     args = [*pieces]
-    specs = [pl.BlockSpec((block, angles, LANES), lambda k, g: (k, 0, g))] * size
+    specs = [pl.BlockSpec(memory_space=pltpu.VMEM)] * size
     aliases = {}
     if whole is not None:
         aliases = {len(args): 0}
@@ -84,12 +113,14 @@
     return pl.pallas_call(
         kernel,
         name="unpack",
-        grid=((stop - start) // block, width // LANES),
+        compiler_params=pltpu.CompilerParams(vmem_limit_bytes=GRANT),
         in_specs=specs,
-        out_specs=pl.BlockSpec(
-            (block, angles, size, LANES), lambda k, g: (start // block + k, 0, chunk, g)
-        ),
+        out_specs=pl.BlockSpec(memory_space=pl.ANY),
         out_shape=jax.ShapeDtypeStruct(shape, jnp.float32),
+        scratch_shapes=[
+            pltpu.VMEM((lanes, amount, angles, size, LANES), jnp.float32),
+            pltpu.SemaphoreType.DMA((lanes,)),
+        ],
         input_output_aliases=aliases,
     )(*args)
 
@@ -116,6 +147,7 @@
     return pl.pallas_call(
         kernel,
         name="gather",
+        compiler_params=pltpu.CompilerParams(vmem_limit_bytes=GRANT),
         in_specs=[pl.BlockSpec(memory_space=pl.ANY)] * size,
         out_specs=pl.BlockSpec(memory_space=pltpu.VMEM),
         out_shape=jax.ShapeDtypeStruct(shape, jnp.float32),
@@ -169,6 +201,7 @@
     return pl.pallas_call(
         kernel,
         name="edges",
+        compiler_params=pltpu.CompilerParams(vmem_limit_bytes=GRANT),
         in_specs=[pl.BlockSpec(memory_space=pl.ANY)] * (size * len(spans)),
         out_specs=[pl.BlockSpec(memory_space=pltpu.VMEM)] * 2,
         out_shape=[shape] * 2,
@@ -276,6 +309,7 @@
     results = pl.pallas_call(
         kernel,
         name="window",
+        compiler_params=pltpu.CompilerParams(vmem_limit_bytes=GRANT),
         in_specs=[
             pl.BlockSpec(memory_space=pltpu.SMEM),
             pl.BlockSpec(memory_space=pltpu.VMEM),
@@ -335,17 +369,18 @@
     spans = [[(0, count)] for _ in range(chunks)]
     spans[0] = [(0, quarter), (quarter, count)]
     result_spans = [[(0, count)] for _ in range(chunks)]
-    result_spans[-1] = [(0, count - quarter), (count - quarter, count)]
+    tail = max(count // 8, 1)
+    result_spans[-1] = [(0, count - tail), (count - tail, count)]
 
     received = []
     for c in range(chunks):
         segments = []
         for s, span in enumerate(spans[c]):
-            sent = pack(wavepacket, c, span, potential if (c, s) == (0, 0) else None)
+            sent = pack(wavepacket, c, span, potential if (c, s) == (0, 1) else None)
             segments.append(swap(sent, "ang", ranks))
         received.append(segments)
     slabs = len(slabs_of(chunks))
-    potentials = spread_potential(gather(received[0][0], quarter, quarter + slabs), chunks)
+    potentials = spread_potential(gather(received[0][1], count - quarter, count - quarter + slabs), chunks)
 
     orders = jnp.arange(ang_basis.shape[1], dtype=jnp.int32)
     mask = (orders[None, :] < truncation[:, None]).astype(jnp.float32)

time: 453 us -> 434 us (0.958)
  the two profiles are of different devices: /device:TPU:13 before, /device:TPU:11 now
where the time goes in v4:
time: 434 us; the launch traced here: 433 us
  waiting for transfers between devices  180 us (41%)
  starting transfers between devices  116 us (27%)
  Pallas kernels  100 us (23%)
  local copies, waits for them, and re-layouts  29.6 us (7%)
  other arithmetic  4.5 us (1%)
    ppermute x73, waiting for transfers between devices, swap(): lax.ppermute(arrays[d], axis, [(i, i ^ d) for i in range(size)])  180 us
    ppermute x73, starting transfers between devices, swap(): lax.ppermute(arrays[d], axis, [(i, i ^ d) for i in range(size)])  84.9 us
    pallas_call x4, Pallas kernels, window(): pl.pallas_call(kernel, name='window', compiler_params=pltpu.CompilerParam...  74.8 us
    ppermute x10, starting transfers between devices, along_hel(): lax.ppermute(array, 'hel', [(i, i + step) for i in range(size) if 0 <= i...  30.8 us
    unnamed x132, local copies, waits for them, and re-layouts  28.8 us
    pallas_call x5, Pallas kernels, pack(): pl.pallas_call(kernel, name='pack', compiler_params=pltpu.CompilerParams(...  12.2 us
  transfers between devices with their start and end apart: 83, of which 28 were waited for; matrix products, arithmetic and copies ran while one was open for 2% of the time, Pallas kernels for 23%

profile of v4, /device:TPU:11, one launch (start us, length us, event | category | flops | bytes accessed | tf_op | source)
XLA Modules:
  0.0 432.9 jit_solution(1453622783888853853)
XLA Ops:
  12.3 4.0 collective-permute-start.40
  21.7 3.7 collective-permute-start.30
  27.8 6.1 %collective-permute-done.29.refs_2_.refs_10_.refs_13_ = f32[13,16,256]{2,1,0:T(8,128)S(1)} collective-permute-done((f32[13,16,256]{2,1,0:T(8,128)S(1)}, f32[13,16,256]{2,1,0:T(8,128)S(1)}, u32[]{:S(2)}, u32[]{:S(2)}) %collective-permute-start.29) | collective-permute-done | bytes 213024 | tf_op jit(solution)/shard_map/ppermute | solution.py:21
  41.6 12.0 %collective-permute-done.32.refs_5_.refs_13_.refs_16_ = f32[13,16,256]{2,1,0:T(8,128)S(1)} collective-permute-done((f32[13,16,256]{2,1,0:T(8,128)S(1)}, f32[13,16,256]{2,1,0:T(8,128)S(1)}, u32[]{:S(2)}, u32[]{:S(2)}) %collective-permute-start.32) | collective-permute-done | bytes 213024 | tf_op jit(solution)/shard_map/ppermute | solution.py:21
  58.3 12.1 %collective-permute-done.34.refs_7_.refs_15_.refs_18_ = f32[13,16,256]{2,1,0:T(8,128)S(1)} collective-permute-done((f32[13,16,256]{2,1,0:T(8,128)S(1)}, f32[13,16,256]{2,1,0:T(8,128)S(1)}, u32[]{:S(2)}, u32[]{:S(2)}) %collective-permute-start.34) | collective-permute-done | bytes 213024 | tf_op jit(solution)/shard_map/ppermute | solution.py:21
  77.1 13.6 %collective-permute-done.17.refs_4_.refs_7_ = f32[16,16,256]{2,1,0:T(8,128)S(1)} collective-permute-done((f32[16,16,256]{2,1,0:T(8,128)S(1)}, f32[16,16,256]{2,1,0:T(8,128)S(1)}, u32[]{:S(2)}, u32[]{:S(2)}) %collective-permute-start.17) | collective-permute-done | bytes 262176 | tf_op jit(solution)/shard_map/ppermute | solution.py:21
  92.8 3.6 collective-permute-done.18.refs_5_.refs_8_
  102.9 12.4 %collective-permute-done.20.refs_7_.refs_10_ = f32[16,16,256]{2,1,0:T(8,128)S(1)} collective-permute-done((f32[16,16,256]{2,1,0:T(8,128)S(1)}, f32[16,16,256]{2,1,0:T(8,128)S(1)}, u32[]{:S(2)}, u32[]{:S(2)}) %collective-permute-start.20) | collective-permute-done | bytes 262176 | tf_op jit(solution)/shard_map/ppermute | solution.py:21
  117.1 3.7 pack.5
  126.6 9.0 %collective-permute-done.10.refs_4_.refs_7_ = f32[16,16,256]{2,1,0:T(8,128)S(1)} collective-permute-done((f32[16,16,256]{2,1,0:T(8,128)S(1)}, f32[16,16,256]{2,1,0:T(8,128)S(1)}, u32[]{:S(2)}, u32[]{:S(2)}) %collective-permute-start.10) | collective-permute-done | bytes 262176 | tf_op jit(solution)/shard_map/ppermute | solution.py:21
  137.8 3.6 collective-permute-done.11.refs_5_.refs_8_
  143.8 3.5 collective-permute-done.12.refs_6_.refs_9_
  150.4 10.0 %collective-permute-done.13.refs_7_.refs_10_ = f32[16,16,256]{2,1,0:T(8,128)S(1)} collective-permute-done((f32[16,16,256]{2,1,0:T(8,128)S(1)}, f32[16,16,256]{2,1,0:T(8,128)S(1)}, u32[]{:S(2)}, u32[]{:S(2)}) %collective-permute-start.13) | collective-permute-done | bytes 262176 | tf_op jit(solution)/shard_map/ppermute | solution.py:21
  162.1 3.9 collective-permute-start.38
  186.0 4.1 collective-permute-start.43
  201.9 18.7 %window.4 = (f32[16,16,256]{2,1,0:T(8,128)S(1)}, f32[16,16,256]{2,1,0:T(8,128)S(1)}, f32[16,16,256]{2,1,0:T(8,128)S(1)}, f32[16,16,256]{2,1,0:T(8,128)S(1)}, f32...) custom-call(f32[23]{0:T(128)S(1)} %get-tuple-element.137.refs_0_, ...), custom_call_target="tpu_custom_call" | custom-call | tf_op jit(solution)/shard_map/window/pallas_call | solution.py:309
  228.0 9.7 %collective-permute-done.77.refs_2_ = f32[16,16,256]{2,1,0:T(8,128)S(1)} collective-permute-done((f32[16,16,256]{2,1,0:T(8,128)S(1)}, f32[16,16,256]{2,1,0:T(8,128)S(1)}, u32[]{:S(2)}, u32[]{:S(2)}) %collective-permute-start.77) | collective-permute-done | bytes 262176 | tf_op jit(solution)/shard_map/ppermute | solution.py:21
  241.3 18.5 %window.5 = (f32[16,16,256]{2,1,0:T(8,128)S(1)}, f32[16,16,256]{2,1,0:T(8,128)S(1)}, f32[16,16,256]{2,1,0:T(8,128)S(1)}, f32[16,16,256]{2,1,0:T(8,128)S(1)}, f32...) custom-call(f32[23]{0:T(128)S(1)} %copy-done.56, ...), custom_call_target="tpu_custom_call" | custom-call | tf_op jit(solution)/shard_map/window/pallas_call | solution.py:309
  267.1 5.9 %collective-permute-done.82.refs_7_ = f32[16,16,256]{2,1,0:T(8,128)S(1)} collective-permute-done((f32[16,16,256]{2,1,0:T(8,128)S(1)}, f32[16,16,256]{2,1,0:T(8,128)S(1)}, u32[]{:S(2)}, u32[]{:S(2)}) %collective-permute-start.82) | collective-permute-done | bytes 262176 | tf_op jit(solution)/shard_map/ppermute | solution.py:21
  276.3 4.3 collective-permute-start.44
  280.6 4.2 collective-permute-start.45
  284.8 3.7 collective-permute-start.73
  291.1 18.5 %window.7 = (f32[16,16,256]{2,1,0:T(8,128)S(1)}, f32[16,16,256]{2,1,0:T(8,128)S(1)}, f32[16,16,256]{2,1,0:T(8,128)S(1)}, f32[16,16,256]{2,1,0:T(8,128)S(1)}, f32...) custom-call(f32[23]{0:T(128)S(1)} %get-tuple-element.195.refs_0_, ...), custom_call_target="tpu_custom_call" | custom-call | tf_op jit(solution)/shard_map/window/pallas_call | solution.py:309
  311.6 6.4 %collective-permute-done.74.refs_6_ = f32[16,16,256]{2,1,0:T(8,128)S(1)} collective-permute-done((f32[16,16,256]{2,1,0:T(8,128)S(1)}, f32[16,16,256]{2,1,0:T(8,128)S(1)}, u32[]{:S(2)}, u32[]{:S(2)}) %collective-permute-start.74) | collective-permute-done | bytes 262176 | tf_op jit(solution)/shard_map/ppermute | solution.py:21
  320.5 19.0 %window.6 = (f32[14,16,256]{2,1,0:T(8,128)S(1)}, f32[14,16,256]{2,1,0:T(8,128)S(1)}, f32[14,16,256]{2,1,0:T(8,128)S(1)}, f32[14,16,256]{2,1,0:T(8,128)S(1)}, f32...) custom-call(f32[23]{0:T(128)S(1)} %get-tuple-element.229.refs_0_, ...), custom_call_target="tpu_custom_call" | custom-call | tf_op jit(solution)/shard_map/window/pallas_call | solution.py:309
  350.8 18.9 %collective-permute-done.66.refs_5_ = f32[16,16,256]{2,1,0:T(8,128)S(1)} collective-permute-done((f32[16,16,256]{2,1,0:T(8,128)S(1)}, f32[16,16,256]{2,1,0:T(8,128)S(1)}, u32[]{:S(2)}, u32[]{:S(2)}) %collective-permute-start.66) | collective-permute-done | bytes 262176 | tf_op jit(solution)/shard_map/ppermute | solution.py:21
  372.4 4.2 collective-permute-done.67.refs_6_
  376.6 10.3 %collective-permute-done.68.refs_7_ = f32[16,16,256]{2,1,0:T(8,128)S(1)} collective-permute-done((f32[16,16,256]{2,1,0:T(8,128)S(1)}, f32[16,16,256]{2,1,0:T(8,128)S(1)}, u32[]{:S(2)}, u32[]{:S(2)}) %collective-permute-start.68) | collective-permute-done | bytes 262176 | tf_op jit(solution)/shard_map/ppermute | solution.py:21
  389.1 3.9 collective-permute-start.48
  393.0 12.4 %collective-permute-done.56.refs_4_ = f32[14,16,256]{2,1,0:T(8,128)S(1)} collective-permute-done((f32[14,16,256]{2,1,0:T(8,128)S(1)}, f32[14,16,256]{2,1,0:T(8,128)S(1)}, u32[]{:S(2)}, u32[]{:S(2)}) %collective-permute-start.56) | collective-permute-done | bytes 229408 | tf_op jit(solution)/shard_map/ppermute | solution.py:21
  414.4 4.3 %collective-permute-done.58.refs_6_ = f32[14,16,256]{2,1,0:T(8,128)S(1)} collective-permute-done((f32[14,16,256]{2,1,0:T(8,128)S(1)}, f32[14,16,256]{2,1,0:T(8,128)S(1)}, u32[]{:S(2)}, u32[]{:S(2)}) %collective-permute-start.58) | collective-permute-done | bytes 229408 | tf_op jit(solution)/shard_map/ppermute | solution.py:21
  419.3 4.7 %collective-permute-done.59.refs_7_ = f32[14,16,256]{2,1,0:T(8,128)S(1)} collective-permute-done((f32[14,16,256]{2,1,0:T(8,128)S(1)}, f32[14,16,256]{2,1,0:T(8,128)S(1)}, u32[]{:S(2)}, u32[]{:S(2)}) %collective-permute-start.59) | collective-permute-done | bytes 229408 | tf_op jit(solution)/shard_map/ppermute | solution.py:21
  (295 shorter events, 159.0 us)
Async XLA Ops:
  33.9 36.5 %collective-permute-start.34 = (f32[13,16,256]{2,1,0:T(8,128)S(1)}, f32[13,16,256]{2,1,0:T(8,128)S(1)}, u32[]{:S(2)}, u32[]{:S(2)}) collective-permute-start(f32[13,16,256]{2,1,0:T(8,128)S(1)} %get-tuple-element.153), channel_id=1, source_target_pairs={{0,7},{1,6},{2,5},{3,4},{4,3},{5,2},{6,1},{7,0},{8,15},{9,14},{10,... | collective-permute-start | bytes 638984 | tf_op jit(solution)/shard_map/ppermute | solution.py:21
  38.7 31.7 %collective-permute-start.14 = (f32[16,16,256]{2,1,0:T(8,128)S(1)}, f32[16,16,256]{2,1,0:T(8,128)S(1)}, u32[]{:S(2)}, u32[]{:S(2)}) collective-permute-start(f32[16,16,256]{2,1,0:T(8,128)S(1)} %get-tuple-element.129), channel_id=1, source_target_pairs={{0,1},{1,0},{2,3},{3,2},{4,5},{5,4},{6,7},{7,6},{8,9},{9,8},{10,11... | collective-permute-start | bytes 786440 | tf_op jit(solution)/shard_map/ppermute | solution.py:21
  39.2 34.9 %collective-permute-start.15 = (f32[16,16,256]{2,1,0:T(8,128)S(1)}, f32[16,16,256]{2,1,0:T(8,128)S(1)}, u32[]{:S(2)}, u32[]{:S(2)}) collective-permute-start(f32[16,16,256]{2,1,0:T(8,128)S(1)} %get-tuple-element.130), channel_id=1, source_target_pairs={{0,2},{1,3},{2,0},{3,1},{4,6},{5,7},{6,4},{7,5},{8,10},{9,11},{10,... | collective-permute-start | bytes 786440 | tf_op jit(solution)/shard_map/ppermute | solution.py:21
  58.3 32.4 %collective-permute-start.17 = (f32[16,16,256]{2,1,0:T(8,128)S(1)}, f32[16,16,256]{2,1,0:T(8,128)S(1)}, u32[]{:S(2)}, u32[]{:S(2)}) collective-permute-start(f32[16,16,256]{2,1,0:T(8,128)S(1)} %get-tuple-element.132), channel_id=1, source_target_pairs={{0,4},{1,5},{2,6},{3,7},{4,0},{5,1},{6,2},{7,3},{8,12},{9,13},{10,... | collective-permute-start | bytes 786440 | tf_op jit(solution)/shard_map/ppermute | solution.py:21
  70.4 31.8 %collective-permute-start.19 = (f32[16,16,256]{2,1,0:T(8,128)S(1)}, f32[16,16,256]{2,1,0:T(8,128)S(1)}, u32[]{:S(2)}, u32[]{:S(2)}) collective-permute-start(f32[16,16,256]{2,1,0:T(8,128)S(1)} %get-tuple-element.134), channel_id=1, source_target_pairs={{0,6},{1,7},{2,4},{3,5},{4,2},{5,3},{6,0},{7,1},{8,14},{9,15},{10,... | collective-permute-start | bytes 786440 | tf_op jit(solution)/shard_map/ppermute | solution.py:21
  74.8 40.5 %collective-permute-start.20 = (f32[16,16,256]{2,1,0:T(8,128)S(1)}, f32[16,16,256]{2,1,0:T(8,128)S(1)}, u32[]{:S(2)}, u32[]{:S(2)}) collective-permute-start(f32[16,16,256]{2,1,0:T(8,128)S(1)} %get-tuple-element.135), channel_id=1, source_target_pairs={{0,7},{1,6},{2,5},{3,4},{4,3},{5,2},{6,1},{7,0},{8,15},{9,14},{10,... | collective-permute-start | bytes 786440 | tf_op jit(solution)/shard_map/ppermute | solution.py:21
  75.7 40.4 %collective-permute-start.7 = (f32[16,16,256]{2,1,0:T(8,128)S(1)}, f32[16,16,256]{2,1,0:T(8,128)S(1)}, u32[]{:S(2)}, u32[]{:S(2)}) collective-permute-start(f32[16,16,256]{2,1,0:T(8,128)S(1)} %get-tuple-element.121), channel_id=1, source_target_pairs={{0,1},{1,0},{2,3},{3,2},{4,5},{5,4},{6,7},{7,6},{8,9},{9,8},{10,11... | collective-permute-start | bytes 786440 | tf_op jit(solution)/shard_map/ppermute | solution.py:21
  91.4 32.2 %collective-permute-start.8 = (f32[16,16,256]{2,1,0:T(8,128)S(1)}, f32[16,16,256]{2,1,0:T(8,128)S(1)}, u32[]{:S(2)}, u32[]{:S(2)}) collective-permute-start(f32[16,16,256]{2,1,0:T(8,128)S(1)} %get-tuple-element.122), channel_id=1, source_target_pairs={{0,2},{1,3},{2,0},{3,1},{4,6},{5,7},{6,4},{7,5},{8,10},{9,11},{10,... | collective-permute-start | bytes 786440 | tf_op jit(solution)/shard_map/ppermute | solution.py:21
  102.9 32.6 %collective-permute-start.10 = (f32[16,16,256]{2,1,0:T(8,128)S(1)}, f32[16,16,256]{2,1,0:T(8,128)S(1)}, u32[]{:S(2)}, u32[]{:S(2)}) collective-permute-start(f32[16,16,256]{2,1,0:T(8,128)S(1)} %get-tuple-element.124), channel_id=1, source_target_pairs={{0,4},{1,5},{2,6},{3,7},{4,0},{5,1},{6,2},{7,3},{8,12},{9,13},{10,... | collective-permute-start | bytes 786440 | tf_op jit(solution)/shard_map/ppermute | solution.py:21
  116.8 30.5 %collective-permute-start.12 = (f32[16,16,256]{2,1,0:T(8,128)S(1)}, f32[16,16,256]{2,1,0:T(8,128)S(1)}, u32[]{:S(2)}, u32[]{:S(2)}) collective-permute-start(f32[16,16,256]{2,1,0:T(8,128)S(1)} %get-tuple-element.126), channel_id=1, source_target_pairs={{0,6},{1,7},{2,4},{3,5},{4,2},{5,3},{6,0},{7,1},{8,14},{9,15},{10,... | collective-permute-start | bytes 786440 | tf_op jit(solution)/shard_map/ppermute | solution.py:21
  124.4 36.0 %collective-permute-start.13 = (f32[16,16,256]{2,1,0:T(8,128)S(1)}, f32[16,16,256]{2,1,0:T(8,128)S(1)}, u32[]{:S(2)}, u32[]{:S(2)}) collective-permute-start(f32[16,16,256]{2,1,0:T(8,128)S(1)} %get-tuple-element.127), channel_id=1, source_target_pairs={{0,7},{1,6},{2,5},{3,4},{4,3},{5,2},{6,1},{7,0},{8,15},{9,14},{10,... | collective-permute-start | bytes 786440 | tf_op jit(solution)/shard_map/ppermute | solution.py:21
  125.2 36.2 %collective-permute-start = (f32[16,16,256]{2,1,0:T(8,128)S(1)}, f32[16,16,256]{2,1,0:T(8,128)S(1)}, u32[]{:S(2)}, u32[]{:S(2)}) collective-permute-start(f32[16,16,256]{2,1,0:T(8,128)S(1)} %get-tuple-element.113), channel_id=1, source_target_pairs={{0,1},{1,0},{2,3},{3,2},{4,5},{5,4},{6,7},{7,6},{8,9},{9,8},{10,11... | collective-permute-start | bytes 786440 | tf_op jit(solution)/shard_map/ppermute | solution.py:21
  136.3 30.6 %collective-permute-start.1 = (f32[16,16,256]{2,1,0:T(8,128)}, f32[16,16,256]{2,1,0:T(8,128)}, u32[]{:S(2)}, u32[]{:S(2)}) collective-permute-start(f32[16,16,256]{2,1,0:T(8,128)} %get-tuple-element.114), channel_id=1, source_target_pairs={{0,2},{1,3},{2,0},{3,1},{4,6},{5,7},{6,4},{7,5},{8,10},{9,11},{10,... | collective-permute-start | bytes 786440 | tf_op jit(solution)/shard_map/ppermute | solution.py:21
  169.7 51.0 %collective-permute-start.4 = (f32[16,16,256]{2,1,0:T(8,128)}, f32[16,16,256]{2,1,0:T(8,128)}, u32[]{:S(2)}, u32[]{:S(2)}) collective-permute-start(f32[16,16,256]{2,1,0:T(8,128)} %copy-done.60), channel_id=1, source_target_pairs={{0,5},{1,4},{2,7},{3,6},{4,1},{5,0},{6,3},{7,2},{8,13},{9,12},{10,... | collective-permute-start | bytes 786440 | tf_op jit(solution)/shard_map/ppermute | solution.py:21
  183.9 36.9 %collective-permute-start.5 = (f32[16,16,256]{2,1,0:T(8,128)}, f32[16,16,256]{2,1,0:T(8,128)S(1)}, u32[]{:S(2)}, u32[]{:S(2)}) collective-permute-start(f32[16,16,256]{2,1,0:T(8,128)} %copy-done.59), channel_id=1, source_target_pairs={{0,6},{1,7},{2,4},{3,5},{4,2},{5,3},{6,0},{7,1},{8,14},{9,15},{10,... | collective-permute-start | bytes 786440 | tf_op jit(solution)/shard_map/ppermute | solution.py:21
  186.0 40.4 %collective-permute-start.43 = (f32[8,3,16,256]{3,2,1,0:T(8,128)S(1)}, f32[8,3,16,256]{3,2,1,0:T(8,128)S(1)}, u32[]{:S(2)}, u32[]{:S(2)}) collective-permute-start(f32[8,3,16,256]{3,2,1,0:T(8,128)S(1)} %get-tuple-element.136), channel_id=1, source_target_pairs={{8,0},{16,8},{24,16},{9,1},{17,9},{25,17},{10,2},{18,10},{26,18},{... | collective-permute-start | bytes 1179656 | tf_op jit(solution)/shard_map/ppermute | solution.py:350
  190.1 33.7 %collective-permute-start.42 = (f32[8,3,16,256]{3,2,1,0:T(8,128)S(1)}, f32[8,3,16,256]{3,2,1,0:T(8,128)S(1)}, u32[]{:S(2)}, u32[]{:S(2)}) collective-permute-start(f32[8,3,16,256]{3,2,1,0:T(8,128)S(1)} %get-tuple-element.167), channel_id=1, source_target_pairs={{0,8},{8,16},{16,24},{1,9},{9,17},{17,25},{2,10},{10,18},{18,26},{... | collective-permute-start | bytes 1179656 | tf_op jit(solution)/shard_map/ppermute | solution.py:350
  223.5 36.4 %collective-permute-start.78 = (f32[16,16,256]{2,1,0:T(8,128)S(1)}, f32[16,16,256]{2,1,0:T(8,128)S(1)}, u32[]{:S(2)}, u32[]{:S(2)}) collective-permute-start(f32[16,16,256]{2,1,0:T(8,128)S(1)} %get-tuple-element.214), channel_id=1, source_target_pairs={{0,3},{1,2},{2,1},{3,0},{4,7},{5,6},{6,5},{7,4},{8,11},{9,10},{10,... | collective-permute-start | bytes 786440 | tf_op jit(solution)/shard_map/ppermute | solution.py:21
  223.9 36.1 %collective-permute-start.79 = (f32[16,16,256]{2,1,0:T(8,128)S(1)}, f32[16,16,256]{2,1,0:T(8,128)S(1)}, u32[]{:S(2)}, u32[]{:S(2)}) collective-permute-start(f32[16,16,256]{2,1,0:T(8,128)S(1)} %get-tuple-element.215), channel_id=1, source_target_pairs={{0,4},{1,5},{2,6},{3,7},{4,0},{5,1},{6,2},{7,3},{8,12},{9,13},{10,... | collective-permute-start | bytes 786440 | tf_op jit(solution)/shard_map/ppermute | solution.py:21
  226.4 35.5 %collective-permute-start.80 = (f32[16,16,256]{2,1,0:T(8,128)S(1)}, f32[16,16,256]{2,1,0:T(8,128)S(1)}, u32[]{:S(2)}, u32[]{:S(2)}) collective-permute-start(f32[16,16,256]{2,1,0:T(8,128)S(1)} %get-tuple-element.216), channel_id=1, source_target_pairs={{0,5},{1,4},{2,7},{3,6},{4,1},{5,0},{6,3},{7,2},{8,13},{9,12},{10,... | collective-permute-start | bytes 786440 | tf_op jit(solution)/shard_map/ppermute | solution.py:21
  226.8 40.3 %collective-permute-start.81 = (f32[16,16,256]{2,1,0:T(8,128)S(1)}, f32[16,16,256]{2,1,0:T(8,128)S(1)}, u32[]{:S(2)}, u32[]{:S(2)}) collective-permute-start(f32[16,16,256]{2,1,0:T(8,128)S(1)} %get-tuple-element.217), channel_id=1, source_target_pairs={{0,6},{1,7},{2,4},{3,5},{4,2},{5,3},{6,0},{7,1},{8,14},{9,15},{10,... | collective-permute-start | bytes 786440 | tf_op jit(solution)/shard_map/ppermute | solution.py:21
  237.6 35.3 %collective-permute-start.82 = (f32[16,16,256]{2,1,0:T(8,128)S(1)}, f32[16,16,256]{2,1,0:T(8,128)S(1)}, u32[]{:S(2)}, u32[]{:S(2)}) collective-permute-start(f32[16,16,256]{2,1,0:T(8,128)S(1)} %get-tuple-element.218), channel_id=1, source_target_pairs={{0,7},{1,6},{2,5},{3,4},{4,3},{5,2},{6,1},{7,0},{8,15},{9,14},{10,... | collective-permute-start | bytes 786440 | tf_op jit(solution)/shard_map/ppermute | solution.py:21
  276.3 41.7 %collective-permute-start.44 = (f32[8,3,16,256]{3,2,1,0:T(8,128)S(1)}, f32[8,3,16,256]{3,2,1,0:T(8,128)S(1)}, u32[]{:S(2)}, u32[]{:S(2)}) collective-permute-start(f32[8,3,16,256]{3,2,1,0:T(8,128)S(1)} %get-tuple-element.177), channel_id=1, source_target_pairs={{0,8},{8,16},{16,24},{1,9},{9,17},{17,25},{2,10},{10,18},{18,26},{... | collective-permute-start | bytes 1179656 | tf_op jit(solution)/shard_map/ppermute | solution.py:350
  280.6 39.6 %collective-permute-start.45 = (f32[8,3,16,256]{3,2,1,0:T(8,128)S(1)}, f32[8,3,16,256]{3,2,1,0:T(8,128)S(1)}, u32[]{:S(2)}, u32[]{:S(2)}) collective-permute-start(f32[8,3,16,256]{3,2,1,0:T(8,128)S(1)} %get-tuple-element.178), channel_id=1, source_target_pairs={{8,0},{16,8},{24,16},{9,1},{17,9},{25,17},{10,2},{18,10},{26,18},{... | collective-permute-start | bytes 1179656 | tf_op jit(solution)/shard_map/ppermute | solution.py:350
  289.3 50.2 %collective-permute-start.75 = (f32[16,16,256]{2,1,0:T(8,128)S(1)}, f32[16,16,256]{2,1,0:T(8,128)S(1)}, u32[]{:S(2)}, u32[]{:S(2)}) collective-permute-start(f32[16,16,256]{2,1,0:T(8,128)S(1)} %get-tuple-element.211), channel_id=1, source_target_pairs={{0,7},{1,6},{2,5},{3,4},{4,3},{5,2},{6,1},{7,0},{8,15},{9,14},{10,... | collective-permute-start | bytes 786440 | tf_op jit(solution)/shard_map/ppermute | solution.py:21
  311.0 35.8 %collective-permute-start.62 = (f32[16,16,256]{2,1,0:T(8,128)S(1)}, f32[16,16,256]{2,1,0:T(8,128)S(1)}, u32[]{:S(2)}, u32[]{:S(2)}) collective-permute-start(f32[16,16,256]{2,1,0:T(8,128)S(1)} %get-tuple-element.198), channel_id=1, source_target_pairs={{0,1},{1,0},{2,3},{3,2},{4,5},{5,4},{6,7},{7,6},{8,9},{9,8},{10,11... | collective-permute-start | bytes 786440 | tf_op jit(solution)/shard_map/ppermute | solution.py:21
  347.7 39.1 %collective-permute-start.68 = (f32[16,16,256]{2,1,0:T(8,128)S(1)}, f32[16,16,256]{2,1,0:T(8,128)S(1)}, u32[]{:S(2)}, u32[]{:S(2)}) collective-permute-start(f32[16,16,256]{2,1,0:T(8,128)S(1)} %get-tuple-element.204), channel_id=1, source_target_pairs={{0,7},{1,6},{2,5},{3,4},{4,3},{5,2},{6,1},{7,0},{8,15},{9,14},{10,... | collective-permute-start | bytes 786440 | tf_op jit(solution)/shard_map/ppermute | solution.py:21
  347.7 39.1 %collective-permute-start.53 = (f32[14,16,256]{2,1,0:T(8,128)S(1)}, f32[14,16,256]{2,1,0:T(8,128)S(1)}, u32[]{:S(2)}, u32[]{:S(2)}) collective-permute-start(f32[14,16,256]{2,1,0:T(8,128)S(1)} %get-tuple-element.188), channel_id=1, source_target_pairs={{0,1},{1,0},{2,3},{3,2},{4,5},{5,4},{6,7},{7,6},{8,9},{9,8},{10,11... | collective-permute-start | bytes 688136 | tf_op jit(solution)/shard_map/ppermute | solution.py:21
  348.7 38.5 %collective-permute-start.54 = (f32[14,16,256]{2,1,0:T(8,128)S(1)}, f32[14,16,256]{2,1,0:T(8,128)S(1)}, u32[]{:S(2)}, u32[]{:S(2)}) collective-permute-start(f32[14,16,256]{2,1,0:T(8,128)S(1)} %get-tuple-element.189), channel_id=1, source_target_pairs={{0,2},{1,3},{2,0},{3,1},{4,6},{5,7},{6,4},{7,5},{8,10},{9,11},{10,... | collective-permute-start | bytes 688136 | tf_op jit(solution)/shard_map/ppermute | solution.py:21
  386.8 31.9 %collective-permute-start.58 = (f32[14,16,256]{2,1,0:T(8,128)S(1)}, f32[14,16,256]{2,1,0:T(8,128)S(1)}, u32[]{:S(2)}, u32[]{:S(2)}) collective-permute-start(f32[14,16,256]{2,1,0:T(8,128)S(1)} %get-tuple-element.193), channel_id=1, source_target_pairs={{0,6},{1,7},{2,4},{3,5},{4,2},{5,3},{6,0},{7,1},{8,14},{9,15},{10,... | collective-permute-start | bytes 688136 | tf_op jit(solution)/shard_map/ppermute | solution.py:21
  387.1 36.9 %collective-permute-start.59 = (f32[14,16,256]{2,1,0:T(8,128)S(1)}, f32[14,16,256]{2,1,0:T(8,128)S(1)}, u32[]{:S(2)}, u32[]{:S(2)}) collective-permute-start(f32[14,16,256]{2,1,0:T(8,128)S(1)} %get-tuple-element.194), channel_id=1, source_target_pairs={{0,7},{1,6},{2,5},{3,4},{4,3},{5,2},{6,1},{7,0},{8,15},{9,14},{10,... | collective-permute-start | bytes 688136 | tf_op jit(solution)/shard_map/ppermute | solution.py:21
  389.1 42.8 %collective-permute-start.48 = (f32[2,16,256]{2,1,0:T(8,128)S(1)}, f32[2,16,256]{2,1,0:T(8,128)S(1)}, u32[]{:S(2)}, u32[]{:S(2)}) collective-permute-start(f32[2,16,256]{2,1,0:T(8,128)S(1)} %get-tuple-element.182), channel_id=1, source_target_pairs={{0,3},{1,2},{2,1},{3,0},{4,7},{5,6},{6,5},{7,4},{8,11},{9,10},{10,... | collective-permute-start | bytes 98312 | tf_op jit(solution)/shard_map/ppermute | solution.py:21
  (117 other events, 3215.4 us)
